TPU v7x, 32 devices: a whole 2x2x4 slice. The times are simulated.
32 devices in a mesh: seq: 8 (over y, x, core), dp: 4 (over z).
Axes of the slice: x: 2, y: 2, z: 4, core: 2. Of those that a mesh axis runs over, the one named last changes fastest.
Arguments:
- projected: bfloat16 [3, 4096, 4096], P(None, 'seq', 'dp'), may hold values from -6 to 6
- featurizer: bfloat16 [7, 3, 4096], P(None, None, 'dp'), may hold values from -25 to 25
- long_filter: bfloat16 [256, 128], P('dp'), may hold values from -0.5 to 0.5
- skip_gain: bfloat16 [4096], P('dp'), may hold values from -4 to 4
- out_cotangent: bfloat16 [4096, 4096], P('seq', 'dp'), may hold values from -6 to 6
Outputs:
- grad_featurizer: float32 [7, 3, 4096], P(None, None, 'dp')
- grad_filter: float32 [256, 128], P('dp')
- grad_skip: float32 [4096], P('dp')
All inputs are finite; a program needn't handle non-finite values.
Results may differ from a plain program's by a relative error of at most 0.0071.
Values may be sent and summed in bfloat16 or wider, within the bound.
No kernel may reach another device: no remote copies, remote signals or barrier semaphores. Data moves between devices by JAX's collectives and lax.ppermute only.
A program may use at most 64 MiB of HBM per device.

v0:
```python
import math

import jax
import jax.numpy as jnp
from jax import lax
from jax.sharding import PartitionSpec as P


def shifted(array, axis, by):
    length = lax.axis_size(axis)
    pairs = [(i, i + by) for i in range(length) if 0 <= i + by < length]
    return lax.ppermute(array, axis, pairs)


def band_matrix(taps, block_rows):
    groups, filter_taps = taps.shape
    width = block_rows + filter_taps - 1
    pattern = jnp.concatenate([taps, jnp.zeros((groups, block_rows), taps.dtype)], axis=1)
    tiled = jnp.tile(pattern, (1, block_rows))[:, : block_rows * width]
    shaped = tiled.reshape(groups, block_rows, width)
    return jnp.concatenate([shaped, jnp.zeros((groups, block_rows, 1), taps.dtype)], axis=2)


def window_blocks(source, block_rows, filter_taps, groups):
    rows, channels = source.shape
    blocks_out = (rows - filter_taps + 1) // block_rows
    total_rows = (blocks_out + 1) * block_rows
    padded = jnp.concatenate(
        [source, jnp.zeros((total_rows - rows, channels), source.dtype)], axis=0
    )
    shaped = padded.reshape(blocks_out + 1, block_rows, groups, channels // groups)
    return (shaped[:-1], shaped[1:, :filter_taps])


def apply_band(taps, source, block_rows):
    groups, filter_taps = taps.shape
    channels = source.shape[1]
    left, right = window_blocks(source, block_rows, filter_taps, groups)
    blocks_out = left.shape[0]
    step = math.gcd(groups, 4)

    def apply_one_step(number):
        part_taps = lax.dynamic_slice_in_dim(taps, number * step, step, 0)
        band = band_matrix(part_taps, block_rows)
        part_left = lax.dynamic_slice_in_dim(left, number * step, step, 2)
        part_right = lax.dynamic_slice_in_dim(right, number * step, step, 2)
        near = jnp.einsum(
            "gts,bsgi->btgi", band[:, :, :block_rows], part_left, preferred_element_type=jnp.float32
        )
        far = jnp.einsum(
            "gts,bsgi->btgi",
            band[:, :, block_rows:],
            part_right,
            preferred_element_type=jnp.float32,
        )
        return near + far

    pieces = lax.map(apply_one_step, jnp.arange(groups // step))
    return jnp.moveaxis(pieces, 0, 2).reshape(blocks_out * block_rows, channels)


def filter_gradient(cotangent, source, filter_taps, groups, block_rows):
    rows, channels = cotangent.shape
    members = channels // groups
    left, right = window_blocks(source, block_rows, filter_taps, groups)
    blocks_out = left.shape[0]
    cot_blocks = cotangent.reshape(blocks_out, block_rows, groups, members)
    step = math.gcd(groups, 4)
    span = block_rows + filter_taps

    def filter_one_step(number):
        part_cot = lax.dynamic_slice_in_dim(cot_blocks, number * step, step, 2)
        part_left = lax.dynamic_slice_in_dim(left, number * step, step, 2)
        part_right = lax.dynamic_slice_in_dim(right, number * step, step, 2)
        near = jnp.einsum("btgi,bsgi->gts", part_cot, part_left, preferred_element_type=jnp.float32)
        far = jnp.einsum("btgi,bsgi->gts", part_cot, part_right, preferred_element_type=jnp.float32)
        full = jnp.concatenate([near, far], axis=2)
        flat = full.reshape(step, block_rows * span)
        flat = jnp.concatenate([flat, jnp.zeros((step, block_rows), jnp.float32)], axis=1)
        diagonal = flat.reshape(step, block_rows, span + 1)[:, :, :filter_taps]
        return jnp.sum(diagonal, axis=1)

    stacked = lax.map(filter_one_step, jnp.arange(groups // step)).reshape(groups, filter_taps)
    return jnp.flip(stacked, 1)


def body(projected, featurizer, long_filter, skip_gain, out_cotangent):
    parts, local_rows, channels = projected.shape
    groups, filter_taps = long_filter.shape
    feat_taps = featurizer.shape[0]
    block_rows = min(local_rows, 256)
    feat_f32 = featurizer.astype(jnp.float32)
    input_rim = shifted(projected[:, local_rows - (feat_taps - 1) :, :], "seq", 1)
    extended = jnp.concatenate([input_rim, projected], axis=1)
    featured_f32 = feat_f32[0][:, None, :] * projected.astype(jnp.float32)
    for tap_index in range(1, feat_taps):
        begin = feat_taps - 1 - tap_index
        featured_f32 = featured_f32 + feat_f32[tap_index][:, None, :] * extended[
            :, begin : begin + local_rows, :
        ].astype(jnp.float32)
    featured = featured_f32.astype(jnp.bfloat16)
    queries_f32 = featured[0].astype(jnp.float32)
    key_f32 = featured[1].astype(jnp.float32)
    value_f32 = featured[2].astype(jnp.float32)
    product = (key_f32 * value_f32).astype(jnp.bfloat16)
    product_rim = shifted(product[local_rows - (filter_taps - 1) :], "seq", 1)
    forward_source = jnp.concatenate([product_rim, product], axis=0)
    filtered = apply_band(jnp.flip(long_filter, 1), forward_source, block_rows)
    skip_f32 = skip_gain.astype(jnp.float32)
    product_f32 = product.astype(jnp.float32)
    inner_sum = filtered + skip_f32 * product_f32
    output = queries_f32 * inner_sum
    cot_f32 = out_cotangent.astype(jnp.float32)
    square_part = jnp.sum(output * output, axis=1)
    cross_part = jnp.sum(cot_f32 * output, axis=1)
    square_sum, cross_sum = lax.psum((square_part, cross_part), "dp")
    channels_all = channels * lax.axis_size("dp")
    rms = jnp.sqrt(square_sum / channels_all + 1e-05)
    cross_mean = cross_sum / channels_all
    token_scale = 1.0 / math.sqrt(local_rows * lax.axis_size("seq"))
    out_grad = (cot_f32 / rms[:, None] - output * (cross_mean / rms**3)[:, None]) * token_scale
    conv_grad = out_grad * queries_f32
    cotangent = conv_grad.astype(jnp.bfloat16)
    query_grad = out_grad * inner_sum
    cotangent_rim = shifted(cotangent[: filter_taps - 1], "seq", -1)
    backward_source = jnp.concatenate([cotangent, cotangent_rim], axis=0)
    product_grad = apply_band(long_filter, backward_source, block_rows) + skip_f32 * conv_grad
    all_grad = jnp.stack([query_grad, product_grad * value_f32, product_grad * key_f32])
    per_tap = []
    for tap_index in range(feat_taps):
        begin = feat_taps - 1 - tap_index
        per_tap.append(
            jnp.sum(
                all_grad * extended[:, begin : begin + local_rows, :].astype(jnp.float32), axis=1
            )
        )
    feat_grad = jnp.stack(per_tap)
    skip_grad = jnp.sum(conv_grad * product_f32, axis=0)
    filter_grad = filter_gradient(cotangent, forward_source, filter_taps, groups, block_rows)
    feat_out, filter_out, skip_out = lax.psum((feat_grad, filter_grad, skip_grad), "seq")
    return (feat_out, filter_out, skip_out)


def solution(mesh):
    return jax.shard_map(
        body,
        mesh=mesh,
        in_specs=(
            P(None, "seq", "dp"),
            P(None, None, "dp"),
            P("dp", None),
            P("dp"),
            P("seq", "dp"),
        ),
        out_specs=(P(None, None, "dp"), P("dp", None), P("dp")),
        check_vma=False,
    )
```

profile of v0, /device:TPU:0, one launch (start us, length us, event | category | flops | bytes accessed | tf_op | source)
XLA Modules:
  0.0 508.7 jit_solution(7150622783251583654)
XLA Ops:
  8.0 2.4 collective-permute-start
  11.7 3.2 copy.25
  16.4 13.6 %fusion.31 = bf16[3,512,1024]{1,2,0:T(8,128)(2,1)S(1)} fusion(bf16[3,512,1024]{1,2,0:T(8,128)(2,1)S(1)} %copy.25, bf16[3,6,1024]{1,2,0:T(8,128)(2,1)} %copy.26, f32[3,1024]{1,0:T(4,128)S(1)} %get-tuple-element.211, f32[3,1024]{1,0:T(4,128)S(1)} %get-tuple-element.212, f32[3,1024]{1,0:T(4,128)S(1)} %get-tuple-element.213, ...), kind=kLoop, calls=%fused_computation.64 | loop fusion | flops 61341696 | bytes 6414336 | tf_op jit(solution)/shard_map/convert_element_type | solution.py:101
  33.2 4.5 collective-permute-start.1
  37.8 2.3 copy.24
  40.2 2.0 maximum_maximum_fusion
  42.2 2.2 reshape.67
  44.4 1.8 slice.153
  50.8 107.1 %while.30 = (s32[]{:T(128)}, f32[16,2,256,4,16]{2,4,1,3,0:T(8,128)}, s32[16]{0:T(128)S(1)}, bf16[2,256,64,16]{1,3,0,2:T(8,128)(2,1)}, bf16[64,128]{1,0:T(8,128)(...) while((s32[]{:T(128)}, ...), condition=%wide.region_1.2_spmd, body=%wide.region_0.1_spmd.sunk | while | flops 25198596 | bytes 7306933 | solution.py:58
  55.7 1.8 fusion.72
  62.4 1.8 fusion.72
  69.1 1.8 fusion.72
  75.8 1.8 fusion.72
  82.5 1.8 fusion.72
  89.2 1.8 fusion.72
  95.9 1.8 fusion.72
  102.6 1.8 fusion.72
  109.3 1.8 fusion.72
  116.0 1.8 fusion.72
  122.7 1.8 fusion.72
  142.8 1.8 fusion.72
  149.5 1.8 fusion.72
  156.1 1.8 fusion.72
  158.0 3.5 copy.30
  161.7 2.4 copy-done.1
  165.3 12.1 %all-reduce.6 = (f32[512]{0:T(512)S(1)}, f32[512]{0:T(512)S(1)}) all-reduce(f32[512]{0:T(512)S(1)} %get-tuple-element.152, f32[512]{0:T(512)S(1)} %get-tuple-element.151), channel_id=1, replica_groups=mesh['seq'=8,'dp'=4] {'dp'}, use_global_device_ids=true, to_apply=%region_5.6 | all-reduce | flops 1024 | bytes 8192 | tf_op jit(solution)/shard_map/psum | solution.py:116
  177.5 4.1 fusion.48
  186.8 2.2 reshape.69
  189.0 1.8 slice.155
  192.4 95.6 %while.31 = (s32[]{:T(128)}, f32[16,2,256,4,16]{2,4,1,3,0:T(8,128)}, s32[16]{0:T(128)S(1)}, bf16[2,256,64,16]{1,3,0,2:T(8,128)(2,1)}, bf16[64,128]{1,0:T(8,128)(...) while((s32[]{:T(128)}, ...), condition=%wide.region_7.8_spmd, body=%wide.region_6.7_spmd.sunk | while | flops 25198596 | bytes 7372469 | solution.py:58
  196.6 1.8 fusion.77
  202.5 1.8 fusion.77
  208.5 1.8 fusion.77
  214.5 1.8 fusion.77
  220.5 1.8 fusion.77
  226.5 1.8 fusion.77
  238.4 1.8 fusion.77
  244.4 1.8 fusion.77
  250.4 1.8 fusion.77
  256.3 1.8 fusion.77
  262.3 1.8 fusion.77
  274.3 1.8 fusion.77
  280.2 1.8 fusion.77
  286.2 1.8 fusion.77
  288.0 3.7 copy.33
  296.3 12.7 %fusion.37 = (f32[3,1024]{1,0:T(4,128)S(1)}, f32[3,1024]{1,0:T(4,128)S(1)}, f32[3,1024]{1,0:T(4,128)S(1)}, f32[3,1024]{1,0:T(4,128)S(1)}, f32[3,1024]{1,0:T(4,12...) fusion(bf16[3,512,1024]{1,2,0:T(8,128)(2,1)S(1)} %copy-done.4, bf16[3,6,1024]{1,2,0:T(8,128)(2,1)S(1)} %copy-done.12, ...), kind=kLoop, calls=%fused_computation.70 | loop fusion | flops 64465920 | bytes 9560064 | tf_op jit(solution)/shard_map/reduce_sum | solution.py:133
  309.8 161.5 %while.32 = (s32[]{:T(128)}, f32[16,4,128]{2,1,0:T(4,128)S(1)}, s32[16]{0:T(128)S(1)}, bf16[2,256,64,16]{1,3,0,2:T(8,128)(2,1)}, bf16[2,256,64,16]{1,3,0,2:T(8,1...) while((s32[]{:T(128)}, f32[16,4,128]{2,1,0:T(4,128)S(1)}, ...), condition=%wide.region_18.19_spmd, body=%wide.region_16.18_spmd.sunk | while | flops 25689604 | bytes 18075824 | solution.py:83
  315.5 3.5 reshape.86
  325.5 3.5 reshape.86
  335.6 3.5 reshape.86
  345.7 3.5 reshape.86
  355.8 3.5 reshape.86
  365.9 3.5 reshape.86
  375.9 3.5 reshape.86
  386.0 3.5 reshape.86
  396.1 3.5 reshape.86
  406.2 3.5 reshape.86
  416.3 3.5 reshape.86
  426.3 3.5 reshape.86
  436.4 3.5 reshape.86
  446.5 3.5 reshape.86
  456.6 3.5 reshape.86
  466.7 3.5 reshape.86
  471.3 28.9 %all-reduce.5 = (f32[64,128]{1,0:T(8,128)}, f32[1024]{0:T(1024)}) all-reduce(f32[64,128]{1,0:T(8,128)S(1)} %rev.9, f32[1024]{0:T(1024)S(1)} %get-tuple-element.193), channel_id=1, replica_groups=mesh['seq'=8,'dp'=4] {'seq'}, use_global_device_ids=true, to_apply=%region_19.20 | all-reduce | flops 9216 | bytes 73728 | tf_op jit(solution)/shard_map/psum | solution.py:140
  (500 shorter events, 250.7 us)
Async XLA Ops:
  7.2 493.1 %all-reduce.9.cloned.1.call-start = ((), (), s32[]{:S(2)}) async-start(), calls=%async_computation | async-start | bytes 229376 | tf_op jit(solution)/shard_map/psum | solution.py:140
  8.0 6.9 %collective-permute-start = (bf16[3,6,1024]{2,1,0:T(8,128)(2,1)S(1)}, bf16[3,6,1024]{2,1,0:T(8,128)(2,1)S(1)}, u32[]{:S(2)}, u32[]{:S(2)}) collective-permute-start(bf16[3,6,1024]{2,1,0:T(8,128)(2,1)S(1)} %slice.105), channel_id=1, source_target_pairs={{0,4},{4,8},{8,12},{12,16},{16,20},{20,24},{24,28},{1,5},{5,9},{9,... | collective-permute-start | bytes 110600 | tf_op jit(solution)/shard_map/ppermute | solution.py:12
  14.9 15.1 %copy-start.3 = (bf16[3,512,1024]{1,2,0:T(8,128)(2,1)}, bf16[3,512,1024]{1,2,0:T(8,128)(2,1)S(1)}, u32[]{:S(2)}) copy-start(bf16[3,512,1024]{1,2,0:T(8,128)(2,1)S(1)} %copy.25) | copy-start | bytes 9437188
  30.0 1.7 copy-start
  31.7 6.0 %copy-start.14 = (bf16[64,128]{1,0:T(8,128)(2,1)S(1)}, bf16[64,128]{1,0:T(8,128)(2,1)}, u32[]{:S(2)}) copy-start(bf16[64,128]{1,0:T(8,128)(2,1)} %param.13) | copy-start | bytes 49156
  31.7 6.1 %copy-start.15 = (bf16[1024]{0:T(1024)(128)(2,1)S(1)}, bf16[1024]{0:T(1024)(128)(2,1)}, u32[]{:S(2)}) copy-start(bf16[1024]{0:T(1024)(128)(2,1)} %param.14) | copy-start | bytes 6148
  32.0 1.1 copy-start.8
  33.2 7.0 %collective-permute-start.1 = (bf16[127,1024]{0,1:T(8,128)(2,1)S(1)}, bf16[127,1024]{0,1:T(8,128)(2,1)S(1)}, u32[]{:S(2)}, u32[]{:S(2)}) collective-permute-start(bf16[127,1024]{0,1:T(8,128)(2,1)S(1)} %slice.152), channel_id=1, source_target_pairs={{0,4},{4,8},{8,12},{12,16},{16,20},{20,24},{24,28},{1,5},{5,9},{9,... | collective-permute-start | bytes 780296 | tf_op jit(solution)/shard_map/ppermute | solution.py:12
  42.2 4.9 copy-start.9
  161.5 2.6 copy-start.1
  161.5 2.9 copy-start.10
  161.7 3.6 copy-start.7
  181.6 1.4 copy-start.5
  183.1 3.4 collective-permute-start.2
  288.0 3.8 copy-start.6
  291.7 1.9 copy-start.2
  293.6 1.9 copy-start.4
  293.6 2.5 copy-start.11
  293.6 2.7 copy-start.12
  309.1 0.7 copy-start.13
Sparse Core Ops, SparseCore 0:
  309.9 55.6 all-reduce.8
where the time goes:
time: 515 us; the launch traced here: 509 us
  local copies, waits for them, and re-layouts  244 us (47%)
  matrix products  112 us (22%)
  other arithmetic  54.1 us (11%)
  blocking collectives  41 us (8%)
  loops' own time  34.4 us (7%)
  between operations  14.4 us (3%)
  starting transfers between devices  8.24 us (2%)
    dot_general x32, matrix products, apply_one_step(): jnp.einsum('gts,bsgi->btgi', band[:, :, :block_rows], part_left, preferre...  57.2 us
    reshape x16, local copies, waits for them, and re-layouts, filter_one_step(): diagonal = flat.reshape(step, block_rows, span + 1)[:, :, :filter_taps]  55.8 us
    reshape x32, local copies, waits for them, and re-layouts, band_matrix(): shaped = tiled.reshape(groups, block_rows, width)  55.3 us
    while x80, local copies, waits for them, and re-layouts  38.1 us
    psum x1, blocking collectives, body(): lax.psum((feat_grad, filter_grad, skip_grad), 'seq')  28.9 us
    dynamic_slice x48, local copies, waits for them, and re-layouts, apply_band(): pieces = lax.map(apply_one_step, jnp.arange(groups // step))  28.1 us
    another operation x2, loops' own time, apply_band(): pieces = lax.map(apply_one_step, jnp.arange(groups // step))  22.7 us
    dot_general x16, matrix products, filter_one_step(): jnp.einsum('btgi,bsgi->gts', part_cot, part_left, preferred_element_type=...  19.5 us
  transfers between devices with their start and end apart: 4, of which 1 were waited for; matrix products, arithmetic and copies ran while one was open for 31% of the time, Pallas kernels for 0%

commit v1 on v0

v1 whole, which is shorter than its diff:
```python
import functools
import math

import jax
import jax.numpy as jnp
from jax import lax
from jax.experimental import pallas as pl
from jax.experimental.pallas import tpu as pltpu
from jax.sharding import PartitionSpec as P

F32 = jnp.float32
BF16 = jnp.bfloat16
LANES = 128
HALO = 8
EDGE = 16


def matmul(a, b, contract):
    return lax.dot_general(
        a, b, ((contract[0], contract[1]), ((), ())), preferred_element_type=F32
    )


def featurize(buf, part, start, rows, taps_ref):
    taps = taps_ref.shape[1]
    total = None
    for tap in range(taps):
        weight = taps_ref[part, tap : tap + 1, :].astype(F32)
        term = weight * buf[part, start - tap : start - tap + rows, :]
        total = term if total is None else total + term
    return total.astype(BF16)


def lag_masks(block):
    row = lax.broadcasted_iota(jnp.int32, (block, block), 0)
    col = lax.broadcasted_iota(jnp.int32, (block, block), 1)
    return row, col


def front_kernel(
    x_ref, taps_ref, filt_ref, cot_ref,
    kv_ref, q0_ref, pt_ref, qt_ref, ct_ref, w_ref,
    buf,
):
    parts, rows, lanes = x_ref.shape
    groups, block = filt_ref.shape
    members = lanes // groups
    blocks = rows // block
    buf[:, :HALO, :] = jnp.zeros((parts, HALO, lanes), F32)
    for part in range(parts):
        buf[part, HALO:, :] = x_ref[part].astype(F32)
    for number in range(blocks):
        span = slice(number * block, (number + 1) * block)
        start = HALO + number * block
        q, k, v = (featurize(buf, part, start, block, taps_ref) for part in range(3))
        kv_ref[0, span, :] = k
        kv_ref[1, span, :] = v
        if number == 0:
            q0_ref[...] = q
        else:
            place = slice((number - 1) * members, number * members)
            product = (k.astype(F32) * v.astype(F32)).astype(BF16)
            pt_ref[:, place, :] = product.T.reshape(groups, members, block)
            qt_ref[:, place, :] = q.T.reshape(groups, members, block)
        place = slice(number * members, (number + 1) * members)
        ct_ref[:, place, :] = cot_ref[span, :].T.reshape(groups, members, block)
    row, col = lag_masks(block)
    for group in range(groups):
        taps = jnp.broadcast_to(filt_ref[group : group + 1, :].astype(F32), (block, block))
        circ = pltpu.roll(taps, 0, 1, stride=1, stride_axis=0)
        w_ref[group, :block, :] = jnp.where(col >= row, circ, 0.0).astype(BF16)
        w_ref[group, block:, :] = jnp.where(col < row, circ, 0.0).astype(BF16)


def skip_columns(skip_ref, block):
    lanes = skip_ref.shape[1]
    return jnp.broadcast_to(skip_ref[...].astype(F32), (block, lanes)).T


def middle_kernel(
    rim_ref, x0_ref, taps_ref, skip_ref, kv_ref, q0_ref, pt_ref, qt_ref, ct_ref, w_ref,
    kvr_ref, pta_ref, qta_ref, inner_ref, stats_ref,
    buf, acc,
):
    block = q0_ref.shape[0]
    groups, width, lanes = w_ref.shape[0], ct_ref.shape[1], q0_ref.shape[1]
    members = lanes // groups
    blocks = width // members
    tail = block + HALO
    step = pl.program_id(0)

    @pl.when(step == 0)
    def _():
        acc[...] = jnp.zeros_like(acc)

    for part in range(2):
        buf[1 + part, :tail, :] = rim_ref[part * tail : (part + 1) * tail, :].astype(F32)
        buf[1 + part, tail : tail + EDGE, :] = x0_ref[1 + part].astype(F32)
    buf[0, :HALO, :] = rim_ref[2 * tail : 2 * tail + HALO, :].astype(F32)
    buf[0, HALO : HALO + EDGE, :] = x0_ref[0].astype(F32)
    q_edge = featurize(buf, 0, HALO, EDGE, taps_ref)
    k_rim = featurize(buf, 1, HALO, block, taps_ref)
    v_rim = featurize(buf, 2, HALO, block, taps_ref)
    k_edge = featurize(buf, 1, tail, EDGE, taps_ref)
    v_edge = featurize(buf, 2, tail, EDGE, taps_ref)
    kvr_ref[0, :block, :] = k_rim
    kvr_ref[1, :block, :] = v_rim
    kvr_ref[0, block:, :] = k_edge
    kvr_ref[1, block:, :] = v_edge
    k0 = jnp.concatenate([k_edge, kv_ref[0, EDGE:, :]], axis=0)
    v0 = jnp.concatenate([v_edge, kv_ref[1, EDGE:, :]], axis=0)
    q0 = jnp.concatenate([q_edge, q0_ref[EDGE:, :]], axis=0)
    p_rim = (k_rim.astype(F32) * v_rim.astype(F32)).astype(BF16)
    p0 = (k0.astype(F32) * v0.astype(F32)).astype(BF16)
    pta_ref[:, :members, :] = p_rim.T.reshape(groups, members, block)
    pta_ref[:, members:, :] = p0.T.reshape(groups, members, block)
    qta_ref[...] = q0.T.reshape(groups, members, block)
    skip = skip_columns(skip_ref, block)
    for group in range(groups):
        every = jnp.concatenate([pta_ref[group], pt_ref[group]], axis=0)
        now = every[members:]
        filtered = matmul(
            jnp.concatenate([now, every[:width]], axis=1), w_ref[group], ((1,), (0,))
        )
        own = skip[group * members : (group + 1) * members]
        own = jnp.concatenate([own] * blocks, axis=0)
        inner = filtered + own * now.astype(F32)
        inner_ref[group] = inner
        q = jnp.concatenate([qta_ref[group], qt_ref[group]], axis=0).astype(F32)
        output = q * inner
        square = output * output
        cross = ct_ref[group].astype(F32) * output
        for number in range(blocks):
            for half in range(0, members, 8):
                at = number * members + half
                place = slice(number * 8, number * 8 + 8)
                acc[0, place, :] += square[at : at + 8]
                acc[1, place, :] += cross[at : at + 8]

    @pl.when(step == pl.num_programs(0) - 1)
    def _():
        for which in range(2):
            for number in range(blocks):
                at = which * blocks + number
                stats_ref[at : at + 1, :] = jnp.sum(
                    acc[which, number * 8 : number * 8 + 8, :], axis=0, keepdims=True
                )


def back_kernel(
    channels_all, token_scale, n_stats, *refs
):
    stats_refs = refs[:n_stats]
    (rim_ref, x_ref, skip_ref, kv_ref, kvr_ref, pt_ref, pta_ref, qt_ref, qta_ref, ct_ref,
     inner_ref, w_ref, out_ref, buf, coef, skip_acc, filt_acc, pg, qg, gn) = refs[n_stats:]
    parts, rows, lanes = x_ref.shape
    groups, width, block = ct_ref.shape
    members = lanes // groups
    blocks = rows // block
    tail = block + HALO
    taps = 7
    step = pl.program_id(0)

    @pl.when(step == 0)
    def _():
        if n_stats == 4:
            total = (stats_refs[0][...] + stats_refs[1][...]) + (stats_refs[2][...] + stats_refs[3][...])
        else:
            total = stats_refs[0][...]
        square = total[:blocks]
        cross = total[blocks : 2 * blocks] / channels_all
        rms = jnp.sqrt(square / channels_all + 1e-05)
        inv = token_scale / rms
        fall = token_scale * cross / (rms * rms * rms)
        for number in range(blocks):
            place = slice(number * members, (number + 1) * members)
            coef[0, place, :] = jnp.broadcast_to(inv[number : number + 1], (members, block))
            coef[1, place, :] = jnp.broadcast_to(fall[number : number + 1], (members, block))

    buf[0, tail - HALO : tail, :] = rim_ref[2 * tail : 2 * tail + HALO, :].astype(F32)
    for part in range(parts):
        if part:
            buf[part, :tail, :] = rim_ref[(part - 1) * tail : part * tail, :].astype(F32)
        buf[part, tail:, :] = x_ref[part].astype(F32)
    skip = skip_columns(skip_ref, block)
    row, col = lag_masks(block)
    near_side = col <= row
    for group in range(groups):
        members_at = slice(group * members, (group + 1) * members)
        every = jnp.concatenate([pta_ref[group], pt_ref[group]], axis=0)
        now = every[members:]
        q = jnp.concatenate([qta_ref[group], qt_ref[group]], axis=0).astype(F32)
        inner = inner_ref[group]
        output = q * inner
        out_grad = coef[0] * ct_ref[group].astype(F32) - coef[1] * output
        conv_grad = out_grad * q
        cot = conv_grad.astype(BF16)
        query_grad = out_grad * inner
        weighted = conv_grad * now.astype(F32)
        part_sum = weighted[:members]
        for number in range(1, blocks):
            part_sum = part_sum + weighted[number * members : (number + 1) * members]
        skip_acc[members_at, :] = part_sum
        gap = jnp.zeros((members, block), BF16)
        here = jnp.concatenate([gap, cot], axis=0)
        later = jnp.concatenate([cot, gap], axis=0)
        grad = matmul(here, w_ref[group, :block, :], ((1,), (1,))) + matmul(
            later, w_ref[group, block:, :], ((1,), (1,))
        )
        own = skip[members_at]
        pg[0, members_at, :] = grad[:members]
        for number in range(blocks):
            span = slice(number * members, (number + 1) * members)
            pg[1 + number, members_at, :] = (
                grad[(number + 1) * members : (number + 2) * members] + own * conv_grad[span]
            )
            qg[number, members_at, :] = query_grad[span]
        both = matmul(cot, jnp.concatenate([now, every[:width]], axis=1), ((0,), (0,)))
        lagged = jnp.where(near_side, both[:, :block], both[:, block:])
        skewed = lagged[:8]
        for at in range(8, block, 8):
            skewed = skewed + pltpu.roll(lagged[at : at + 8], block - at, 1)
        filt_acc[group * 8 : group * 8 + 8, :] = skewed
    flip = jnp.where(((row + col) % block) == 0, 1.0, 0.0).astype(F32)
    lags = filt_acc[pl.ds(0, groups, stride=8), :]
    for at in range(1, 8):
        lags = lags + pltpu.roll(filt_acc[pl.ds(at, groups, stride=8), :], block - at, 1)
    out_ref[3 * 8 :, :] = lax.dot_general(
        lags, flip, (((1,), (0,)), ((), ())),
        preferred_element_type=F32, precision=lax.Precision.HIGHEST,
    )
    skip_row = jnp.sum(skip_acc[...].T, axis=0, keepdims=True)
    for number in range(blocks + 1):
        span = slice(number * block, (number + 1) * block)
        back = pg[number].T
        if number == 0:
            k, v = kvr_ref[0, :block, :], kvr_ref[1, :block, :]
        elif number == 1:
            k = jnp.concatenate([kvr_ref[0, block:, :], kv_ref[0, EDGE:block, :]], axis=0)
            v = jnp.concatenate([kvr_ref[1, block:, :], kv_ref[1, EDGE:block, :]], axis=0)
        else:
            local = slice((number - 1) * block, number * block)
            k, v = kv_ref[0, local, :], kv_ref[1, local, :]
        gn[1, span, :] = back * v.astype(F32)
        gn[2, span, :] = back * k.astype(F32)
        if number:
            gn[0, span, :] = qg[number - 1].T
    chunk = 64
    for part in range(parts):
        first = 0 if part else block
        sums = [None] * taps
        for at in range(first, rows + block, chunk):
            grads = gn[part, at : at + chunk, :]
            for tap in range(taps):
                start = HALO + at - tap
                term = grads * buf[part, start : start + chunk, :]
                term = term.reshape(chunk // 8, 8, lanes).sum(axis=0)
                sums[tap] = term if sums[tap] is None else sums[tap] + term
        for tap in range(taps):
            at = part * 8 + tap
            out_ref[at : at + 1, :] = jnp.sum(sums[tap], axis=0, keepdims=True)
        out_ref[part * 8 + taps : part * 8 + 8, :] = skip_row


def finish_kernel(n_in, *refs):
    ins = refs[:n_in]
    feat_ref, filt_ref, skip_ref = refs[n_in:]
    if n_in == 4:
        total = (ins[0][...].astype(F32) + ins[1][...].astype(F32)) + (
            ins[2][...].astype(F32) + ins[3][...].astype(F32)
        )
    else:
        total = ins[0][...].astype(F32)
    taps = feat_ref.shape[1]
    for part in range(feat_ref.shape[0]):
        feat_ref[part] = total[part * 8 : part * 8 + taps]
    skip_ref[...] = total[taps : taps + 1]
    filt_ref[...] = total[24:]


def shifted(array, axis, by):
    length = lax.axis_size(axis)
    pairs = [(i, i + by) for i in range(length) if 0 <= i + by < length]
    return lax.ppermute(array, axis, pairs)


def crossed(array, axis, bit):
    length = lax.axis_size(axis)
    return lax.ppermute(array, axis, [(i, i ^ bit) for i in range(length)])


def quartet(array, axis, bit):
    return [array] + [crossed(array, axis, bit * k) for k in (1, 2, 3)]


def merged(parts):
    if len(parts) == 1:
        return parts[0]
    return (parts[0] + parts[1]) + (parts[2] + parts[3])


def body(projected, featurizer, long_filter, skip_gain, out_cotangent):
    parts, rows, channels = projected.shape
    groups, block = long_filter.shape
    taps = featurizer.shape[0]
    members = channels // groups
    chunk_groups = LANES // members
    chunks = channels // LANES
    blocks = rows // block
    width = blocks * members
    tail = block + HALO
    taps_major = jnp.transpose(featurizer, (1, 0, 2))
    skip_row = skip_gain.reshape(1, channels)
    params = pltpu.CompilerParams(vmem_limit_bytes=56 * 1024 * 1024)

    packed = jnp.concatenate(
        [projected[1, rows - tail :], projected[2, rows - tail :], projected[0, rows - HALO :]], axis=0
    )
    rim = shifted(packed, "seq", 1)

    whole = lambda *shape: pl.BlockSpec(shape, lambda i: (0,) * (len(shape) - 1) + (i,))
    grouped = lambda *shape: pl.BlockSpec((chunk_groups,) + shape, lambda i: (i,) + (0,) * len(shape))
    sds = jax.ShapeDtypeStruct

    kv, q0, pt, qt, ct, w = pl.pallas_call(
        front_kernel,
        name="front",
        grid=(chunks,),
        in_specs=[
            whole(parts, rows, LANES),
            whole(parts, taps, LANES),
            pl.BlockSpec((chunk_groups, block), lambda i: (i, 0)),
            whole(rows, LANES),
        ],
        out_specs=[
            whole(2, rows, LANES),
            whole(block, LANES),
            grouped(width - members, block),
            grouped(width - members, block),
            grouped(width, block),
            grouped(2 * block, block),
        ],
        out_shape=[
            sds((2, rows, channels), BF16),
            sds((block, channels), BF16),
            sds((groups, width - members, block), BF16),
            sds((groups, width - members, block), BF16),
            sds((groups, width, block), BF16),
            sds((groups, 2 * block, block), BF16),
        ],
        scratch_shapes=[pltpu.VMEM((parts, HALO + rows, LANES), F32)],
        compiler_params=params,
    )(projected, taps_major, long_filter, out_cotangent)

    kvr, pta, qta, inner, stats = pl.pallas_call(
        middle_kernel,
        name="middle",
        grid=(chunks,),
        in_specs=[
            whole(2 * tail + HALO, LANES),
            whole(parts, EDGE, LANES),
            whole(parts, taps, LANES),
            whole(1, LANES),
            whole(2, block, LANES),
            whole(block, LANES),
            grouped(width - members, block),
            grouped(width - members, block),
            grouped(width, block),
            grouped(2 * block, block),
        ],
        out_specs=[
            whole(2, block + EDGE, LANES),
            grouped(2 * members, block),
            grouped(members, block),
            grouped(width, block),
            pl.BlockSpec((2 * blocks, block), lambda i: (0, 0)),
        ],
        out_shape=[
            sds((2, block + EDGE, channels), BF16),
            sds((groups, 2 * members, block), BF16),
            sds((groups, members, block), BF16),
            sds((groups, width, block), F32),
            sds((2 * blocks, block), F32),
        ],
        scratch_shapes=[
            pltpu.VMEM((parts, tail + EDGE, LANES), F32),
            pltpu.VMEM((2, 8 * blocks, block), F32),
        ],
        compiler_params=params,
    )(rim, projected, taps_major, skip_row, kv, q0, pt, qt, ct, w)

    dp_size = lax.axis_size("dp")
    stat_parts = [stats]
    bit = 1
    while bit < dp_size:
        current = merged(stat_parts)
        if bit * 4 <= dp_size:
            stat_parts = quartet(current, "dp", bit)
            bit *= 4
        else:
            stat_parts = [current + crossed(current, "dp", bit)]
            bit *= 2
    token_scale = 1.0 / math.sqrt(rows * lax.axis_size("seq"))
    small = pl.BlockSpec((2 * blocks, block), lambda i: (0, 0))
    out = pl.pallas_call(
        functools.partial(back_kernel, channels * dp_size, token_scale, len(stat_parts)),
        name="back",
        grid=(chunks,),
        in_specs=[small] * len(stat_parts)
        + [
            whole(2 * tail + HALO, LANES),
            whole(parts, rows, LANES),
            whole(1, LANES),
            whole(2, rows, LANES),
            whole(2, block + EDGE, LANES),
            grouped(width - members, block),
            grouped(2 * members, block),
            grouped(width - members, block),
            grouped(members, block),
            grouped(width, block),
            grouped(width, block),
            grouped(2 * block, block),
        ],
        out_specs=whole(24 + chunk_groups, LANES),
        out_shape=sds((24 + chunk_groups, channels), F32),
        scratch_shapes=[
            pltpu.VMEM((parts, tail + rows, LANES), F32),
            pltpu.VMEM((2, width, block), F32),
            pltpu.VMEM((LANES, block), F32),
            pltpu.VMEM((chunk_groups * 8, block), F32),
            pltpu.VMEM((blocks + 1, LANES, block), F32),
            pltpu.VMEM((blocks, LANES, block), F32),
            pltpu.VMEM((parts, block + rows, LANES), F32),
        ],
        compiler_params=params,
    )(*stat_parts, rim, projected, skip_row, kv, kvr, pt, pta, qt, qta, ct, inner, w)

    seq_size = lax.axis_size("seq")
    out_parts = [out + crossed(out, "seq", 1)]
    bit = 2
    while bit < seq_size:
        current = merged(out_parts) if len(out_parts) == 1 else merged([o.astype(F32) for o in out_parts])
        current = current.astype(BF16)
        if bit * 4 <= seq_size:
            out_parts = quartet(current, "seq", bit)
            bit *= 4
        else:
            out_parts = [current.astype(F32) + crossed(current, "seq", bit).astype(F32)]
            bit *= 2

    feat, filt, skip = pl.pallas_call(
        functools.partial(finish_kernel, len(out_parts)),
        name="finish",
        grid=(chunks,),
        in_specs=[whole(24 + chunk_groups, LANES)] * len(out_parts),
        out_specs=[
            whole(parts, taps, LANES),
            pl.BlockSpec((chunk_groups, block), lambda i: (i, 0)),
            whole(1, LANES),
        ],
        out_shape=[
            sds((parts, taps, channels), F32),
            sds((groups, block), F32),
            sds((1, channels), F32),
        ],
        compiler_params=params,
    )(*out_parts)
    return (jnp.transpose(feat, (1, 0, 2)), filt, skip.reshape(channels))


def solution(mesh):
    return jax.shard_map(
        body,
        mesh=mesh,
        in_specs=(
            P(None, "seq", "dp"),
            P(None, None, "dp"),
            P("dp", None),
            P("dp"),
            P("seq", "dp"),
        ),
        out_specs=(P(None, None, "dp"), P("dp", None), P("dp")),
        check_vma=False,
    )
```

time: 515 us -> 64.2 us (0.12); the launches traced: 509 us -> 63.1 us
  local copies, waits for them, and re-layouts: 244 us -> 4.54 us
  matrix products: 112 us -> 0 us
  other arithmetic: 54.1 us -> 0.96 us
  blocking collectives: 41 us -> 0 us
  Pallas kernels: 0 us -> 36.2 us
  loops' own time: 34.4 us -> 0 us
  between operations: 14.4 us -> 0.72 us
  waiting for transfers between devices: 0.65 us -> 9.19 us
    reshape x50 -> x1, local copies, waits for them, and re-layouts: 115 us -> 0.6 us  [body(): skip_row = skip_gain.reshape(1, channels)]
    dot_general x96 -> x0, matrix products: 112 us -> none  [the longest x32 57.2 us: apply_one_step(): jnp.einsum('gts,bsgi->btgi', band[:, :, :block_rows], part_left, preferre...]
    while x83 -> x0, local copies, waits for them, and re-layouts: 41.4 us -> none
    psum x2 -> x0, blocking collectives: 41 us -> none  [the longest x1 28.9 us: body(): lax.psum((feat_grad, filter_grad, skip_grad), 'seq')]
    pallas_call x0 -> x4, Pallas kernels: none -> 36.2 us  [the longest x1 13.7 us: body(): pl.pallas_call(functools.partial(back_kernel, channels * dp_size, token_s...]
    reduce_sum x19 -> x0, other arithmetic: 35.1 us -> none  [the longest x16 17.4 us: filter_one_step(): return jnp.sum(diagonal, axis=1)]
    another operation x3 -> x0, loops' own time: 34.4 us -> none  [the longest x2 22.7 us: apply_band(): pieces = lax.map(apply_one_step, jnp.arange(groups // step))]
    dynamic_slice x96 -> x0, local copies, waits for them, and re-layouts: 29 us -> none  [the longest x48 28.1 us: apply_band(): pieces = lax.map(apply_one_step, jnp.arange(groups // step))]
  transfers between devices with their start and end apart: 4 -> 8, of which waited for: 1 -> 6; matrix products, arithmetic and copies ran while one was open for 31% -> 1% of each run, Pallas kernels for 0% -> 15%
where the time goes in v1:
time: 64.2 us; the launch traced here: 63.1 us
  Pallas kernels  36.2 us (56%)
  starting transfers between devices  11.5 us (18%)
  waiting for transfers between devices  9.19 us (14%)
  local copies, waits for them, and re-layouts  4.54 us (7%)
  other arithmetic  0.96 us (1%)
  between operations  0.72 us (1%)
    pallas_call x1, Pallas kernels, body(): pl.pallas_call(functools.partial(back_kernel, channels * dp_size, token_s...  13.7 us
    pallas_call x1, Pallas kernels, body(): pl.pallas_call(front_kernel, name='front', grid=(chunks,), in_specs=[whol...  9.27 us
    ppermute x7, waiting for transfers between devices, crossed(): return lax.ppermute(array, axis, [(i, i ^ bit) for i in range(length)])  9.19 us
    ppermute x7, starting transfers between devices, crossed(): return lax.ppermute(array, axis, [(i, i ^ bit) for i in range(length)])  9.06 us
    pallas_call x1, Pallas kernels, body(): pl.pallas_call(middle_kernel, name='middle', grid=(chunks,), in_specs=[wh...  8.97 us
    pallas_call x1, Pallas kernels, body(): pl.pallas_call(functools.partial(finish_kernel, len(out_parts)), name='fi...  4.28 us
    ppermute x1, starting transfers between devices, shifted(): return lax.ppermute(array, axis, pairs)  2.43 us
    unnamed x18, local copies, waits for them, and re-layouts  2.14 us
  transfers between devices with their start and end apart: 8, of which 6 were waited for; matrix products, arithmetic and copies ran while one was open for 1% of the time, Pallas kernels for 15%

profile of v1, /device:TPU:0, one launch (start us, length us, event | category | flops | bytes accessed | tf_op | source)
XLA Modules:
  0.0 63.1 jit_solution(13427000685018819325)
XLA Ops:
  0.6 0.0 copy-start.8
  0.6 0.7 %slice_bitcast_fusion.2 = bf16[8,1024]{1,0:T(8,128)(2,1)S(1)} fusion(bf16[3,512,1024]{2,1,0:T(8,128)(2,1)} %refs_5_.1), kind=kLoop, calls=%fused_computation.4 | loop fusion | bytes 32768 | tf_op jit(solution)/shard_map/squeeze | solution.py:317
  1.4 1.1 %slice_bitcast_fusion.1 = (bf16[136,1024]{1,0:T(8,128)(2,1)S(1)}, bf16[136,1024]{1,0:T(8,128)(2,1)S(1)}) fusion(bf16[3,512,1024]{2,1,0:T(8,128)(2,1)} %refs_5_.1), kind=kLoop, calls=%fused_computation.2 | loop fusion | bytes 1114112 | tf_op jit(solution)/shard_map/squeeze | solution.py:317
  2.5 2.4 %collective-permute-start = (bf16[280,1024]{1,0:T(8,128)(2,1)S(1)}, bf16[280,1024]{1,0:T(8,128)(2,1)S(1)}, u32[]{:S(2)}, u32[]{:S(2)}) collective-permute-start(bf16[280,1024]{1,0:T(8,128)(2,1)S(1)} %pad_maximum_fusion), channel_id=1, source_target_pairs={{0,4},{4,8},{8,12},{12,16},{16,20},{20,24},{24,28},{1,5},{5,9},{9,... | collective-permute-start | bytes 1720328 | tf_op jit(solution)/shard_map/ppermute | solution.py:284
  4.9 0.0 copy-done.8
  4.9 0.6 reshape.12.skip_ref.refs_6_
  5.5 9.3 %front.1 = (bf16[2,512,1024]{2,1,0:T(8,128)(2,1)}, bf16[128,1024]{1,0:T(8,128)(2,1)}, bf16[64,48,128]{2,1,0:T(8,128)(2,1)}, bf16[64,48,128]{2,1,0:T(8,128)(2,1)}...) custom-call(bf16[3,512,1024]{2,1,0:T(8,128)(2,1)} %refs_5_.1, bf16[3,7,1024]{2,1,0:T(8,128)(2,1)} %bitcast.9, ...), custom_call_target="tpu_custom_call" | custom-call | tf_op jit(solution)/shard_map/front/pallas_call | solution.py:325
  14.8 0.0 collective-permute-done.rim_ref.refs_4_
  14.8 0.0 copy-start
  14.8 0.8 %copy-done = bf16[280,1024]{1,0:T(8,128)(2,1)} copy-done((bf16[280,1024]{1,0:T(8,128)(2,1)}, bf16[280,1024]{1,0:T(8,128)(2,1)S(1)}, u32[]{:S(2)}) %copy-start) | copy-done | bytes 573464
  15.6 9.0 %middle.1 = (bf16[2,144,1024]{2,1,0:T(8,128)(2,1)}, bf16[64,32,128]{2,1,0:T(8,128)(2,1)}, bf16[64,16,128]{2,1,0:T(8,128)(2,1)}, f32[64,64,128]{2,1,0:T(8,128)}, f32[8,128]{1,0:T(8,128)}) custom-call(bf16[280,1024]{1,0:T(8,128)(2,1)} %copy-done, bf16[3,512,1024]{2,1,0:T(8,128)(2,1)} %refs_5_.1, bf16[3,7,1024]{2,1,0:T(8,128)(2,1)} %bitcast.10, ...), custom_call_target="tpu_custom_call" | custom-call | tf_op jit(solution)/shard_map/middle/pallas_call | solution.py:355
  24.6 4.5 %collective-permute-start.3 = (f32[8,128]{1,0:T(8,128)}, f32[8,128]{1,0:T(8,128)S(1)}, u32[]{:S(2)}, u32[]{:S(2)}) collective-permute-start(f32[8,128]{1,0:T(8,128)} %get-tuple-element.23.refs_0_), channel_id=1, source_target_pairs={{0,3},{1,2},{2,1},{3,0},{4,7},{5,6},{6,5},{7,4},{8,11},{9,10},{10,... | collective-permute-start | bytes 12296 | tf_op jit(solution)/shard_map/ppermute | solution.py:289
  29.1 0.0 collective-permute-start.2
  29.1 0.6 %collective-permute-start.1 = (f32[8,128]{1,0:T(8,128)}, f32[8,128]{1,0:T(8,128)S(1)}, u32[]{:S(2)}, u32[]{:S(2)}) collective-permute-start(f32[8,128]{1,0:T(8,128)} %get-tuple-element.23.refs_0_), channel_id=1, source_target_pairs={{0,1},{1,0},{2,3},{3,2},{4,5},{5,4},{6,7},{7,6},{8,9},{9,8},{10,11... | collective-permute-start | bytes 12296 | tf_op jit(solution)/shard_map/ppermute | solution.py:289
  29.7 1.2 %collective-permute-done.3.refs_3_ = f32[8,128]{1,0:T(8,128)S(1)} collective-permute-done((f32[8,128]{1,0:T(8,128)}, f32[8,128]{1,0:T(8,128)S(1)}, u32[]{:S(2)}, u32[]{:S(2)}) %collective-permute-start.3) | collective-permute-done | bytes 4128 | tf_op jit(solution)/shard_map/ppermute | solution.py:289
  30.9 0.0 copy-start.5
  30.9 2.9 %collective-permute-done.2.refs_2_ = f32[8,128]{1,0:T(8,128)S(1)} collective-permute-done((f32[8,128]{1,0:T(8,128)}, f32[8,128]{1,0:T(8,128)S(1)}, u32[]{:S(2)}, u32[]{:S(2)}) %collective-permute-start.2) | collective-permute-done | bytes 4128 | tf_op jit(solution)/shard_map/ppermute | solution.py:289
  33.8 0.0 copy-start.6
  33.8 0.0 collective-permute-done.1.refs_1_
  33.8 0.0 copy-start.7
  33.8 0.0 copy-done.5
  33.8 0.6 copy-done.6
  34.4 0.0 copy-done.7
  34.4 13.7 %back.1 = f32[32,1024]{1,0:T(8,128)} custom-call(f32[8,128]{1,0:T(8,128)} %get-tuple-element.23.refs_0_, f32[8,128]{1,0:T(8,128)} %copy-done.7, f32[8,128]{1,0:T(8,128)} %copy-done.6, f32[8,128]{1,0:T(8,128)} %copy-done.5, bf16[280,1024]{1,0:T(8,128)(2,1)} %copy-done, bf16[3,512,1024]{2,1,0:T(8,128)(2,1)} %refs_5_.1, ...), custom_call_target="tpu_custom_call" | custom-call | tf_op jit(solution)/shard_map/back/pallas_call | solution.py:405
  48.1 0.4 collective-permute-start.4
  48.5 1.2 %collective-permute-done.4 = f32[32,1024]{1,0:T(8,128)S(1)} collective-permute-done((f32[32,1024]{1,0:T(8,128)}, f32[32,1024]{1,0:T(8,128)S(1)}, u32[]{:S(2)}, u32[]{:S(2)}) %collective-permute-start.4) | collective-permute-done | bytes 131104 | tf_op jit(solution)/shard_map/ppermute | solution.py:289
  49.8 0.9 %add_convert_fusion.refs_0_ = bf16[32,1024]{1,0:T(8,128)(2,1)S(1)} fusion(f32[32,1024]{1,0:T(8,128)} %back.1, f32[32,1024]{1,0:T(8,128)S(1)} %collective-permute-done.4), kind=kLoop, calls=%fused_computation.3 | loop fusion | flops 65536 | bytes 327680 | tf_op jit(solution)/shard_map/convert_element_type | solution.py:443
  50.7 0.0 copy-start.1
  50.7 2.7 %collective-permute-start.7 = (bf16[32,1024]{1,0:T(8,128)(2,1)S(1)}, bf16[32,1024]{1,0:T(8,128)(2,1)S(1)}, u32[]{:S(2)}, u32[]{:S(2)}) collective-permute-start(bf16[32,1024]{1,0:T(8,128)(2,1)S(1)} %add_convert_fusion.refs_0_), channel_id=1, source_target_pairs={{0,24},{4,28},{8,16},{12,20},{16,8},{20,12},{24,0},{28,4},{1,25},{... | collective-permute-start | bytes 196616 | tf_op jit(solution)/shard_map/ppermute | solution.py:289
  53.4 0.5 collective-permute-start.6
  53.9 0.4 collective-permute-start.5
  54.3 1.7 %collective-permute-done.7.refs_3_ = bf16[32,1024]{1,0:T(8,128)(2,1)S(1)} collective-permute-done((bf16[32,1024]{1,0:T(8,128)(2,1)S(1)}, bf16[32,1024]{1,0:T(8,128)(2,1)S(1)}, u32[]{:S(2)}, u32[]{:S(2)}) %collective-permute-start.7) | collective-permute-done | bytes 65568 | tf_op jit(solution)/shard_map/ppermute | solution.py:289
  56.0 0.0 copy-start.2
  56.0 1.6 %collective-permute-done.6.refs_2_ = bf16[32,1024]{1,0:T(8,128)(2,1)S(1)} collective-permute-done((bf16[32,1024]{1,0:T(8,128)(2,1)S(1)}, bf16[32,1024]{1,0:T(8,128)(2,1)S(1)}, u32[]{:S(2)}, u32[]{:S(2)}) %collective-permute-start.6) | collective-permute-done | bytes 65568 | tf_op jit(solution)/shard_map/ppermute | solution.py:289
  57.6 0.0 copy-start.3
  57.6 0.5 collective-permute-done.5.refs_1_
  58.1 0.0 copy-done.1
  58.1 0.0 copy-done.2
  58.1 0.1 copy-done.3
  58.2 0.0 copy-start.4
  58.2 0.6 copy-done.4
  58.9 4.3 %finish.1 = (f32[3,7,1024]{2,1,0:T(8,128)}, f32[64,128]{1,0:T(8,128)}, f32[1,1024]{1,0:T(1,128)}) custom-call(bf16[32,1024]{1,0:T(8,128)(2,1)} %copy-done.1, bf16[32,1024]{1,0:T(8,128)(2,1)} %copy-done.4, bf16[32,1024]{1,0:T(8,128)(2,1)} %copy-done.3, bf16[32,1024]{1,0:T(8,128)(2,1)} %copy-done.2), custom_call_target="tpu_custom_call" | custom-call | tf_op jit(solution)/shard_map/finish/pallas_call | solution.py:451
  (1 shorter events, 0.0 us)
Async XLA Ops:
  0.6 4.3 %copy-start.8 = (bf16[1024]{0:T(1024)(128)(2,1)S(1)}, bf16[1024]{0:T(1024)(128)(2,1)}, u32[]{:S(2)}) copy-start(bf16[1024]{0:T(1024)(128)(2,1)} %param.8) | copy-start | bytes 6148
  2.5 12.3 %collective-permute-start = (bf16[280,1024]{1,0:T(8,128)(2,1)S(1)}, bf16[280,1024]{1,0:T(8,128)(2,1)S(1)}, u32[]{:S(2)}, u32[]{:S(2)}) collective-permute-start(bf16[280,1024]{1,0:T(8,128)(2,1)S(1)} %pad_maximum_fusion), channel_id=1, source_target_pairs={{0,4},{4,8},{8,12},{12,16},{16,20},{20,24},{24,28},{1,5},{5,9},{9,... | collective-permute-start | bytes 1720328 | tf_op jit(solution)/shard_map/ppermute | solution.py:284
  14.8 0.8 %copy-start = (bf16[280,1024]{1,0:T(8,128)(2,1)}, bf16[280,1024]{1,0:T(8,128)(2,1)S(1)}, u32[]{:S(2)}) copy-start(bf16[280,1024]{1,0:T(8,128)(2,1)S(1)} %collective-permute-done.rim_ref.refs_4_) | copy-start | bytes 1720324
  24.6 6.3 %collective-permute-start.3 = (f32[8,128]{1,0:T(8,128)}, f32[8,128]{1,0:T(8,128)S(1)}, u32[]{:S(2)}, u32[]{:S(2)}) collective-permute-start(f32[8,128]{1,0:T(8,128)} %get-tuple-element.23.refs_0_), channel_id=1, source_target_pairs={{0,3},{1,2},{2,1},{3,0},{4,7},{5,6},{6,5},{7,4},{8,11},{9,10},{10,... | collective-permute-start | bytes 12296 | tf_op jit(solution)/shard_map/ppermute | solution.py:289
  29.1 4.7 %collective-permute-start.2 = (f32[8,128]{1,0:T(8,128)}, f32[8,128]{1,0:T(8,128)S(1)}, u32[]{:S(2)}, u32[]{:S(2)}) collective-permute-start(f32[8,128]{1,0:T(8,128)} %get-tuple-element.23.refs_0_), channel_id=1, source_target_pairs={{0,2},{1,3},{2,0},{3,1},{4,6},{5,7},{6,4},{7,5},{8,10},{9,11},{10,... | collective-permute-start | bytes 12296 | tf_op jit(solution)/shard_map/ppermute | solution.py:289
  29.1 4.7 %collective-permute-start.1 = (f32[8,128]{1,0:T(8,128)}, f32[8,128]{1,0:T(8,128)S(1)}, u32[]{:S(2)}, u32[]{:S(2)}) collective-permute-start(f32[8,128]{1,0:T(8,128)} %get-tuple-element.23.refs_0_), channel_id=1, source_target_pairs={{0,1},{1,0},{2,3},{3,2},{4,5},{5,4},{6,7},{7,6},{8,9},{9,8},{10,11... | collective-permute-start | bytes 12296 | tf_op jit(solution)/shard_map/ppermute | solution.py:289
  30.9 2.9 %copy-start.5 = (f32[8,128]{1,0:T(8,128)}, f32[8,128]{1,0:T(8,128)S(1)}, u32[]{:S(2)}) copy-start(f32[8,128]{1,0:T(8,128)S(1)} %collective-permute-done.3.refs_3_) | copy-start | bytes 12292
  33.8 0.6 copy-start.6
  33.8 0.6 copy-start.7
  48.1 1.6 %collective-permute-start.4 = (f32[32,1024]{1,0:T(8,128)}, f32[32,1024]{1,0:T(8,128)S(1)}, u32[]{:S(2)}, u32[]{:S(2)}) collective-permute-start(f32[32,1024]{1,0:T(8,128)} %back.1), channel_id=1, source_target_pairs={{0,4},{4,0},{8,12},{12,8},{16,20},{20,16},{24,28},{28,24},{1,5},{5... | collective-permute-start | bytes 393224 | tf_op jit(solution)/shard_map/ppermute | solution.py:289
  50.7 7.4 %copy-start.1 = (bf16[32,1024]{1,0:T(8,128)(2,1)}, bf16[32,1024]{1,0:T(8,128)(2,1)S(1)}, u32[]{:S(2)}) copy-start(bf16[32,1024]{1,0:T(8,128)(2,1)S(1)} %add_convert_fusion.refs_0_) | copy-start | bytes 196612
  50.7 5.3 %collective-permute-start.7 = (bf16[32,1024]{1,0:T(8,128)(2,1)S(1)}, bf16[32,1024]{1,0:T(8,128)(2,1)S(1)}, u32[]{:S(2)}, u32[]{:S(2)}) collective-permute-start(bf16[32,1024]{1,0:T(8,128)(2,1)S(1)} %add_convert_fusion.refs_0_), channel_id=1, source_target_pairs={{0,24},{4,28},{8,16},{12,20},{16,8},{20,12},{24,0},{28,4},{1,25},{... | collective-permute-start | bytes 196616 | tf_op jit(solution)/shard_map/ppermute | solution.py:289
  53.4 4.3 %collective-permute-start.6 = (bf16[32,1024]{1,0:T(8,128)(2,1)S(1)}, bf16[32,1024]{1,0:T(8,128)(2,1)S(1)}, u32[]{:S(2)}, u32[]{:S(2)}) collective-permute-start(bf16[32,1024]{1,0:T(8,128)(2,1)S(1)} %add_convert_fusion.refs_0_), channel_id=1, source_target_pairs={{0,16},{4,20},{8,24},{12,28},{16,0},{20,4},{24,8},{28,12},{1,17},{... | collective-permute-start | bytes 196616 | tf_op jit(solution)/shard_map/ppermute | solution.py:289
  53.9 4.3 %collective-permute-start.5 = (bf16[32,1024]{1,0:T(8,128)(2,1)S(1)}, bf16[32,1024]{1,0:T(8,128)(2,1)S(1)}, u32[]{:S(2)}, u32[]{:S(2)}) collective-permute-start(bf16[32,1024]{1,0:T(8,128)(2,1)S(1)} %add_convert_fusion.refs_0_), channel_id=1, source_target_pairs={{0,8},{4,12},{8,0},{12,4},{16,24},{20,28},{24,16},{28,20},{1,9},{5... | collective-permute-start | bytes 196616 | tf_op jit(solution)/shard_map/ppermute | solution.py:289
  56.0 2.1 %copy-start.2 = (bf16[32,1024]{1,0:T(8,128)(2,1)}, bf16[32,1024]{1,0:T(8,128)(2,1)S(1)}, u32[]{:S(2)}) copy-start(bf16[32,1024]{1,0:T(8,128)(2,1)S(1)} %collective-permute-done.7.refs_3_) | copy-start | bytes 196612
  57.6 0.6 copy-start.3
  58.2 0.6 copy-start.4

commit v2 on v1

--- a/solution.py
+++ b/solution.py
@@ -42,11 +42,33 @@
     kv_ref, q0_ref, pt_ref, qt_ref, ct_ref, w_ref,
     buf,
 ):
+    parts, rows, channels = x_ref.shape
+    block = filt_ref.shape[1]
+    members = channels // filt_ref.shape[0]
+    groups = LANES // members
+    blocks = rows // block
+    buf[:, :HALO, :] = jnp.zeros((parts, HALO, LANES), F32)
+
+    @pl.loop(0, channels // LANES)
+    def _(chunk):
+        lane = pl.ds(pl.multiple_of(chunk * LANES, LANES), LANES)
+        group_at = pl.ds(pl.multiple_of(chunk * groups, groups), groups)
+        front_chunk(
+            x_ref.at[:, :, lane], taps_ref.at[:, :, lane], filt_ref.at[group_at], cot_ref.at[:, lane],
+            kv_ref.at[:, :, lane], q0_ref.at[:, lane], pt_ref.at[group_at], qt_ref.at[group_at],
+            ct_ref.at[group_at], w_ref.at[group_at], buf,
+        )
+
+
+def front_chunk(
+    x_ref, taps_ref, filt_ref, cot_ref,
+    kv_ref, q0_ref, pt_ref, qt_ref, ct_ref, w_ref,
+    buf,
+):
     parts, rows, lanes = x_ref.shape
     groups, block = filt_ref.shape
     members = lanes // groups
     blocks = rows // block
-    buf[:, :HALO, :] = jnp.zeros((parts, HALO, lanes), F32)
     for part in range(parts):
         buf[part, HALO:, :] = x_ref[part].astype(F32)
     for number in range(blocks):
@@ -78,8 +100,39 @@
 
 
 def middle_kernel(
+    rim_ref, x_ref, taps_ref, skip_ref, kv_ref, q0_ref, pt_ref, qt_ref, ct_ref, w_ref,
+    kvr_ref, pta_ref, qta_ref, inner_ref, stats_ref,
+    buf, acc,
+):
+    channels = rim_ref.shape[1]
+    block = q0_ref.shape[0]
+    members = channels // w_ref.shape[0]
+    groups = LANES // members
+    blocks = ct_ref.shape[1] // members
+    acc[...] = jnp.zeros_like(acc)
+
+    @pl.loop(0, channels // LANES)
+    def _(chunk):
+        lane = pl.ds(pl.multiple_of(chunk * LANES, LANES), LANES)
+        group_at = pl.ds(pl.multiple_of(chunk * groups, groups), groups)
+        middle_chunk(
+            rim_ref.at[:, lane], x_ref.at[:, :EDGE, lane], taps_ref.at[:, :, lane], skip_ref.at[:, lane],
+            kv_ref.at[:, :block, lane], q0_ref.at[:, lane], pt_ref.at[group_at], qt_ref.at[group_at],
+            ct_ref.at[group_at], w_ref.at[group_at], kvr_ref.at[:, :, lane], pta_ref.at[group_at],
+            qta_ref.at[group_at], inner_ref.at[group_at], buf, acc,
+        )
+
+    for which in range(2):
+        for number in range(blocks):
+            at = which * blocks + number
+            stats_ref[at : at + 1, :] = jnp.sum(
+                acc[which, number * 8 : number * 8 + 8, :], axis=0, keepdims=True
+            )
+
+
+def middle_chunk(
     rim_ref, x0_ref, taps_ref, skip_ref, kv_ref, q0_ref, pt_ref, qt_ref, ct_ref, w_ref,
-    kvr_ref, pta_ref, qta_ref, inner_ref, stats_ref,
+    kvr_ref, pta_ref, qta_ref, inner_ref,
     buf, acc,
 ):
     block = q0_ref.shape[0]
@@ -87,12 +140,6 @@
     members = lanes // groups
     blocks = width // members
     tail = block + HALO
-    step = pl.program_id(0)
-
-    @pl.when(step == 0)
-    def _():
-        acc[...] = jnp.zeros_like(acc)
-
     for part in range(2):
         buf[1 + part, :tail, :] = rim_ref[part * tail : (part + 1) * tail, :].astype(F32)
         buf[1 + part, tail : tail + EDGE, :] = x0_ref[1 + part].astype(F32)
@@ -137,46 +184,48 @@
                 acc[0, place, :] += square[at : at + 8]
                 acc[1, place, :] += cross[at : at + 8]
 
-    @pl.when(step == pl.num_programs(0) - 1)
-    def _():
-        for which in range(2):
-            for number in range(blocks):
-                at = which * blocks + number
-                stats_ref[at : at + 1, :] = jnp.sum(
-                    acc[which, number * 8 : number * 8 + 8, :], axis=0, keepdims=True
-                )
-
-
-def back_kernel(
-    channels_all, token_scale, n_stats, *refs
-):
+
+def back_kernel(channels_all, token_scale, taps, n_stats, *refs):
     stats_refs = refs[:n_stats]
     (rim_ref, x_ref, skip_ref, kv_ref, kvr_ref, pt_ref, pta_ref, qt_ref, qta_ref, ct_ref,
      inner_ref, w_ref, out_ref, buf, coef, skip_acc, filt_acc, pg, qg, gn) = refs[n_stats:]
+    parts, rows, channels = x_ref.shape
+    block = ct_ref.shape[2]
+    members = channels // ct_ref.shape[0]
+    groups = LANES // members
+    blocks = rows // block
+    total = merged([ref[...] for ref in stats_refs])
+    square = total[:blocks]
+    cross = total[blocks : 2 * blocks] / channels_all
+    rms = jnp.sqrt(square / channels_all + 1e-05)
+    inv = token_scale / rms
+    fall = token_scale * cross / (rms * rms * rms)
+    for number in range(blocks):
+        place = slice(number * members, (number + 1) * members)
+        coef[0, place, :] = jnp.broadcast_to(inv[number : number + 1], (members, block))
+        coef[1, place, :] = jnp.broadcast_to(fall[number : number + 1], (members, block))
+
+    @pl.loop(0, channels // LANES)
+    def _(chunk):
+        lane = pl.ds(pl.multiple_of(chunk * LANES, LANES), LANES)
+        group_at = pl.ds(pl.multiple_of(chunk * groups, groups), groups)
+        back_chunk(
+            taps, rim_ref.at[:, lane], x_ref.at[:, :, lane], skip_ref.at[:, lane], kv_ref.at[:, :, lane],
+            kvr_ref.at[:, :, lane], pt_ref.at[group_at], pta_ref.at[group_at], qt_ref.at[group_at],
+            qta_ref.at[group_at], ct_ref.at[group_at], inner_ref.at[group_at], w_ref.at[group_at],
+            out_ref.at[:, lane], buf, coef, skip_acc, filt_acc, pg, qg, gn,
+        )
+
+
+def back_chunk(
+    taps, rim_ref, x_ref, skip_ref, kv_ref, kvr_ref, pt_ref, pta_ref, qt_ref, qta_ref, ct_ref,
+    inner_ref, w_ref, out_ref, buf, coef, skip_acc, filt_acc, pg, qg, gn,
+):
     parts, rows, lanes = x_ref.shape
     groups, width, block = ct_ref.shape
     members = lanes // groups
     blocks = rows // block
     tail = block + HALO
-    taps = 7
-    step = pl.program_id(0)
-
-    @pl.when(step == 0)
-    def _():
-        if n_stats == 4:
-            total = (stats_refs[0][...] + stats_refs[1][...]) + (stats_refs[2][...] + stats_refs[3][...])
-        else:
-            total = stats_refs[0][...]
-        square = total[:blocks]
-        cross = total[blocks : 2 * blocks] / channels_all
-        rms = jnp.sqrt(square / channels_all + 1e-05)
-        inv = token_scale / rms
-        fall = token_scale * cross / (rms * rms * rms)
-        for number in range(blocks):
-            place = slice(number * members, (number + 1) * members)
-            coef[0, place, :] = jnp.broadcast_to(inv[number : number + 1], (members, block))
-            coef[1, place, :] = jnp.broadcast_to(fall[number : number + 1], (members, block))
-
     buf[0, tail - HALO : tail, :] = rim_ref[2 * tail : 2 * tail + HALO, :].astype(F32)
     for part in range(parts):
         if part:
@@ -265,17 +314,14 @@
 def finish_kernel(n_in, *refs):
     ins = refs[:n_in]
     feat_ref, filt_ref, skip_ref = refs[n_in:]
-    if n_in == 4:
-        total = (ins[0][...].astype(F32) + ins[1][...].astype(F32)) + (
-            ins[2][...].astype(F32) + ins[3][...].astype(F32)
-        )
-    else:
-        total = ins[0][...].astype(F32)
+    total = merged([ref[...].astype(F32) for ref in ins])
     taps = feat_ref.shape[1]
     for part in range(feat_ref.shape[0]):
         feat_ref[part] = total[part * 8 : part * 8 + taps]
     skip_ref[...] = total[taps : taps + 1]
-    filt_ref[...] = total[24:]
+    groups = total.shape[0] - 24
+    for chunk in range(total.shape[1] // LANES):
+        filt_ref[chunk * groups : (chunk + 1) * groups, :] = total[24:, chunk * LANES : (chunk + 1) * LANES]
 
 
 def shifted(array, axis, by):
@@ -297,6 +343,22 @@
     if len(parts) == 1:
         return parts[0]
     return (parts[0] + parts[1]) + (parts[2] + parts[3])
+
+
+def on_chip(name, kernel, out_shape, scratch, args, final=False):
+    place = pl.BlockSpec(memory_space=pltpu.VMEM)
+    if not final:
+        out_shape = [pltpu.VMEM(out.shape, out.dtype) for out in out_shape]
+    args = [pltpu.with_memory_space_constraint(arg, pltpu.VMEM) for arg in args]
+    return pl.pallas_call(
+        kernel,
+        name=name,
+        in_specs=[place] * len(args),
+        out_specs=[place] * len(out_shape),
+        out_shape=out_shape,
+        scratch_shapes=scratch,
+        compiler_params=pltpu.CompilerParams(vmem_limit_bytes=16 * 1024 * 1024),
+    )(*args)
 
 
 def body(projected, featurizer, long_filter, skip_gain, out_cotangent):
@@ -305,42 +367,23 @@
     taps = featurizer.shape[0]
     members = channels // groups
     chunk_groups = LANES // members
-    chunks = channels // LANES
     blocks = rows // block
     width = blocks * members
     tail = block + HALO
     taps_major = jnp.transpose(featurizer, (1, 0, 2))
     skip_row = skip_gain.reshape(1, channels)
-    params = pltpu.CompilerParams(vmem_limit_bytes=56 * 1024 * 1024)
 
     packed = jnp.concatenate(
         [projected[1, rows - tail :], projected[2, rows - tail :], projected[0, rows - HALO :]], axis=0
     )
     rim = shifted(packed, "seq", 1)
 
-    whole = lambda *shape: pl.BlockSpec(shape, lambda i: (0,) * (len(shape) - 1) + (i,))
-    grouped = lambda *shape: pl.BlockSpec((chunk_groups,) + shape, lambda i: (i,) + (0,) * len(shape))
     sds = jax.ShapeDtypeStruct
 
-    kv, q0, pt, qt, ct, w = pl.pallas_call(
+    kv, q0, pt, qt, ct, w = on_chip(
+        "front",
         front_kernel,
-        name="front",
-        grid=(chunks,),
-        in_specs=[
-            whole(parts, rows, LANES),
-            whole(parts, taps, LANES),
-            pl.BlockSpec((chunk_groups, block), lambda i: (i, 0)),
-            whole(rows, LANES),
-        ],
-        out_specs=[
-            whole(2, rows, LANES),
-            whole(block, LANES),
-            grouped(width - members, block),
-            grouped(width - members, block),
-            grouped(width, block),
-            grouped(2 * block, block),
-        ],
-        out_shape=[
+        [
             sds((2, rows, channels), BF16),
             sds((block, channels), BF16),
             sds((groups, width - members, block), BF16),
@@ -348,46 +391,25 @@
             sds((groups, width, block), BF16),
             sds((groups, 2 * block, block), BF16),
         ],
-        scratch_shapes=[pltpu.VMEM((parts, HALO + rows, LANES), F32)],
-        compiler_params=params,
-    )(projected, taps_major, long_filter, out_cotangent)
-
-    kvr, pta, qta, inner, stats = pl.pallas_call(
+        [pltpu.VMEM((parts, HALO + rows, LANES), F32)],
+        (projected, taps_major, long_filter, out_cotangent),
+    )
+    kvr, pta, qta, inner, stats = on_chip(
+        "middle",
         middle_kernel,
-        name="middle",
-        grid=(chunks,),
-        in_specs=[
-            whole(2 * tail + HALO, LANES),
-            whole(parts, EDGE, LANES),
-            whole(parts, taps, LANES),
-            whole(1, LANES),
-            whole(2, block, LANES),
-            whole(block, LANES),
-            grouped(width - members, block),
-            grouped(width - members, block),
-            grouped(width, block),
-            grouped(2 * block, block),
-        ],
-        out_specs=[
-            whole(2, block + EDGE, LANES),
-            grouped(2 * members, block),
-            grouped(members, block),
-            grouped(width, block),
-            pl.BlockSpec((2 * blocks, block), lambda i: (0, 0)),
-        ],
-        out_shape=[
+        [
             sds((2, block + EDGE, channels), BF16),
             sds((groups, 2 * members, block), BF16),
             sds((groups, members, block), BF16),
             sds((groups, width, block), F32),
             sds((2 * blocks, block), F32),
         ],
-        scratch_shapes=[
+        [
             pltpu.VMEM((parts, tail + EDGE, LANES), F32),
             pltpu.VMEM((2, 8 * blocks, block), F32),
         ],
-        compiler_params=params,
-    )(rim, projected, taps_major, skip_row, kv, q0, pt, qt, ct, w)
+        (rim, projected, taps_major, skip_row, kv, q0, pt, qt, ct, w),
+    )
 
     dp_size = lax.axis_size("dp")
     stat_parts = [stats]
@@ -401,29 +423,11 @@
             stat_parts = [current + crossed(current, "dp", bit)]
             bit *= 2
     token_scale = 1.0 / math.sqrt(rows * lax.axis_size("seq"))
-    small = pl.BlockSpec((2 * blocks, block), lambda i: (0, 0))
-    out = pl.pallas_call(
-        functools.partial(back_kernel, channels * dp_size, token_scale, len(stat_parts)),
-        name="back",
-        grid=(chunks,),
-        in_specs=[small] * len(stat_parts)
-        + [
-            whole(2 * tail + HALO, LANES),
-            whole(parts, rows, LANES),
-            whole(1, LANES),
-            whole(2, rows, LANES),
-            whole(2, block + EDGE, LANES),
-            grouped(width - members, block),
-            grouped(2 * members, block),
-            grouped(width - members, block),
-            grouped(members, block),
-            grouped(width, block),
-            grouped(width, block),
-            grouped(2 * block, block),
-        ],
-        out_specs=whole(24 + chunk_groups, LANES),
-        out_shape=sds((24 + chunk_groups, channels), F32),
-        scratch_shapes=[
+    (out,) = on_chip(
+        "back",
+        functools.partial(back_kernel, channels * dp_size, token_scale, taps, len(stat_parts)),
+        [sds((24 + chunk_groups, channels), F32)],
+        [
             pltpu.VMEM((parts, tail + rows, LANES), F32),
             pltpu.VMEM((2, width, block), F32),
             pltpu.VMEM((LANES, block), F32),
@@ -432,15 +436,14 @@
             pltpu.VMEM((blocks, LANES, block), F32),
             pltpu.VMEM((parts, block + rows, LANES), F32),
         ],
-        compiler_params=params,
-    )(*stat_parts, rim, projected, skip_row, kv, kvr, pt, pta, qt, qta, ct, inner, w)
+        (*stat_parts, rim, projected, skip_row, kv, kvr, pt, pta, qt, qta, ct, inner, w),
+    )
 
     seq_size = lax.axis_size("seq")
     out_parts = [out + crossed(out, "seq", 1)]
     bit = 2
     while bit < seq_size:
-        current = merged(out_parts) if len(out_parts) == 1 else merged([o.astype(F32) for o in out_parts])
-        current = current.astype(BF16)
+        current = merged([part.astype(F32) for part in out_parts]).astype(BF16)
         if bit * 4 <= seq_size:
             out_parts = quartet(current, "seq", bit)
             bit *= 4
@@ -448,23 +451,18 @@
             out_parts = [current.astype(F32) + crossed(current, "seq", bit).astype(F32)]
             bit *= 2
 
-    feat, filt, skip = pl.pallas_call(
+    feat, filt, skip = on_chip(
+        "finish",
         functools.partial(finish_kernel, len(out_parts)),
-        name="finish",
-        grid=(chunks,),
-        in_specs=[whole(24 + chunk_groups, LANES)] * len(out_parts),
-        out_specs=[
-            whole(parts, taps, LANES),
-            pl.BlockSpec((chunk_groups, block), lambda i: (i, 0)),
-            whole(1, LANES),
-        ],
-        out_shape=[
+        [
             sds((parts, taps, channels), F32),
             sds((groups, block), F32),
             sds((1, channels), F32),
         ],
-        compiler_params=params,
-    )(*out_parts)
+        [],
+        out_parts,
+        final=True,
+    )
     return (jnp.transpose(feat, (1, 0, 2)), filt, skip.reshape(channels))
 
 

time: 64.2 us -> 47.7 us (0.74); the launches traced: 63.1 us -> 47.5 us
  Pallas kernels: 36.2 us -> 20.9 us
  starting transfers between devices: 11.5 us -> 13.6 us
  other arithmetic: 0.96 us -> 0.06 us
  waiting for transfers between devices: 9.19 us -> 8.42 us
  local copies, waits for them, and re-layouts: 4.54 us -> 3.79 us
    pallas_call x4, Pallas kernels: 36.2 us -> 20.9 us  [on_chip(): pl.pallas_call(kernel, name=name, in_specs=[place] * len(args), out_specs...]
    ppermute x7, starting transfers between devices: 9.06 us -> 11.1 us  [crossed(): return lax.ppermute(array, axis, [(i, i ^ bit) for i in range(length)])]
    convert_element_type x1, other arithmetic: 0.92 us -> 0.02 us  [body(): current = merged([part.astype(F32) for part in out_parts]).astype(BF16)]
    ppermute x7, waiting for transfers between devices: 9.19 us -> 8.42 us  [crossed(): return lax.ppermute(array, axis, [(i, i ^ bit) for i in range(length)])]
    unnamed x18 -> x10, local copies, waits for them, and re-layouts: 2.14 us -> 1.9 us
  transfers between devices with their start and end apart: 8 -> 8, of which waited for: 6 -> 6; matrix products, arithmetic and copies ran while one was open for 1% -> 0% of each run, Pallas kernels for 15% -> 12%
where the time goes in v2:
time: 47.7 us; the launch traced here: 47.5 us
  Pallas kernels  20.9 us (44%)
  starting transfers between devices  13.6 us (29%)
  waiting for transfers between devices  8.42 us (18%)
  local copies, waits for them, and re-layouts  3.79 us (8%)
  between operations  0.77 us (2%)
    pallas_call x4, Pallas kernels, on_chip(): pl.pallas_call(kernel, name=name, in_specs=[place] * len(args), out_specs...  20.9 us
    ppermute x7, starting transfers between devices, crossed(): return lax.ppermute(array, axis, [(i, i ^ bit) for i in range(length)])  11.1 us
    ppermute x7, waiting for transfers between devices, crossed(): return lax.ppermute(array, axis, [(i, i ^ bit) for i in range(length)])  8.42 us
    ppermute x1, starting transfers between devices, shifted(): return lax.ppermute(array, axis, pairs)  2.43 us
    unnamed x10, local copies, waits for them, and re-layouts  1.9 us
    squeeze x1, local copies, waits for them, and re-layouts, body(): projected[1, rows - tail:]  1.08 us
  transfers between devices with their start and end apart: 8, of which 6 were waited for; matrix products, arithmetic and copies ran while one was open for 0% of the time, Pallas kernels for 12%

profile of v2, /device:TPU:0, one launch (start us, length us, event | category | flops | bytes accessed | tf_op | source)
XLA Modules:
  0.0 47.5 jit_solution(8785695997290437521)
XLA Ops:
  0.6 0.0 copy-start.4
  0.6 0.0 copy-start.1
  0.7 0.0 copy-start.3
  0.7 0.0 copy-start.2
  0.7 0.8 %slice_bitcast_fusion.2 = bf16[8,1024]{1,0:T(8,128)(2,1)S(1)} fusion(bf16[3,512,1024]{2,1,0:T(8,128)(2,1)} %refs_5_.1), kind=kLoop, calls=%fused_computation.4 | loop fusion | bytes 32768 | tf_op jit(solution)/shard_map/squeeze | solution.py:377
  1.5 1.1 %slice_bitcast_fusion.1 = (bf16[136,1024]{1,0:T(8,128)(2,1)S(1)}, bf16[136,1024]{1,0:T(8,128)(2,1)S(1)}) fusion(bf16[3,512,1024]{2,1,0:T(8,128)(2,1)} %refs_5_.1), kind=kLoop, calls=%fused_computation.2 | loop fusion | bytes 1114112 | tf_op jit(solution)/shard_map/squeeze | solution.py:377
  2.6 2.4 %collective-permute-start = (bf16[280,1024]{1,0:T(8,128)(2,1)S(1)}, bf16[280,1024]{1,0:T(8,128)(2,1)S(1)}, u32[]{:S(2)}, u32[]{:S(2)}) collective-permute-start(bf16[280,1024]{1,0:T(8,128)(2,1)S(1)} %pad_maximum_fusion), channel_id=1, source_target_pairs={{0,4},{4,8},{8,12},{12,16},{16,20},{20,24},{24,28},{1,5},{5,9},{9,... | collective-permute-start | bytes 1720328 | tf_op jit(solution)/shard_map/ppermute | solution.py:330
  5.0 0.0 copy-done.4
  5.1 0.0 copy-done.1
  5.1 0.0 copy-done.3
  5.1 0.0 copy-done.2
  5.1 0.0 copy-start
  5.1 1.9 %copy-done = bf16[3,512,1024]{2,1,0:T(8,128)(2,1)S(1)} copy-done((bf16[3,512,1024]{2,1,0:T(8,128)(2,1)S(1)}, bf16[3,512,1024]{2,1,0:T(8,128)(2,1)}, u32[]{:S(2)}) %copy-start) | copy-done | bytes 3145752
  7.0 5.6 %front.1 = (bf16[2,512,1024]{2,1,0:T(8,128)(2,1)S(1)}, bf16[128,1024]{1,0:T(8,128)(2,1)S(1)}, bf16[64,48,128]{2,1,0:T(8,128)(2,1)S(1)}, bf16[64,48,128]{2,1,0:T(...) custom-call(bf16[3,512,1024]{2,1,0:T(8,128)(2,1)S(1)} %copy-done, ...), custom_call_target="tpu_custom_call" | custom-call | tf_op jit(solution)/shard_map/front/pallas_call | solution.py:353
  12.6 0.0 collective-permute-done.rim_ref.refs_4_
  12.6 3.2 %middle.1 = (bf16[2,144,1024]{2,1,0:T(8,128)(2,1)S(1)}, bf16[64,32,128]{2,1,0:T(8,128)(2,1)S(1)}, bf16[64,16,128]{2,1,0:T(8,128)(2,1)S(1)}, f32[64,64,128]{2,1,0:T(8,128)S(1)}, f32[8,128]{1,0:T(8,128)S(1)}) custom-call(bf16[280,1024]{1,0:T(8,128)(2,1)S(1)} %collective-permute-done.rim_ref.refs_4_, bf16[3,512,1024]{2,1,0:T(8,128)(2,1)S(1)} %copy-done, ...), custom_call_target="tpu_custom_call" | custom-call | tf_op jit(solution)/shard_map/middle/pallas_call | solution.py:353
  15.8 4.5 %collective-permute-start.3 = (f32[8,128]{1,0:T(8,128)S(1)}, f32[8,128]{1,0:T(8,128)S(1)}, u32[]{:S(2)}, u32[]{:S(2)}) collective-permute-start(f32[8,128]{1,0:T(8,128)S(1)} %get-tuple-element.23.refs_0_), channel_id=1, source_target_pairs={{0,3},{1,2},{2,1},{3,0},{4,7},{5,6},{6,5},{7,4},{8,11},{9,10},{10,... | collective-permute-start | bytes 12296 | tf_op jit(solution)/shard_map/ppermute | solution.py:335
  20.3 0.0 collective-permute-start.2
  20.3 0.6 %collective-permute-start.1 = (f32[8,128]{1,0:T(8,128)S(1)}, f32[8,128]{1,0:T(8,128)S(1)}, u32[]{:S(2)}, u32[]{:S(2)}) collective-permute-start(f32[8,128]{1,0:T(8,128)S(1)} %get-tuple-element.23.refs_0_), channel_id=1, source_target_pairs={{0,1},{1,0},{2,3},{3,2},{4,5},{5,4},{6,7},{7,6},{8,9},{9,8},{10,11... | collective-permute-start | bytes 12296 | tf_op jit(solution)/shard_map/ppermute | solution.py:335
  20.9 0.9 %collective-permute-done.3.refs_3_ = f32[8,128]{1,0:T(8,128)S(1)} collective-permute-done((f32[8,128]{1,0:T(8,128)S(1)}, f32[8,128]{1,0:T(8,128)S(1)}, u32[]{:S(2)}, u32[]{:S(2)}) %collective-permute-start.3) | collective-permute-done | bytes 4128 | tf_op jit(solution)/shard_map/ppermute | solution.py:335
  21.9 2.9 %collective-permute-done.2.refs_2_ = f32[8,128]{1,0:T(8,128)S(1)} collective-permute-done((f32[8,128]{1,0:T(8,128)S(1)}, f32[8,128]{1,0:T(8,128)S(1)}, u32[]{:S(2)}, u32[]{:S(2)}) %collective-permute-start.2) | collective-permute-done | bytes 4128 | tf_op jit(solution)/shard_map/ppermute | solution.py:335
  24.8 0.0 collective-permute-done.1.refs_1_
  24.8 11.4 %back.1 = f32[32,1024]{1,0:T(8,128)S(1)} custom-call(f32[8,128]{1,0:T(8,128)S(1)} %get-tuple-element.23.refs_0_, f32[8,128]{1,0:T(8,128)S(1)} %collective-permute-done.1.refs_1_, f32[8,128]{1,0:T(8,128)S(1)} %collective-permute-done.2.refs_2_, f32[8,128]{1,0:T(8,128)S(1)} %collective-permute-done.3.refs_3_, ...), custom_call_target="tpu_custom_call" | custom-call | tf_op jit(solution)/shard_map/back/pallas_call | solution.py:353
  36.2 0.4 collective-permute-start.4
  36.6 1.0 %collective-permute-done.4 = f32[32,1024]{1,0:T(8,128)S(1)} collective-permute-done((f32[32,1024]{1,0:T(8,128)S(1)}, f32[32,1024]{1,0:T(8,128)S(1)}, u32[]{:S(2)}, u32[]{:S(2)}) %collective-permute-start.4) | collective-permute-done | bytes 131104 | tf_op jit(solution)/shard_map/ppermute | solution.py:335
  37.6 4.2 %collective-permute-start.7 = (bf16[32,1024]{1,0:T(8,128)(2,1)S(1)}, bf16[32,1024]{1,0:T(8,128)(2,1)S(1)}, u32[]{:S(2)}, u32[]{:S(2)}) collective-permute-start(bf16[32,1024]{1,0:T(8,128)(2,1)S(1)} %add_convert_fusion.refs_0_), channel_id=1, source_target_pairs={{0,24},{4,28},{8,16},{12,20},{16,8},{20,12},{24,0},{28,4},{1,25},{... | collective-permute-start | bytes 196616 | tf_op jit(solution)/shard_map/ppermute | solution.py:335
  41.8 0.5 %collective-permute-start.6 = (bf16[32,1024]{1,0:T(8,128)(2,1)S(1)}, bf16[32,1024]{1,0:T(8,128)(2,1)S(1)}, u32[]{:S(2)}, u32[]{:S(2)}) collective-permute-start(bf16[32,1024]{1,0:T(8,128)(2,1)S(1)} %add_convert_fusion.refs_0_), channel_id=1, source_target_pairs={{0,16},{4,20},{8,24},{12,28},{16,0},{20,4},{24,8},{28,12},{1,17},{... | collective-permute-start | bytes 196616 | tf_op jit(solution)/shard_map/ppermute | solution.py:335
  42.3 0.9 %collective-permute-start.5 = (bf16[32,1024]{1,0:T(8,128)(2,1)S(1)}, bf16[32,1024]{1,0:T(8,128)(2,1)S(1)}, u32[]{:S(2)}, u32[]{:S(2)}) collective-permute-start(bf16[32,1024]{1,0:T(8,128)(2,1)S(1)} %add_convert_fusion.refs_0_), channel_id=1, source_target_pairs={{0,8},{4,12},{8,0},{12,4},{16,24},{20,28},{24,16},{28,20},{1,9},{5... | collective-permute-start | bytes 196616 | tf_op jit(solution)/shard_map/ppermute | solution.py:335
  43.3 1.0 %collective-permute-done.7.refs_3_ = bf16[32,1024]{1,0:T(8,128)(2,1)S(1)} collective-permute-done((bf16[32,1024]{1,0:T(8,128)(2,1)S(1)}, bf16[32,1024]{1,0:T(8,128)(2,1)S(1)}, u32[]{:S(2)}, u32[]{:S(2)}) %collective-permute-start.7) | collective-permute-done | bytes 65568 | tf_op jit(solution)/shard_map/ppermute | solution.py:335
  44.2 1.9 %collective-permute-done.6.refs_2_ = bf16[32,1024]{1,0:T(8,128)(2,1)S(1)} collective-permute-done((bf16[32,1024]{1,0:T(8,128)(2,1)S(1)}, bf16[32,1024]{1,0:T(8,128)(2,1)S(1)}, u32[]{:S(2)}, u32[]{:S(2)}) %collective-permute-start.6) | collective-permute-done | bytes 65568 | tf_op jit(solution)/shard_map/ppermute | solution.py:335
  46.1 0.7 %collective-permute-done.5.refs_1_ = bf16[32,1024]{1,0:T(8,128)(2,1)S(1)} collective-permute-done((bf16[32,1024]{1,0:T(8,128)(2,1)S(1)}, bf16[32,1024]{1,0:T(8,128)(2,1)S(1)}, u32[]{:S(2)}, u32[]{:S(2)}) %collective-permute-start.5) | collective-permute-done | bytes 65568 | tf_op jit(solution)/shard_map/ppermute | solution.py:335
  46.8 0.7 %finish.1 = (f32[3,7,1024]{2,1,0:T(8,128)}, f32[64,128]{1,0:T(8,128)}, f32[1,1024]{1,0:T(1,128)}) custom-call(bf16[32,1024]{1,0:T(8,128)(2,1)S(1)} %add_convert_fusion.refs_0_, bf16[32,1024]{1,0:T(8,128)(2,1)S(1)} %collective-permute-done.5.refs_1_, bf16[32,1024]{1,0:T(8,128)(2,1)S(1)} %collective-permute-done.6.refs_2_, ...), custom_call_target="tpu_custom_call" | custom-call | tf_op jit(solution)/shard_map/finish/pallas_call | solution.py:353
  (3 shorter events, 0.1 us)
Async XLA Ops:
  0.6 4.4 %copy-start.4 = (bf16[1024]{0:T(1024)(128)(2,1)S(1)}, bf16[1024]{0:T(1024)(128)(2,1)}, u32[]{:S(2)}) copy-start(bf16[1024]{0:T(1024)(128)(2,1)} %param.8) | copy-start | bytes 6148
  0.6 4.4 %copy-start.1 = (bf16[512,1024]{1,0:T(8,128)(2,1)S(1)}, bf16[512,1024]{1,0:T(8,128)(2,1)}, u32[]{:S(2)}) copy-start(bf16[512,1024]{1,0:T(8,128)(2,1)} %cot_ref.1) | copy-start | bytes 3145732
  0.7 4.4 %copy-start.3 = (bf16[64,128]{1,0:T(8,128)(2,1)S(1)}, bf16[64,128]{1,0:T(8,128)(2,1)}, u32[]{:S(2)}) copy-start(bf16[64,128]{1,0:T(8,128)(2,1)} %filt_ref.1) | copy-start | bytes 49156
  0.7 4.4 %copy-start.2 = (bf16[7,3,1024]{2,0,1:T(8,128)(2,1)S(1)}, bf16[7,3,1024]{2,0,1:T(8,128)(2,1)}, u32[]{:S(2)}) copy-start(bf16[7,3,1024]{2,0,1:T(8,128)(2,1)} %param.6) | copy-start | bytes 129028
  2.6 10.0 %collective-permute-start = (bf16[280,1024]{1,0:T(8,128)(2,1)S(1)}, bf16[280,1024]{1,0:T(8,128)(2,1)S(1)}, u32[]{:S(2)}, u32[]{:S(2)}) collective-permute-start(bf16[280,1024]{1,0:T(8,128)(2,1)S(1)} %pad_maximum_fusion), channel_id=1, source_target_pairs={{0,4},{4,8},{8,12},{12,16},{16,20},{20,24},{24,28},{1,5},{5,9},{9,... | collective-permute-start | bytes 1720328 | tf_op jit(solution)/shard_map/ppermute | solution.py:330
  5.1 1.9 %copy-start = (bf16[3,512,1024]{2,1,0:T(8,128)(2,1)S(1)}, bf16[3,512,1024]{2,1,0:T(8,128)(2,1)}, u32[]{:S(2)}) copy-start(bf16[3,512,1024]{2,1,0:T(8,128)(2,1)} %refs_5_.1) | copy-start | bytes 9437188
  15.8 6.1 %collective-permute-start.3 = (f32[8,128]{1,0:T(8,128)S(1)}, f32[8,128]{1,0:T(8,128)S(1)}, u32[]{:S(2)}, u32[]{:S(2)}) collective-permute-start(f32[8,128]{1,0:T(8,128)S(1)} %get-tuple-element.23.refs_0_), channel_id=1, source_target_pairs={{0,3},{1,2},{2,1},{3,0},{4,7},{5,6},{6,5},{7,4},{8,11},{9,10},{10,... | collective-permute-start | bytes 12296 | tf_op jit(solution)/shard_map/ppermute | solution.py:335
  20.3 4.5 %collective-permute-start.2 = (f32[8,128]{1,0:T(8,128)S(1)}, f32[8,128]{1,0:T(8,128)S(1)}, u32[]{:S(2)}, u32[]{:S(2)}) collective-permute-start(f32[8,128]{1,0:T(8,128)S(1)} %get-tuple-element.23.refs_0_), channel_id=1, source_target_pairs={{0,2},{1,3},{2,0},{3,1},{4,6},{5,7},{6,4},{7,5},{8,10},{9,11},{10,... | collective-permute-start | bytes 12296 | tf_op jit(solution)/shard_map/ppermute | solution.py:335
  20.3 4.5 %collective-permute-start.1 = (f32[8,128]{1,0:T(8,128)S(1)}, f32[8,128]{1,0:T(8,128)S(1)}, u32[]{:S(2)}, u32[]{:S(2)}) collective-permute-start(f32[8,128]{1,0:T(8,128)S(1)} %get-tuple-element.23.refs_0_), channel_id=1, source_target_pairs={{0,1},{1,0},{2,3},{3,2},{4,5},{5,4},{6,7},{7,6},{8,9},{9,8},{10,11... | collective-permute-start | bytes 12296 | tf_op jit(solution)/shard_map/ppermute | solution.py:335
  36.2 1.4 %collective-permute-start.4 = (f32[32,1024]{1,0:T(8,128)S(1)}, f32[32,1024]{1,0:T(8,128)S(1)}, u32[]{:S(2)}, u32[]{:S(2)}) collective-permute-start(f32[32,1024]{1,0:T(8,128)S(1)} %back.1), channel_id=1, source_target_pairs={{0,4},{4,0},{8,12},{12,8},{16,20},{20,16},{24,28},{28,24},{1,5},{5... | collective-permute-start | bytes 393224 | tf_op jit(solution)/shard_map/ppermute | solution.py:335
  37.6 6.6 %collective-permute-start.7 = (bf16[32,1024]{1,0:T(8,128)(2,1)S(1)}, bf16[32,1024]{1,0:T(8,128)(2,1)S(1)}, u32[]{:S(2)}, u32[]{:S(2)}) collective-permute-start(bf16[32,1024]{1,0:T(8,128)(2,1)S(1)} %add_convert_fusion.refs_0_), channel_id=1, source_target_pairs={{0,24},{4,28},{8,16},{12,20},{16,8},{20,12},{24,0},{28,4},{1,25},{... | collective-permute-start | bytes 196616 | tf_op jit(solution)/shard_map/ppermute | solution.py:335
  41.8 4.3 %collective-permute-start.6 = (bf16[32,1024]{1,0:T(8,128)(2,1)S(1)}, bf16[32,1024]{1,0:T(8,128)(2,1)S(1)}, u32[]{:S(2)}, u32[]{:S(2)}) collective-permute-start(bf16[32,1024]{1,0:T(8,128)(2,1)S(1)} %add_convert_fusion.refs_0_), channel_id=1, source_target_pairs={{0,16},{4,20},{8,24},{12,28},{16,0},{20,4},{24,8},{28,12},{1,17},{... | collective-permute-start | bytes 196616 | tf_op jit(solution)/shard_map/ppermute | solution.py:335
  42.3 4.5 %collective-permute-start.5 = (bf16[32,1024]{1,0:T(8,128)(2,1)S(1)}, bf16[32,1024]{1,0:T(8,128)(2,1)S(1)}, u32[]{:S(2)}, u32[]{:S(2)}) collective-permute-start(bf16[32,1024]{1,0:T(8,128)(2,1)S(1)} %add_convert_fusion.refs_0_), channel_id=1, source_target_pairs={{0,8},{4,12},{8,0},{12,4},{16,24},{20,28},{24,16},{28,20},{1,9},{5... | collective-permute-start | bytes 196616 | tf_op jit(solution)/shard_map/ppermute | solution.py:335

commit v3 on v2

v3 whole, which is shorter than its diff:
```python
import functools
import math

import jax
import jax.numpy as jnp
from jax import lax
from jax.experimental import pallas as pl
from jax.experimental.pallas import tpu as pltpu
from jax.sharding import PartitionSpec as P


F32 = jnp.float32
BF16 = jnp.bfloat16
LANES = 128
HALO = 8
EDGE = 16


def matmul(a, b, contract):
    return lax.dot_general(
        a, b, ((contract[0], contract[1]), ((), ())), preferred_element_type=F32
    )


def featurize(buf, part, start, rows, taps_ref):
    taps = taps_ref.shape[1]
    total = None
    for tap in range(taps):
        weight = taps_ref[part, tap : tap + 1, :].astype(F32)
        term = weight * buf[part, start - tap : start - tap + rows, :]
        total = term if total is None else total + term
    return total.astype(BF16)


def lag_masks(block):
    row = lax.broadcasted_iota(jnp.int32, (block, block), 0)
    col = lax.broadcasted_iota(jnp.int32, (block, block), 1)
    return row, col


def edge_kernel(x_ref, taps_hbm, near_ref, taps_ref, far_ref, buf, sems):
    _, rows, channels = x_ref.shape
    tail = far_ref.shape[1]
    block = tail - HALO
    copies = [
        pltpu.make_async_copy(
            x_ref.at[1 + part, pl.ds(rows - tail, tail), :], far_ref.at[part], sems.at[part]
        )
        for part in range(2)
    ]
    copies.append(
        pltpu.make_async_copy(
            x_ref.at[0, pl.ds(rows - HALO, HALO), :], near_ref.at[pl.ds(block, HALO), :], sems.at[2]
        )
    )
    copies.append(pltpu.make_async_copy(taps_hbm, taps_ref, sems.at[3]))
    for copy in copies:
        copy.start()
    for copy in copies:
        copy.wait()

    @pl.loop(0, channels // LANES)
    def _(chunk):
        lane = pl.ds(pl.multiple_of(chunk * LANES, LANES), LANES)
        for part in range(2):
            buf[1 + part] = far_ref[part, :, lane].astype(F32)
            at = block + (1 + part) * HALO
            near_ref[at : at + HALO, lane] = far_ref[part, tail - HALO :, lane]
        k = featurize(buf, 1, HALO, block, taps_ref.at[:, :, lane])
        v = featurize(buf, 2, HALO, block, taps_ref.at[:, :, lane])
        near_ref[:block, lane] = (k.astype(F32) * v.astype(F32)).astype(BF16)


def front_kernel(
    x_ref, taps_ref, filt_ref, cot_ref,
    far_ref, x_all, kv_ref, q0_ref, pt_ref, qt_ref, ct_ref, w_ref,
    buf, mask, cot_all, x_sems, cot_sems,
):
    parts, rows, channels = x_ref.shape
    block = filt_ref.shape[1]
    members = channels // filt_ref.shape[0]
    groups = LANES // members

    def copies(chunk):
        lane = pl.ds(pl.multiple_of(chunk * LANES, LANES), LANES)
        return (
            pltpu.make_async_copy(x_ref.at[:, :, lane], x_all.at[chunk], x_sems.at[chunk]),
            pltpu.make_async_copy(cot_ref.at[:, lane], cot_all.at[chunk], cot_sems.at[chunk]),
        )

    @pl.loop(0, channels // LANES)
    def _(chunk):
        for copy in copies(chunk):
            copy.start()

    buf[:, :HALO, :] = jnp.zeros((parts, HALO, LANES), F32)
    row, col = lag_masks(block)
    mask[...] = jnp.where(col >= row, 1.0, 0.0).astype(BF16)

    @pl.loop(0, channels // LANES)
    def _(chunk):
        rows_here = filt_ref[pl.ds(pl.multiple_of(chunk * groups, groups), groups), :].astype(F32)
        for number in range(groups):
            group = chunk * groups + number
            taps = jnp.broadcast_to(rows_here[number : number + 1], (block, block))
            circ = pltpu.roll(taps, 0, 1, stride=1, stride_axis=0).astype(BF16)
            near = circ * mask[...]
            w_ref[group, :block, :] = near
            w_ref[group, block:, :] = circ - near

    @pl.loop(0, channels // LANES)
    def _(chunk):
        lane = pl.ds(pl.multiple_of(chunk * LANES, LANES), LANES)
        group_at = pl.ds(pl.multiple_of(chunk * groups, groups), groups)
        for copy in copies(chunk):
            copy.wait()
        front_chunk(
            x_all.at[chunk], taps_ref.at[:, :, lane], cot_all.at[chunk],
            kv_ref.at[chunk], q0_ref.at[:, lane], pt_ref.at[group_at], qt_ref.at[group_at],
            ct_ref.at[group_at], buf,
        )
        tail = far_ref.shape[0] // 2
        for part in range(2):
            far_ref[part * tail : (part + 1) * tail, lane] = x_all[chunk, 1 + part, rows - tail :, :]


def front_chunk(x_ref, taps_ref, cot_ref, kv_ref, q0_ref, pt_ref, qt_ref, ct_ref, buf):
    parts, rows, lanes = x_ref.shape
    groups, _, block = ct_ref.shape
    members = lanes // groups
    blocks = rows // block
    for part in range(parts):
        buf[part, HALO:, :] = x_ref[part].astype(F32)
    for number in range(blocks):
        span = slice(number * block, (number + 1) * block)
        start = HALO + number * block
        q, k, v = (featurize(buf, part, start, block, taps_ref) for part in range(3))
        kv_ref[0, span, :] = k
        kv_ref[1, span, :] = v
        if number == 0:
            q0_ref[...] = q
        else:
            place = slice((number - 1) * members, number * members)
            product = (k.astype(F32) * v.astype(F32)).astype(BF16)
            pt_ref[:, place, :] = product.T.reshape(groups, members, block)
            qt_ref[:, place, :] = q.T.reshape(groups, members, block)
        place = slice(number * members, (number + 1) * members)
        ct_ref[:, place, :] = cot_ref[span, :].T.reshape(groups, members, block)


def skip_columns(skip_ref, block):
    lanes = skip_ref.shape[1]
    return jnp.broadcast_to(skip_ref[...].astype(F32), (block, lanes)).T


def middle_kernel(
    near_ref, x_ref, taps_ref, skip_ref, kv_ref, q0_ref, pt_ref, qt_ref, ct_ref, w_ref,
    kve_ref, pta_ref, qta_ref, inner_ref, stats_ref,
    buf, acc,
):
    channels = near_ref.shape[1]
    block = q0_ref.shape[0]
    members = channels // w_ref.shape[0]
    groups = LANES // members
    blocks = ct_ref.shape[1] // members
    acc[...] = jnp.zeros_like(acc)

    @pl.loop(0, channels // LANES)
    def _(chunk):
        lane = pl.ds(pl.multiple_of(chunk * LANES, LANES), LANES)
        group_at = pl.ds(pl.multiple_of(chunk * groups, groups), groups)
        middle_chunk(
            near_ref.at[:, lane], x_ref.at[chunk, :, :EDGE], taps_ref.at[:, :, lane], skip_ref.at[:, lane],
            kv_ref.at[chunk, :, :block], q0_ref.at[:, lane], pt_ref.at[group_at], qt_ref.at[group_at],
            ct_ref.at[group_at], w_ref.at[group_at], kve_ref.at[chunk], pta_ref.at[group_at],
            qta_ref.at[group_at], inner_ref.at[group_at], buf, acc,
        )

    for which in range(2):
        for number in range(blocks):
            at = which * blocks + number
            stats_ref[at : at + 1, :] = jnp.sum(
                acc[which, number * 8 : number * 8 + 8, :], axis=0, keepdims=True
            )


def middle_chunk(
    near_ref, x0_ref, taps_ref, skip_ref, kv_ref, q0_ref, pt_ref, qt_ref, ct_ref, w_ref,
    kve_ref, pta_ref, qta_ref, inner_ref,
    buf, acc,
):
    block = q0_ref.shape[0]
    groups, width, lanes = w_ref.shape[0], ct_ref.shape[1], q0_ref.shape[1]
    members = lanes // groups
    blocks = width // members
    for part in range(3):
        at = block + part * HALO
        buf[part, :HALO, :] = near_ref[at : at + HALO, :].astype(F32)
        buf[part, HALO:, :] = x0_ref[part].astype(F32)
    q_edge, k_edge, v_edge = (featurize(buf, part, HALO, EDGE, taps_ref) for part in range(3))
    kve_ref[0] = k_edge
    kve_ref[1] = v_edge
    k0 = jnp.concatenate([k_edge, kv_ref[0, EDGE:, :]], axis=0)
    v0 = jnp.concatenate([v_edge, kv_ref[1, EDGE:, :]], axis=0)
    q0 = jnp.concatenate([q_edge, q0_ref[EDGE:, :]], axis=0)
    p_rim = near_ref[:block, :]
    p0 = (k0.astype(F32) * v0.astype(F32)).astype(BF16)
    pta_ref[:, :members, :] = p_rim.T.reshape(groups, members, block)
    pta_ref[:, members:, :] = p0.T.reshape(groups, members, block)
    qta_ref[...] = q0.T.reshape(groups, members, block)
    skip = skip_columns(skip_ref, block)
    for group in range(groups):
        every = jnp.concatenate([pta_ref[group], pt_ref[group]], axis=0)
        now = every[members:]
        filtered = matmul(
            jnp.concatenate([now, every[:width]], axis=1), w_ref[group], ((1,), (0,))
        )
        own = skip[group * members : (group + 1) * members]
        own = jnp.concatenate([own] * blocks, axis=0)
        inner = filtered + own * now.astype(F32)
        inner_ref[group] = inner
        q = jnp.concatenate([qta_ref[group], qt_ref[group]], axis=0).astype(F32)
        output = q * inner
        square = output * output
        cross = ct_ref[group].astype(F32) * output
        for number in range(blocks):
            for half in range(0, members, 8):
                at = number * members + half
                place = slice(number * 8, number * 8 + 8)
                acc[0, place, :] += square[at : at + 8]
                acc[1, place, :] += cross[at : at + 8]


def prep_kernel(near_ref, x_ref, kv_ref, kve_ref, xf_ref, kvf_ref):
    parts, _, _ = x_ref.shape[1:]
    block = near_ref.shape[0] - parts * HALO

    @pl.loop(0, x_ref.shape[0])
    def _(chunk):
        lane = pl.ds(pl.multiple_of(chunk * LANES, LANES), LANES)
        for part in range(parts):
            at = block + part * HALO
            xf_ref[chunk, part, :HALO, :] = near_ref[at : at + HALO, lane].astype(F32)
            xf_ref[chunk, part, HALO:, :] = x_ref[chunk, part].astype(F32)
        for part in range(2):
            kvf_ref[chunk, part, :EDGE, :] = kve_ref[chunk, part].astype(F32)
            kvf_ref[chunk, part, EDGE:, :] = kv_ref[chunk, part, EDGE:, :].astype(F32)


def rim_kernel(far_ref, taps_ref, pgr_ref, out_ref, sum_ref, buf):
    chunks, block = pgr_ref.shape[:2]
    taps = taps_ref.shape[1]
    tail = block + HALO
    sum_ref[:8, :] = out_ref[:8, :]
    sum_ref[24:, :] = out_ref[24:, :]

    @pl.loop(0, chunks)
    def _(chunk):
        lane = pl.ds(pl.multiple_of(chunk * LANES, LANES), LANES)
        for part in range(2):
            buf[1 + part] = far_ref[part * tail : (part + 1) * tail, lane].astype(F32)
        back = pgr_ref[chunk].T
        for part in (1, 2):
            other = featurize(buf, 3 - part, HALO, block, taps_ref.at[:, :, lane]).astype(F32)
            grads = back * other
            for tap in range(taps):
                at = part * 8 + tap
                term = grads * buf[part, HALO - tap : HALO - tap + block, :]
                sum_ref[at : at + 1, lane] = out_ref[at : at + 1, lane] + jnp.sum(term, axis=0, keepdims=True)
            sum_ref[part * 8 + taps : part * 8 + 8, lane] = out_ref[part * 8 + taps : part * 8 + 8, lane]


def back_kernel(channels_all, token_scale, taps, n_stats, *refs):
    stats_refs = refs[:n_stats]
    (skip_ref, xf_ref, kvf_ref, pt_ref, pta_ref, qt_ref, qta_ref, ct_ref,
     inner_ref, w_ref, out_ref, pgr_ref, coef, *slots) = refs[n_stats:]
    chunks = xf_ref.shape[0]
    block = ct_ref.shape[2]
    members = chunks * LANES // ct_ref.shape[0]
    groups = LANES // members
    blocks = ct_ref.shape[1] // members
    slots = (slots[: len(slots) // 2], slots[len(slots) // 2 :])
    total = merged([ref[...] for ref in stats_refs])
    square = total[:blocks]
    cross = total[blocks : 2 * blocks] / channels_all
    rms = jnp.sqrt(square / channels_all + 1e-05)
    inv = token_scale / rms
    fall = token_scale * cross / (rms * rms * rms)
    for number in range(blocks):
        place = slice(number * members, (number + 1) * members)
        coef[0, place, :] = jnp.broadcast_to(inv[number : number + 1], (members, block))
        coef[1, place, :] = jnp.broadcast_to(fall[number : number + 1], (members, block))

    def at(chunk):
        lane = pl.ds(pl.multiple_of(chunk * LANES, LANES), LANES)
        group_at = pl.ds(pl.multiple_of(chunk * groups, groups), groups)
        return lane, group_at

    def first(chunk, slot):
        lane, group_at = at(chunk)
        return group_steps(
            skip_ref.at[:, lane], pt_ref.at[group_at], pta_ref.at[group_at], qt_ref.at[group_at],
            qta_ref.at[group_at], ct_ref.at[group_at], inner_ref.at[group_at], w_ref.at[group_at],
            coef, pgr_ref.at[chunk], *slots[slot][:4],
        )

    def second(chunk, slot):
        lane, _ = at(chunk)
        return tap_steps(
            taps, groups, xf_ref.at[chunk], kvf_ref.at[chunk], out_ref.at[:, lane], *slots[slot],
        )

    braid(first(0, 0), [])
    pairs = (chunks - 1) // 2

    @pl.loop(0, pairs)
    def _(pair):
        braid(first(2 * pair + 1, 1), second(2 * pair, 0))
        braid(first(2 * pair + 2, 0), second(2 * pair + 1, 1))

    if chunks % 2 == 0:
        braid(first(chunks - 1, 1), second(chunks - 2, 0))
        braid([], second(chunks - 1, 1))
    else:
        braid([], second(chunks - 1, 0))


def braid(one, two):
    done = 0
    for number, step in enumerate(one):
        step()
        upto = (number + 1) * len(two) // len(one)
        for other in two[done:upto]:
            other()
        done = upto
    for other in two[done:]:
        other()


def group_steps(
    skip_ref, pt_ref, pta_ref, qt_ref, qta_ref, ct_ref, inner_ref, w_ref, coef, pgr_ref, skip_acc, filt_acc, pg, qg
):
    groups, width, block = ct_ref.shape
    members = LANES // groups
    blocks = width // members
    row, col = lag_masks(block)
    near_side = col <= row
    skip = skip_columns(skip_ref, block)

    def step(group):
        members_at = slice(group * members, (group + 1) * members)
        every = jnp.concatenate([pta_ref[group], pt_ref[group]], axis=0)
        now = every[members:]
        q = jnp.concatenate([qta_ref[group], qt_ref[group]], axis=0).astype(F32)
        inner = inner_ref[group]
        output = q * inner
        out_grad = coef[0] * ct_ref[group].astype(F32) - coef[1] * output
        conv_grad = out_grad * q
        cot = conv_grad.astype(BF16)
        query_grad = out_grad * inner
        weighted = conv_grad * now.astype(F32)
        part_sum = weighted[:members]
        for number in range(1, blocks):
            part_sum = part_sum + weighted[number * members : (number + 1) * members]
        skip_acc[members_at, :] = part_sum
        gap = jnp.zeros((members, block), BF16)
        here = jnp.concatenate([gap, cot], axis=0)
        later = jnp.concatenate([cot, gap], axis=0)
        grad = matmul(here, w_ref[group, :block, :], ((1,), (1,))) + matmul(
            later, w_ref[group, block:, :], ((1,), (1,))
        )
        own = skip[members_at]
        pgr_ref[members_at, :] = grad[:members]
        for number in range(blocks):
            span = slice(number * members, (number + 1) * members)
            pg[number, members_at, :] = (
                grad[(number + 1) * members : (number + 2) * members] + own * conv_grad[span]
            )
            qg[number, members_at, :] = query_grad[span]
        both = matmul(cot, jnp.concatenate([now, every[:width]], axis=1), ((0,), (0,)))
        lagged = jnp.where(near_side, both[:, :block], both[:, block:])
        skewed = lagged[:8]
        for start in range(8, block, 8):
            skewed = skewed + pltpu.roll(lagged[start : start + 8], block - start, 1)
        filt_acc[group * 8 : group * 8 + 8, :] = skewed

    return [functools.partial(step, group) for group in range(groups)]


def tap_steps(taps, groups, xf_ref, kvf_ref, out_ref, skip_acc, filt_acc, pg, qg, gn):
    parts, lanes = xf_ref.shape[0], xf_ref.shape[2]
    block = pg.shape[2]
    blocks = qg.shape[0]
    piece = 32
    sums = {}

    def step(number, part):
        if part != 2:
            gn[...] = pg[number].T if part else qg[number].T
        for at in range(0, block, piece):
            begin = number * block + at
            grads = gn[at : at + piece, :]
            if part:
                grads = grads * kvf_ref[2 - part, begin : begin + piece, :]
            for tap in range(taps):
                start = HALO + begin - tap
                term = grads * xf_ref[part, start : start + piece, :]
                term = term.reshape(piece // 8, 8, lanes).sum(axis=0)
                sums[part, tap] = term if (part, tap) not in sums else sums[part, tap] + term
        if number == blocks - 1:
            for tap in range(taps):
                at = part * 8 + tap
                out_ref[at : at + 1, :] = jnp.sum(sums[part, tap], axis=0, keepdims=True)

    def last():
        row, col = lag_masks(block)
        flip = jnp.where(((row + col) % block) == 0, 1.0, 0.0).astype(F32)
        lags = filt_acc[pl.ds(0, groups, stride=8), :]
        for at in range(1, 8):
            lags = lags + pltpu.roll(filt_acc[pl.ds(at, groups, stride=8), :], block - at, 1)
        out_ref[3 * 8 :, :] = lax.dot_general(
            lags, flip, (((1,), (0,)), ((), ())),
            preferred_element_type=F32, precision=lax.Precision.HIGHEST,
        )
        skip_row = jnp.sum(skip_acc[...].T, axis=0, keepdims=True)
        for part in range(parts):
            out_ref[part * 8 + taps : part * 8 + 8, :] = skip_row

    steps = [functools.partial(step, number, 0) for number in range(blocks)]
    steps += [functools.partial(step, number, part) for number in range(blocks) for part in (1, 2)]
    return [last] + steps


def finish_kernel(n_in, *refs):
    ins = refs[:n_in]
    feat_ref, filt_ref, skip_ref = refs[n_in:]
    total = merged([ref[...].astype(F32) for ref in ins])
    taps = feat_ref.shape[1]
    for part in range(feat_ref.shape[0]):
        feat_ref[part] = total[part * 8 : part * 8 + taps]
    skip_ref[...] = total[taps : taps + 1]
    groups = total.shape[0] - 24
    for chunk in range(total.shape[1] // LANES):
        filt_ref[chunk * groups : (chunk + 1) * groups, :] = total[24:, chunk * LANES : (chunk + 1) * LANES]


def shifted(array, axis, by):
    length = lax.axis_size(axis)
    pairs = [(i, i + by) for i in range(length) if 0 <= i + by < length]
    return lax.ppermute(array, axis, pairs)


def crossed(array, axis, bit):
    length = lax.axis_size(axis)
    return lax.ppermute(array, axis, [(i, i ^ bit) for i in range(length)])


def quartet(array, axis, bit):
    return [array] + [crossed(array, axis, bit * k) for k in (1, 2, 3)]


def merged(parts):
    if len(parts) == 1:
        return parts[0]
    return (parts[0] + parts[1]) + (parts[2] + parts[3])


def on_chip(kernel, out_shape, scratch, args, outside=(), final=False):
    place = pl.BlockSpec(memory_space=pltpu.VMEM)
    apart = pl.BlockSpec(memory_space=pl.ANY)
    if not final:
        out_shape = [pltpu.VMEM(out.shape, out.dtype) for out in out_shape]
    args = [
        pltpu.with_memory_space_constraint(arg, pltpu.HBM if number in outside else pltpu.VMEM)
        for number, arg in enumerate(args)
    ]
    return pl.pallas_call(
        kernel,
        in_specs=[apart if number in outside else place for number in range(len(args))],
        out_specs=[place] * len(out_shape),
        out_shape=out_shape,
        scratch_shapes=scratch,
        compiler_params=pltpu.CompilerParams(vmem_limit_bytes=16 * 1024 * 1024),
    )(*args)


def body(projected, featurizer, long_filter, skip_gain, out_cotangent):
    parts, rows, channels = projected.shape
    groups, block = long_filter.shape
    taps = featurizer.shape[0]
    members = channels // groups
    chunk_groups = LANES // members
    blocks = rows // block
    width = blocks * members
    tail = block + HALO
    taps_major = jnp.transpose(featurizer, (1, 0, 2))
    skip_row = skip_gain.reshape(1, channels)

    sds = jax.ShapeDtypeStruct
    chunks = channels // LANES

    near, taps_major = on_chip(
        edge_kernel,
        [sds((block + parts * HALO, channels), BF16), sds((parts, taps, channels), BF16)],
        [
            pltpu.VMEM((2, tail, channels), BF16),
            pltpu.VMEM((parts, tail, LANES), F32),
            pltpu.SemaphoreType.DMA((4,)),
        ],
        (projected, taps_major),
        outside=(0, 1),
    )
    near = shifted(near, "seq", 1)

    far, x_all, kv, q0, pt, qt, ct, w = on_chip(
        front_kernel,
        [
            sds((2 * tail, channels), BF16),
            sds((chunks, parts, rows, LANES), BF16),
            sds((chunks, 2, rows, LANES), BF16),
            sds((block, channels), BF16),
            sds((groups, width - members, block), BF16),
            sds((groups, width - members, block), BF16),
            sds((groups, width, block), BF16),
            sds((groups, 2 * block, block), BF16),
        ],
        [
            pltpu.VMEM((parts, HALO + rows, LANES), F32),
            pltpu.VMEM((block, block), BF16),
            pltpu.VMEM((chunks, rows, LANES), BF16),
            pltpu.SemaphoreType.DMA((chunks,)),
            pltpu.SemaphoreType.DMA((chunks,)),
        ],
        (projected, taps_major, long_filter, out_cotangent),
        outside=(0, 3),
    )
    far = shifted(far, "seq", 1)
    kve, pta, qta, inner, stats = on_chip(
        middle_kernel,
        [
            sds((chunks, 2, EDGE, LANES), BF16),
            sds((groups, 2 * members, block), BF16),
            sds((groups, members, block), BF16),
            sds((groups, width, block), F32),
            sds((2 * blocks, block), F32),
        ],
        [
            pltpu.VMEM((parts, HALO + EDGE, LANES), F32),
            pltpu.VMEM((2, 8 * blocks, block), F32),
        ],
        (near, x_all, taps_major, skip_row, kv, q0, pt, qt, ct, w),
    )

    dp_size = lax.axis_size("dp")
    stat_parts = [stats]
    bit = 1
    while bit < dp_size:
        current = merged(stat_parts)
        if bit * 4 <= dp_size:
            stat_parts = quartet(current, "dp", bit)
            bit *= 4
        else:
            stat_parts = [current + crossed(current, "dp", bit)]
            bit *= 2
    xf, kvf = on_chip(
        prep_kernel,
        [sds((chunks, parts, HALO + rows, LANES), F32), sds((chunks, 2, rows, LANES), F32)],
        [],
        (near, x_all, kv, kve),
    )
    token_scale = 1.0 / math.sqrt(rows * lax.axis_size("seq"))
    out, pgr = on_chip(
        functools.partial(back_kernel, channels * dp_size, token_scale, taps, len(stat_parts)),
        [sds((24 + chunk_groups, channels), F32), sds((chunks, LANES, block), F32)],
        [pltpu.VMEM((2, width, block), F32)]
        + [
            pltpu.VMEM((LANES, block), F32),
            pltpu.VMEM((chunk_groups * 8, block), F32),
            pltpu.VMEM((blocks, LANES, block), F32),
            pltpu.VMEM((blocks, LANES, block), F32),
            pltpu.VMEM((block, LANES), F32),
        ]
        * 2,
        (*stat_parts, skip_row, xf, kvf, pt, pta, qt, qta, ct, inner, w),
    )
    (out,) = on_chip(
        rim_kernel,
        [sds((24 + chunk_groups, channels), F32)],
        [pltpu.VMEM((parts, tail, LANES), F32)],
        (far, taps_major, pgr, out),
    )

    seq_size = lax.axis_size("seq")
    out_parts = [out + crossed(out, "seq", 1)]
    bit = 2
    while bit < seq_size:
        current = merged([part.astype(F32) for part in out_parts]).astype(BF16)
        if bit * 4 <= seq_size:
            out_parts = quartet(current, "seq", bit)
            bit *= 4
        else:
            out_parts = [current.astype(F32) + crossed(current, "seq", bit).astype(F32)]
            bit *= 2

    feat, filt, skip = on_chip(
        functools.partial(finish_kernel, len(out_parts)),
        [
            sds((parts, taps, channels), F32),
            sds((groups, block), F32),
            sds((1, channels), F32),
        ],
        [],
        out_parts,
        final=True,
    )
    return (jnp.transpose(feat, (1, 0, 2)), filt, skip.reshape(channels))


def solution(mesh):
    return jax.shard_map(
        body,
        mesh=mesh,
        in_specs=(
            P(None, "seq", "dp"),
            P(None, None, "dp"),
            P("dp", None),
            P("dp"),
            P("seq", "dp"),
        ),
        out_specs=(P(None, None, "dp"), P("dp", None), P("dp")),
        check_vma=False,
    )
```

time: 47.7 us -> 57.1 us (1.20)
  starting transfers between devices: 13.6 us -> 23.3 us
  local copies, waits for them, and re-layouts: 3.79 us -> 0.01 us
  waiting for transfers between devices: 8.42 us -> 10.9 us
  Pallas kernels: 20.9 us -> 22 us
    ppermute x7, starting transfers between devices: 11.1 us -> 16.4 us  [crossed(): return lax.ppermute(array, axis, [(i, i ^ bit) for i in range(length)])]
    ppermute x1 -> x2, starting transfers between devices: 2.43 us -> 6.91 us  [shifted(): return lax.ppermute(array, axis, pairs)]
    unnamed x10 -> x4, local copies, waits for them, and re-layouts: 1.9 us -> 0.01 us
    squeeze x2 -> x0, local copies, waits for them, and re-layouts: 1.88 us -> none  [the longest x1 1.08 us: body(): projected[1, rows - tail:]]
    ppermute x7, waiting for transfers between devices: 8.42 us -> 9.73 us  [crossed(): return lax.ppermute(array, axis, [(i, i ^ bit) for i in range(length)])]
    ppermute x1 -> x2, waiting for transfers between devices: 0.01 us -> 1.17 us  [shifted(): return lax.ppermute(array, axis, pairs)]
    pallas_call x4 -> x7, Pallas kernels: 20.9 us -> 22 us  [on_chip(): pl.pallas_call(kernel, in_specs=[apart if number in outside else place fo...]
  transfers between devices with their start and end apart: 8 -> 9, of which waited for: 6 -> 6; matrix products, arithmetic and copies ran while one was open for 0% -> 0% of each run, Pallas kernels for 12% -> 21%
where the time goes in v3:
time: 57.1 us; the launch traced here: 57 us
  starting transfers between devices  23.3 us (41%)
  Pallas kernels  22 us (39%)
  waiting for transfers between devices  10.9 us (19%)
  between operations  0.76 us (1%)
    pallas_call x7, Pallas kernels, on_chip(): pl.pallas_call(kernel, in_specs=[apart if number in outside else place fo...  22 us
    ppermute x7, starting transfers between devices, crossed(): return lax.ppermute(array, axis, [(i, i ^ bit) for i in range(length)])  16.4 us
    ppermute x7, waiting for transfers between devices, crossed(): return lax.ppermute(array, axis, [(i, i ^ bit) for i in range(length)])  9.73 us
    ppermute x2, starting transfers between devices, shifted(): return lax.ppermute(array, axis, pairs)  6.91 us
    ppermute x2, waiting for transfers between devices, shifted(): return lax.ppermute(array, axis, pairs)  1.17 us
  transfers between devices with their start and end apart: 9, of which 6 were waited for; matrix products, arithmetic and copies ran while one was open for 0% of the time, Pallas kernels for 21%

profile of v3, /device:TPU:0, one launch (start us, length us, event | category | flops | bytes accessed | tf_op | source)
XLA Modules:
  0.0 57.0 jit_solution(16742004868154495485)
XLA Ops:
  0.6 0.0 copy-start
  0.6 0.0 copy-start.1
  0.7 1.9 %shard_map.76 = (bf16[152,1024]{1,0:T(8,128)(2,1)S(1)}, bf16[3,7,1024]{2,1,0:T(8,128)(2,1)S(1)}) custom-call(bf16[3,512,1024]{2,1,0:T(8,128)(2,1)} %x_ref.3, bf16[3,7,1024]{2,1,0:T(8,128)(2,1)} %bitcast.3), custom_call_target="tpu_custom_call" | custom-call | tf_op jit(solution)/shard_map/pallas_call | solution.py:477
  2.6 0.0 copy-done
  2.6 5.9 %shard_map.77 = (bf16[272,1024]{1,0:T(8,128)(2,1)S(1)}, bf16[8,3,512,128]{3,2,1,0:T(8,128)(2,1)S(1)}, bf16[8,2,512,128]{3,2,1,0:T(8,128)(2,1)S(1)}, bf16[128,102...) custom-call(bf16[3,512,1024]{2,1,0:T(8,128)(2,1)} %x_ref.3, ...), custom_call_target="tpu_custom_call" | custom-call | tf_op jit(solution)/shard_map/pallas_call | solution.py:477
  8.5 2.4 %collective-permute-start = (bf16[272,1024]{1,0:T(8,128)(2,1)S(1)}, bf16[272,1024]{1,0:T(8,128)(2,1)S(1)}, u32[]{:S(2)}, u32[]{:S(2)}) collective-permute-start(bf16[272,1024]{1,0:T(8,128)(2,1)S(1)} %get-tuple-element.26), channel_id=1, source_target_pairs={{0,4},{4,8},{8,12},{12,16},{16,20},{20,24},{24,28},{1,5},{5,9},{9,... | collective-permute-start | bytes 1671176 | tf_op jit(solution)/shard_map/ppermute | solution.py:450
  11.0 4.5 %collective-permute-start.1 = (bf16[152,1024]{1,0:T(8,128)(2,1)S(1)}, bf16[152,1024]{1,0:T(8,128)(2,1)S(1)}, u32[]{:S(2)}, u32[]{:S(2)}) collective-permute-start(bf16[152,1024]{1,0:T(8,128)(2,1)S(1)} %get-tuple-element.27), channel_id=1, source_target_pairs={{0,4},{4,8},{8,12},{12,16},{16,20},{20,24},{24,28},{1,5},{5,9},{9,... | collective-permute-start | bytes 933896 | tf_op jit(solution)/shard_map/ppermute | solution.py:450
  15.5 0.0 copy-done.1
  15.5 1.2 %collective-permute-done.1.near_ref = bf16[152,1024]{1,0:T(8,128)(2,1)S(1)} collective-permute-done((bf16[152,1024]{1,0:T(8,128)(2,1)S(1)}, bf16[152,1024]{1,0:T(8,128)(2,1)S(1)}, u32[]{:S(2)}, u32[]{:S(2)}) %collective-permute-start.1) | collective-permute-done | bytes 311328 | tf_op jit(solution)/shard_map/ppermute | solution.py:450
  16.7 2.5 %shard_map.78 = (bf16[8,2,16,128]{3,2,1,0:T(8,128)(2,1)S(1)}, bf16[64,32,128]{2,1,0:T(8,128)(2,1)S(1)}, bf16[64,16,128]{2,1,0:T(8,128)(2,1)S(1)}, f32[64,64,128]{2,1,0:T(8,128)S(1)}, f32[8,128]{1,0:T(8,128)S(1)}) custom-call(bf16[152,1024]{1,0:T(8,128)(2,1)S(1)} %collective-permute-done.1.near_ref, bf16[8,3,512,128]{3,2,1,0:T(8,128)(2,1)S(1)} %get-tuple-element.28.x_ref, ...), custom_call_target="tpu_custom_call" | custom-call | tf_op jit(solution)/shard_map/pallas_call | solution.py:477
  19.1 1.6 %collective-permute-start.2 = (f32[8,128]{1,0:T(8,128)S(1)}, f32[8,128]{1,0:T(8,128)S(1)}, u32[]{:S(2)}, u32[]{:S(2)}) collective-permute-start(f32[8,128]{1,0:T(8,128)S(1)} %get-tuple-element.35.refs_0_), channel_id=1, source_target_pairs={{0,1},{1,0},{2,3},{3,2},{4,5},{5,4},{6,7},{7,6},{8,9},{9,8},{10,11... | collective-permute-start | bytes 12296 | tf_op jit(solution)/shard_map/ppermute | solution.py:455
  20.8 2.6 %collective-permute-start.3 = (f32[8,128]{1,0:T(8,128)S(1)}, f32[8,128]{1,0:T(8,128)S(1)}, u32[]{:S(2)}, u32[]{:S(2)}) collective-permute-start(f32[8,128]{1,0:T(8,128)S(1)} %get-tuple-element.35.refs_0_), channel_id=1, source_target_pairs={{0,2},{1,3},{2,0},{3,1},{4,6},{5,7},{6,4},{7,5},{8,10},{9,11},{10,... | collective-permute-start | bytes 12296 | tf_op jit(solution)/shard_map/ppermute | solution.py:455
  23.4 0.2 collective-permute-start.4
  23.6 0.7 %shard_map.79 = (f32[8,3,520,128]{3,2,1,0:T(8,128)S(1)}, f32[8,2,512,128]{3,2,1,0:T(8,128)S(1)}) custom-call(bf16[152,1024]{1,0:T(8,128)(2,1)S(1)} %collective-permute-done.1.near_ref, bf16[8,3,512,128]{3,2,1,0:T(8,128)(2,1)S(1)} %get-tuple-element.28.x_ref, bf16[8,2,512,128]{3,2,1,0:T(8,128)(2,1)S(1)} %get-tuple-element.29.kv_ref, ...), custom_call_target="tpu_custom_call" | custom-call | tf_op jit(solution)/shard_map/pallas_call | solution.py:477
  24.3 0.0 collective-permute-done.2.refs_1_
  24.3 1.0 %collective-permute-done.3.refs_2_ = f32[8,128]{1,0:T(8,128)S(1)} collective-permute-done((f32[8,128]{1,0:T(8,128)S(1)}, f32[8,128]{1,0:T(8,128)S(1)}, u32[]{:S(2)}, u32[]{:S(2)}) %collective-permute-start.3) | collective-permute-done | bytes 4128 | tf_op jit(solution)/shard_map/ppermute | solution.py:455
  25.3 3.5 %collective-permute-done.4.refs_3_ = f32[8,128]{1,0:T(8,128)S(1)} collective-permute-done((f32[8,128]{1,0:T(8,128)S(1)}, f32[8,128]{1,0:T(8,128)S(1)}, u32[]{:S(2)}, u32[]{:S(2)}) %collective-permute-start.4) | collective-permute-done | bytes 4128 | tf_op jit(solution)/shard_map/ppermute | solution.py:455
  28.8 8.9 %shard_map.80 = (f32[32,1024]{1,0:T(8,128)S(1)}, f32[8,128,128]{2,1,0:T(8,128)S(1)}) custom-call(f32[8,128]{1,0:T(8,128)S(1)} %get-tuple-element.35.refs_0_, f32[8,128]{1,0:T(8,128)S(1)} %collective-permute-done.2.refs_1_, f32[8,128]{1,0:T(8,128)S(1)} %collective-permute-done.3.refs_2_, f32[8,128]{1,0:T(8,128)S(1)} %collective-permute-done.4.refs_3_, ...), custom_call_target="tpu_custom_call" | custom-call | tf_op jit(solution)/shard_map/pallas_call | solution.py:477
  37.7 0.0 collective-permute-done.far_ref
  37.7 1.4 %shard_map.81 = f32[32,1024]{1,0:T(8,128)S(1)} custom-call(bf16[272,1024]{1,0:T(8,128)(2,1)S(1)} %collective-permute-done.far_ref, bf16[3,7,1024]{2,1,0:T(8,128)(2,1)S(1)} %get-tuple-element.25.taps_ref, f32[8,128,128]{2,1,0:T(8,128)S(1)} %get-tuple-element.42.pgr_ref, f32[32,1024]{1,0:T(8,128)S(1)} %get-tuple-element.43.out_ref), custom_call_target="tpu_custom_call" | custom-call | tf_op jit(solution)/shard_map/pallas_call | solution.py:477
  39.1 5.0 %collective-permute-start.5 = (f32[32,1024]{1,0:T(8,128)S(1)}, f32[32,1024]{1,0:T(8,128)S(1)}, u32[]{:S(2)}, u32[]{:S(2)}) collective-permute-start(f32[32,1024]{1,0:T(8,128)S(1)} %shard_map.81), channel_id=1, source_target_pairs={{0,4},{4,0},{8,12},{12,8},{16,20},{20,16},{24,28},{28,24},{1,5},{5... | collective-permute-start | bytes 393224 | tf_op jit(solution)/shard_map/ppermute | solution.py:455
  44.1 1.0 %collective-permute-done.5 = f32[32,1024]{1,0:T(8,128)S(1)} collective-permute-done((f32[32,1024]{1,0:T(8,128)S(1)}, f32[32,1024]{1,0:T(8,128)S(1)}, u32[]{:S(2)}, u32[]{:S(2)}) %collective-permute-start.5) | collective-permute-done | bytes 131104 | tf_op jit(solution)/shard_map/ppermute | solution.py:455
  45.1 4.5 %collective-permute-start.6 = (bf16[32,1024]{1,0:T(8,128)(2,1)S(1)}, bf16[32,1024]{1,0:T(8,128)(2,1)S(1)}, u32[]{:S(2)}, u32[]{:S(2)}) collective-permute-start(bf16[32,1024]{1,0:T(8,128)(2,1)S(1)} %add_convert_fusion.refs_0_), channel_id=1, source_target_pairs={{0,8},{4,12},{8,0},{12,4},{16,24},{20,28},{24,16},{28,20},{1,9},{5... | collective-permute-start | bytes 196616 | tf_op jit(solution)/shard_map/ppermute | solution.py:455
  49.6 1.5 %collective-permute-start.7 = (bf16[32,1024]{1,0:T(8,128)(2,1)S(1)}, bf16[32,1024]{1,0:T(8,128)(2,1)S(1)}, u32[]{:S(2)}, u32[]{:S(2)}) collective-permute-start(bf16[32,1024]{1,0:T(8,128)(2,1)S(1)} %add_convert_fusion.refs_0_), channel_id=1, source_target_pairs={{0,16},{4,20},{8,24},{12,28},{16,0},{20,4},{24,8},{28,12},{1,17},{... | collective-permute-start | bytes 196616 | tf_op jit(solution)/shard_map/ppermute | solution.py:455
  51.1 0.9 %collective-permute-start.8 = (bf16[32,1024]{1,0:T(8,128)(2,1)S(1)}, bf16[32,1024]{1,0:T(8,128)(2,1)S(1)}, u32[]{:S(2)}, u32[]{:S(2)}) collective-permute-start(bf16[32,1024]{1,0:T(8,128)(2,1)S(1)} %add_convert_fusion.refs_0_), channel_id=1, source_target_pairs={{0,24},{4,28},{8,16},{12,20},{16,8},{20,12},{24,0},{28,4},{1,25},{... | collective-permute-start | bytes 196616 | tf_op jit(solution)/shard_map/ppermute | solution.py:455
  52.0 0.0 collective-permute-done.6.refs_1_
  52.0 1.9 %collective-permute-done.7.refs_2_ = bf16[32,1024]{1,0:T(8,128)(2,1)S(1)} collective-permute-done((bf16[32,1024]{1,0:T(8,128)(2,1)S(1)}, bf16[32,1024]{1,0:T(8,128)(2,1)S(1)}, u32[]{:S(2)}, u32[]{:S(2)}) %collective-permute-start.7) | collective-permute-done | bytes 65568 | tf_op jit(solution)/shard_map/ppermute | solution.py:455
  53.9 2.4 %collective-permute-done.8.refs_3_ = bf16[32,1024]{1,0:T(8,128)(2,1)S(1)} collective-permute-done((bf16[32,1024]{1,0:T(8,128)(2,1)S(1)}, bf16[32,1024]{1,0:T(8,128)(2,1)S(1)}, u32[]{:S(2)}, u32[]{:S(2)}) %collective-permute-start.8) | collective-permute-done | bytes 65568 | tf_op jit(solution)/shard_map/ppermute | solution.py:455
  56.3 0.7 %shard_map.82 = (f32[3,7,1024]{2,1,0:T(8,128)}, f32[64,128]{1,0:T(8,128)}, f32[1,1024]{1,0:T(1,128)}) custom-call(bf16[32,1024]{1,0:T(8,128)(2,1)S(1)} %add_convert_fusion.refs_0_, bf16[32,1024]{1,0:T(8,128)(2,1)S(1)} %collective-permute-done.6.refs_1_, bf16[32,1024]{1,0:T(8,128)(2,1)S(1)} %collective-permute-done.7.refs_2_, ...), custom_call_target="tpu_custom_call" | custom-call | tf_op jit(solution)/shard_map/pallas_call | solution.py:477
  (2 shorter events, 0.0 us)
Async XLA Ops:
  0.6 2.0 %copy-start = (bf16[64,128]{1,0:T(8,128)(2,1)S(1)}, bf16[64,128]{1,0:T(8,128)(2,1)}, u32[]{:S(2)}) copy-start(bf16[64,128]{1,0:T(8,128)(2,1)} %filt_ref.1) | copy-start | bytes 49156
  0.6 14.8 %copy-start.1 = (bf16[1024]{0:T(1024)(128)(2,1)S(1)}, bf16[1024]{0:T(1024)(128)(2,1)}, u32[]{:S(2)}) copy-start(bf16[1024]{0:T(1024)(128)(2,1)} %param.8) | copy-start | bytes 6148
  8.5 29.1 %collective-permute-start = (bf16[272,1024]{1,0:T(8,128)(2,1)S(1)}, bf16[272,1024]{1,0:T(8,128)(2,1)S(1)}, u32[]{:S(2)}, u32[]{:S(2)}) collective-permute-start(bf16[272,1024]{1,0:T(8,128)(2,1)S(1)} %get-tuple-element.26), channel_id=1, source_target_pairs={{0,4},{4,8},{8,12},{12,16},{16,20},{20,24},{24,28},{1,5},{5,9},{9,... | collective-permute-start | bytes 1671176 | tf_op jit(solution)/shard_map/ppermute | solution.py:450
  11.0 5.7 %collective-permute-start.1 = (bf16[152,1024]{1,0:T(8,128)(2,1)S(1)}, bf16[152,1024]{1,0:T(8,128)(2,1)S(1)}, u32[]{:S(2)}, u32[]{:S(2)}) collective-permute-start(bf16[152,1024]{1,0:T(8,128)(2,1)S(1)} %get-tuple-element.27), channel_id=1, source_target_pairs={{0,4},{4,8},{8,12},{12,16},{16,20},{20,24},{24,28},{1,5},{5,9},{9,... | collective-permute-start | bytes 933896 | tf_op jit(solution)/shard_map/ppermute | solution.py:450
  19.1 5.2 %collective-permute-start.2 = (f32[8,128]{1,0:T(8,128)S(1)}, f32[8,128]{1,0:T(8,128)S(1)}, u32[]{:S(2)}, u32[]{:S(2)}) collective-permute-start(f32[8,128]{1,0:T(8,128)S(1)} %get-tuple-element.35.refs_0_), channel_id=1, source_target_pairs={{0,1},{1,0},{2,3},{3,2},{4,5},{5,4},{6,7},{7,6},{8,9},{9,8},{10,11... | collective-permute-start | bytes 12296 | tf_op jit(solution)/shard_map/ppermute | solution.py:455
  20.8 4.5 %collective-permute-start.3 = (f32[8,128]{1,0:T(8,128)S(1)}, f32[8,128]{1,0:T(8,128)S(1)}, u32[]{:S(2)}, u32[]{:S(2)}) collective-permute-start(f32[8,128]{1,0:T(8,128)S(1)} %get-tuple-element.35.refs_0_), channel_id=1, source_target_pairs={{0,2},{1,3},{2,0},{3,1},{4,6},{5,7},{6,4},{7,5},{8,10},{9,11},{10,... | collective-permute-start | bytes 12296 | tf_op jit(solution)/shard_map/ppermute | solution.py:455
  23.4 5.4 %collective-permute-start.4 = (f32[8,128]{1,0:T(8,128)S(1)}, f32[8,128]{1,0:T(8,128)S(1)}, u32[]{:S(2)}, u32[]{:S(2)}) collective-permute-start(f32[8,128]{1,0:T(8,128)S(1)} %get-tuple-element.35.refs_0_), channel_id=1, source_target_pairs={{0,3},{1,2},{2,1},{3,0},{4,7},{5,6},{6,5},{7,4},{8,11},{9,10},{10,... | collective-permute-start | bytes 12296 | tf_op jit(solution)/shard_map/ppermute | solution.py:455
  39.1 6.0 %collective-permute-start.5 = (f32[32,1024]{1,0:T(8,128)S(1)}, f32[32,1024]{1,0:T(8,128)S(1)}, u32[]{:S(2)}, u32[]{:S(2)}) collective-permute-start(f32[32,1024]{1,0:T(8,128)S(1)} %shard_map.81), channel_id=1, source_target_pairs={{0,4},{4,0},{8,12},{12,8},{16,20},{20,16},{24,28},{28,24},{1,5},{5... | collective-permute-start | bytes 393224 | tf_op jit(solution)/shard_map/ppermute | solution.py:455
  45.1 6.9 %collective-permute-start.6 = (bf16[32,1024]{1,0:T(8,128)(2,1)S(1)}, bf16[32,1024]{1,0:T(8,128)(2,1)S(1)}, u32[]{:S(2)}, u32[]{:S(2)}) collective-permute-start(bf16[32,1024]{1,0:T(8,128)(2,1)S(1)} %add_convert_fusion.refs_0_), channel_id=1, source_target_pairs={{0,8},{4,12},{8,0},{12,4},{16,24},{20,28},{24,16},{28,20},{1,9},{5... | collective-permute-start | bytes 196616 | tf_op jit(solution)/shard_map/ppermute | solution.py:455
  49.6 4.3 %collective-permute-start.7 = (bf16[32,1024]{1,0:T(8,128)(2,1)S(1)}, bf16[32,1024]{1,0:T(8,128)(2,1)S(1)}, u32[]{:S(2)}, u32[]{:S(2)}) collective-permute-start(bf16[32,1024]{1,0:T(8,128)(2,1)S(1)} %add_convert_fusion.refs_0_), channel_id=1, source_target_pairs={{0,16},{4,20},{8,24},{12,28},{16,0},{20,4},{24,8},{28,12},{1,17},{... | collective-permute-start | bytes 196616 | tf_op jit(solution)/shard_map/ppermute | solution.py:455
  51.1 5.2 %collective-permute-start.8 = (bf16[32,1024]{1,0:T(8,128)(2,1)S(1)}, bf16[32,1024]{1,0:T(8,128)(2,1)S(1)}, u32[]{:S(2)}, u32[]{:S(2)}) collective-permute-start(bf16[32,1024]{1,0:T(8,128)(2,1)S(1)} %add_convert_fusion.refs_0_), channel_id=1, source_target_pairs={{0,24},{4,28},{8,16},{12,20},{16,8},{20,12},{24,0},{28,4},{1,25},{... | collective-permute-start | bytes 196616 | tf_op jit(solution)/shard_map/ppermute | solution.py:455

commit v4 on v3

--- a/solution.py
+++ b/solution.py
@@ -38,7 +38,7 @@
     return row, col
 
 
-def edge_kernel(x_ref, taps_hbm, near_ref, taps_ref, far_ref, buf, sems):
+def edge_kernel(x_ref, taps_hbm, near_ref, taps_ref, far_ref, bufs, sems):
     _, rows, channels = x_ref.shape
     tail = far_ref.shape[1]
     block = tail - HALO
@@ -59,8 +59,7 @@
     for copy in copies:
         copy.wait()
 
-    @pl.loop(0, channels // LANES)
-    def _(chunk):
+    def product(chunk, buf):
         lane = pl.ds(pl.multiple_of(chunk * LANES, LANES), LANES)
         for part in range(2):
             buf[1 + part] = far_ref[part, :, lane].astype(F32)
@@ -70,10 +69,17 @@
         v = featurize(buf, 2, HALO, block, taps_ref.at[:, :, lane])
         near_ref[:block, lane] = (k.astype(F32) * v.astype(F32)).astype(BF16)
 
+    at_once = math.gcd(channels // LANES, bufs.shape[0])
+
+    @pl.loop(0, channels // LANES // at_once)
+    def _(turn):
+        for number in range(at_once):
+            product(turn * at_once + number, bufs.at[number])
+
 
 def front_kernel(
-    x_ref, taps_ref, filt_ref, cot_ref,
-    far_ref, x_all, kv_ref, q0_ref, pt_ref, qt_ref, ct_ref, w_ref,
+    x_ref, taps_ref, filt_ref, skip_ref, cot_ref,
+    far_ref, skt_ref, x_all, kv_ref, q0_ref, pt_ref, qt_ref, ct_ref, w_ref,
     buf, mask, cot_all, x_sems, cot_sems,
 ):
     parts, rows, channels = x_ref.shape
@@ -99,6 +105,9 @@
 
     @pl.loop(0, channels // LANES)
     def _(chunk):
+        lane = pl.ds(pl.multiple_of(chunk * LANES, LANES), LANES)
+        group_at = pl.ds(pl.multiple_of(chunk * groups, groups), groups)
+        skt_ref[group_at] = skip_columns(skip_ref.at[:, lane], block).reshape(groups, members, block)
         rows_here = filt_ref[pl.ds(pl.multiple_of(chunk * groups, groups), groups), :].astype(F32)
         for number in range(groups):
             group = chunk * groups + number
@@ -154,7 +163,7 @@
 
 
 def middle_kernel(
-    near_ref, x_ref, taps_ref, skip_ref, kv_ref, q0_ref, pt_ref, qt_ref, ct_ref, w_ref,
+    near_ref, x_ref, taps_ref, skt_ref, kv_ref, q0_ref, pt_ref, qt_ref, ct_ref, w_ref,
     kve_ref, pta_ref, qta_ref, inner_ref, stats_ref,
     buf, acc,
 ):
@@ -162,20 +171,63 @@
     block = q0_ref.shape[0]
     members = channels // w_ref.shape[0]
     groups = LANES // members
-    blocks = ct_ref.shape[1] // members
+    width = ct_ref.shape[1]
+    blocks = width // members
+    chunks = channels // LANES
     acc[...] = jnp.zeros_like(acc)
 
-    @pl.loop(0, channels // LANES)
-    def _(chunk):
+    def heads(chunk):
         lane = pl.ds(pl.multiple_of(chunk * LANES, LANES), LANES)
         group_at = pl.ds(pl.multiple_of(chunk * groups, groups), groups)
-        middle_chunk(
-            near_ref.at[:, lane], x_ref.at[chunk, :, :EDGE], taps_ref.at[:, :, lane], skip_ref.at[:, lane],
-            kv_ref.at[chunk, :, :block], q0_ref.at[:, lane], pt_ref.at[group_at], qt_ref.at[group_at],
-            ct_ref.at[group_at], w_ref.at[group_at], kve_ref.at[chunk], pta_ref.at[group_at],
-            qta_ref.at[group_at], inner_ref.at[group_at], buf, acc,
+        for part in range(3):
+            at = block + part * HALO
+            buf[part, :HALO, :] = near_ref[at : at + HALO, lane].astype(F32)
+            buf[part, HALO:, :] = x_ref[chunk, part, :EDGE, :].astype(F32)
+        q_edge, k_edge, v_edge = (
+            featurize(buf, part, HALO, EDGE, taps_ref.at[:, :, lane]) for part in range(3)
         )
-
+        kve_ref[chunk, 0] = k_edge
+        kve_ref[chunk, 1] = v_edge
+        k0 = jnp.concatenate([k_edge, kv_ref[chunk, 0, EDGE:block, :]], axis=0)
+        v0 = jnp.concatenate([v_edge, kv_ref[chunk, 1, EDGE:block, :]], axis=0)
+        q0 = jnp.concatenate([q_edge, q0_ref[EDGE:, lane]], axis=0)
+        p0 = (k0.astype(F32) * v0.astype(F32)).astype(BF16)
+        pta_ref[group_at, :members, :] = near_ref[:block, lane].T.reshape(groups, members, block)
+        pta_ref[group_at, members:, :] = p0.T.reshape(groups, members, block)
+        qta_ref[group_at] = q0.T.reshape(groups, members, block)
+
+    def filters(chunk):
+        sums = [[None] * blocks, [None] * blocks]
+        for within in range(groups):
+            group = chunk * groups + within
+            every = jnp.concatenate([pta_ref[group], pt_ref[group]], axis=0)
+            now = every[members:]
+            filtered = matmul(
+                jnp.concatenate([now, every[:width]], axis=1), w_ref[group], ((1,), (0,))
+            )
+            own = jnp.concatenate([skt_ref[group]] * blocks, axis=0)
+            inner = filtered + own * now.astype(F32)
+            inner_ref[group] = inner
+            q = jnp.concatenate([qta_ref[group], qt_ref[group]], axis=0).astype(F32)
+            output = q * inner
+            for which, value in enumerate((output * output, ct_ref[group].astype(F32) * output)):
+                for number in range(blocks):
+                    span = value[number * members : (number + 1) * members]
+                    span = span.reshape(members // 8, 8, block).sum(axis=0)
+                    sums[which][number] = span if within == 0 else sums[which][number] + span
+        for which in range(2):
+            for number in range(blocks):
+                place = slice(number * 8, number * 8 + 8)
+                acc[which, place, :] += sums[which][number]
+
+    heads(0)
+
+    @pl.loop(1, chunks)
+    def _(chunk):
+        filters(chunk - 1)
+        heads(chunk)
+
+    filters(chunks - 1)
     for which in range(2):
         for number in range(blocks):
             at = which * blocks + number
@@ -184,71 +236,46 @@
             )
 
 
-def middle_chunk(
-    near_ref, x0_ref, taps_ref, skip_ref, kv_ref, q0_ref, pt_ref, qt_ref, ct_ref, w_ref,
-    kve_ref, pta_ref, qta_ref, inner_ref,
-    buf, acc,
-):
-    block = q0_ref.shape[0]
-    groups, width, lanes = w_ref.shape[0], ct_ref.shape[1], q0_ref.shape[1]
-    members = lanes // groups
-    blocks = width // members
-    for part in range(3):
-        at = block + part * HALO
-        buf[part, :HALO, :] = near_ref[at : at + HALO, :].astype(F32)
-        buf[part, HALO:, :] = x0_ref[part].astype(F32)
-    q_edge, k_edge, v_edge = (featurize(buf, part, HALO, EDGE, taps_ref) for part in range(3))
-    kve_ref[0] = k_edge
-    kve_ref[1] = v_edge
-    k0 = jnp.concatenate([k_edge, kv_ref[0, EDGE:, :]], axis=0)
-    v0 = jnp.concatenate([v_edge, kv_ref[1, EDGE:, :]], axis=0)
-    q0 = jnp.concatenate([q_edge, q0_ref[EDGE:, :]], axis=0)
-    p_rim = near_ref[:block, :]
-    p0 = (k0.astype(F32) * v0.astype(F32)).astype(BF16)
-    pta_ref[:, :members, :] = p_rim.T.reshape(groups, members, block)
-    pta_ref[:, members:, :] = p0.T.reshape(groups, members, block)
-    qta_ref[...] = q0.T.reshape(groups, members, block)
-    skip = skip_columns(skip_ref, block)
-    for group in range(groups):
-        every = jnp.concatenate([pta_ref[group], pt_ref[group]], axis=0)
-        now = every[members:]
-        filtered = matmul(
-            jnp.concatenate([now, every[:width]], axis=1), w_ref[group], ((1,), (0,))
-        )
-        own = skip[group * members : (group + 1) * members]
-        own = jnp.concatenate([own] * blocks, axis=0)
-        inner = filtered + own * now.astype(F32)
-        inner_ref[group] = inner
-        q = jnp.concatenate([qta_ref[group], qt_ref[group]], axis=0).astype(F32)
-        output = q * inner
-        square = output * output
-        cross = ct_ref[group].astype(F32) * output
-        for number in range(blocks):
-            for half in range(0, members, 8):
-                at = number * members + half
-                place = slice(number * 8, number * 8 + 8)
-                acc[0, place, :] += square[at : at + 8]
-                acc[1, place, :] += cross[at : at + 8]
-
-
 def prep_kernel(near_ref, x_ref, kv_ref, kve_ref, xf_ref, kvf_ref):
-    parts, _, _ = x_ref.shape[1:]
+    parts, rows, _ = x_ref.shape[1:]
     block = near_ref.shape[0] - parts * HALO
+    blocks = rows // block
 
     @pl.loop(0, x_ref.shape[0])
     def _(chunk):
         lane = pl.ds(pl.multiple_of(chunk * LANES, LANES), LANES)
         for part in range(parts):
             at = block + part * HALO
-            xf_ref[chunk, part, :HALO, :] = near_ref[at : at + HALO, lane].astype(F32)
-            xf_ref[chunk, part, HALO:, :] = x_ref[chunk, part].astype(F32)
+            xf_ref[chunk, 0, part, :HALO, :] = near_ref[at : at + HALO, lane].astype(F32)
+            for number in range(blocks):
+                at = number * block
+                if number:
+                    xf_ref[chunk, number, part, :HALO, :] = x_ref[chunk, part, at - HALO : at, :].astype(F32)
+                xf_ref[chunk, number, part, HALO:, :] = x_ref[chunk, part, at : at + block, :].astype(F32)
         for part in range(2):
-            kvf_ref[chunk, part, :EDGE, :] = kve_ref[chunk, part].astype(F32)
-            kvf_ref[chunk, part, EDGE:, :] = kv_ref[chunk, part, EDGE:, :].astype(F32)
+            kvf_ref[chunk, 0, part, :EDGE, :] = kve_ref[chunk, part].astype(F32)
+            kvf_ref[chunk, 0, part, EDGE:, :] = kv_ref[chunk, part, EDGE:block, :].astype(F32)
+            for number in range(1, blocks):
+                at = number * block
+                kvf_ref[chunk, number, part] = kv_ref[chunk, part, at : at + block, :].astype(F32)
+
+
+def braid(one, two):
+    done = 0
+    for number, step in enumerate(one):
+        step()
+        upto = (number + 1) * len(two) // len(one)
+        for other in two[done:upto]:
+            other()
+        done = upto
+    for other in two[done:]:
+        other()
 
 
 def rim_kernel(far_ref, taps_ref, pgr_ref, out_ref, sum_ref, buf):
-    chunks, block = pgr_ref.shape[:2]
+    members, block = pgr_ref.shape[1:]
+    groups = LANES // members
+    chunks = pgr_ref.shape[0] // groups
     taps = taps_ref.shape[1]
     tail = block + HALO
     sum_ref[:8, :] = out_ref[:8, :]
@@ -259,7 +286,8 @@
         lane = pl.ds(pl.multiple_of(chunk * LANES, LANES), LANES)
         for part in range(2):
             buf[1 + part] = far_ref[part * tail : (part + 1) * tail, lane].astype(F32)
-        back = pgr_ref[chunk].T
+        group_at = pl.ds(pl.multiple_of(chunk * groups, groups), groups)
+        back = pgr_ref[group_at].reshape(LANES, block).T
         for part in (1, 2):
             other = featurize(buf, 3 - part, HALO, block, taps_ref.at[:, :, lane]).astype(F32)
             grads = back * other
@@ -272,14 +300,13 @@
 
 def back_kernel(channels_all, token_scale, taps, n_stats, *refs):
     stats_refs = refs[:n_stats]
-    (skip_ref, xf_ref, kvf_ref, pt_ref, pta_ref, qt_ref, qta_ref, ct_ref,
-     inner_ref, w_ref, out_ref, pgr_ref, coef, *slots) = refs[n_stats:]
-    chunks = xf_ref.shape[0]
-    block = ct_ref.shape[2]
-    members = chunks * LANES // ct_ref.shape[0]
+    (skt_ref, xf_ref, kvf_ref, pt_ref, pta_ref, qt_ref, qta_ref, ct_ref, inner_ref, w_ref,
+     out_ref, pgr_ref, coef, skip_acc, filt_acc, sums, pg, qg, gn) = refs[n_stats:]
+    chunks, blocks = xf_ref.shape[:2]
+    parts = xf_ref.shape[2]
+    width, block = ct_ref.shape[1:]
+    members = width // blocks
     groups = LANES // members
-    blocks = ct_ref.shape[1] // members
-    slots = (slots[: len(slots) // 2], slots[len(slots) // 2 :])
     total = merged([ref[...] for ref in stats_refs])
     square = total[:blocks]
     cross = total[blocks : 2 * blocks] / channels_all
@@ -290,65 +317,11 @@
         place = slice(number * members, (number + 1) * members)
         coef[0, place, :] = jnp.broadcast_to(inv[number : number + 1], (members, block))
         coef[1, place, :] = jnp.broadcast_to(fall[number : number + 1], (members, block))
-
-    def at(chunk):
-        lane = pl.ds(pl.multiple_of(chunk * LANES, LANES), LANES)
-        group_at = pl.ds(pl.multiple_of(chunk * groups, groups), groups)
-        return lane, group_at
-
-    def first(chunk, slot):
-        lane, group_at = at(chunk)
-        return group_steps(
-            skip_ref.at[:, lane], pt_ref.at[group_at], pta_ref.at[group_at], qt_ref.at[group_at],
-            qta_ref.at[group_at], ct_ref.at[group_at], inner_ref.at[group_at], w_ref.at[group_at],
-            coef, pgr_ref.at[chunk], *slots[slot][:4],
-        )
-
-    def second(chunk, slot):
-        lane, _ = at(chunk)
-        return tap_steps(
-            taps, groups, xf_ref.at[chunk], kvf_ref.at[chunk], out_ref.at[:, lane], *slots[slot],
-        )
-
-    braid(first(0, 0), [])
-    pairs = (chunks - 1) // 2
-
-    @pl.loop(0, pairs)
-    def _(pair):
-        braid(first(2 * pair + 1, 1), second(2 * pair, 0))
-        braid(first(2 * pair + 2, 0), second(2 * pair + 1, 1))
-
-    if chunks % 2 == 0:
-        braid(first(chunks - 1, 1), second(chunks - 2, 0))
-        braid([], second(chunks - 1, 1))
-    else:
-        braid([], second(chunks - 1, 0))
-
-
-def braid(one, two):
-    done = 0
-    for number, step in enumerate(one):
-        step()
-        upto = (number + 1) * len(two) // len(one)
-        for other in two[done:upto]:
-            other()
-        done = upto
-    for other in two[done:]:
-        other()
-
-
-def group_steps(
-    skip_ref, pt_ref, pta_ref, qt_ref, qta_ref, ct_ref, inner_ref, w_ref, coef, pgr_ref, skip_acc, filt_acc, pg, qg
-):
-    groups, width, block = ct_ref.shape
-    members = LANES // groups
-    blocks = width // members
     row, col = lag_masks(block)
-    near_side = col <= row
-    skip = skip_columns(skip_ref, block)
-
-    def step(group):
-        members_at = slice(group * members, (group + 1) * members)
+
+    def group_part(chunk, within):
+        group = chunk * groups + within
+        slot = lax.rem(chunk, 2)
         every = jnp.concatenate([pta_ref[group], pt_ref[group]], axis=0)
         now = every[members:]
         q = jnp.concatenate([qta_ref[group], qt_ref[group]], axis=0).astype(F32)
@@ -362,73 +335,89 @@
         part_sum = weighted[:members]
         for number in range(1, blocks):
             part_sum = part_sum + weighted[number * members : (number + 1) * members]
-        skip_acc[members_at, :] = part_sum
+        skip_acc[group] = part_sum
         gap = jnp.zeros((members, block), BF16)
         here = jnp.concatenate([gap, cot], axis=0)
         later = jnp.concatenate([cot, gap], axis=0)
-        grad = matmul(here, w_ref[group, :block, :], ((1,), (1,))) + matmul(
-            later, w_ref[group, block:, :], ((1,), (1,))
+        grad = matmul(
+            jnp.concatenate([here, later], axis=1),
+            jnp.concatenate([w_ref[group, :block, :], w_ref[group, block:, :]], axis=1),
+            ((1,), (1,)),
         )
-        own = skip[members_at]
-        pgr_ref[members_at, :] = grad[:members]
+        own = skt_ref[group]
+        pgr_ref[group] = grad[:members]
         for number in range(blocks):
             span = slice(number * members, (number + 1) * members)
-            pg[number, members_at, :] = (
+            pg[slot, number, within] = (
                 grad[(number + 1) * members : (number + 2) * members] + own * conv_grad[span]
             )
-            qg[number, members_at, :] = query_grad[span]
+            qg[slot, number, within] = query_grad[span]
         both = matmul(cot, jnp.concatenate([now, every[:width]], axis=1), ((0,), (0,)))
-        lagged = jnp.where(near_side, both[:, :block], both[:, block:])
+        lagged = jnp.where(col <= row, both[:, :block], both[:, block:])
         skewed = lagged[:8]
         for start in range(8, block, 8):
             skewed = skewed + pltpu.roll(lagged[start : start + 8], block - start, 1)
-        filt_acc[group * 8 : group * 8 + 8, :] = skewed
-
-    return [functools.partial(step, group) for group in range(groups)]
-
-
-def tap_steps(taps, groups, xf_ref, kvf_ref, out_ref, skip_acc, filt_acc, pg, qg, gn):
-    parts, lanes = xf_ref.shape[0], xf_ref.shape[2]
-    block = pg.shape[2]
-    blocks = qg.shape[0]
-    piece = 32
-    sums = {}
-
-    def step(number, part):
-        if part != 2:
-            gn[...] = pg[number].T if part else qg[number].T
-        for at in range(0, block, piece):
-            begin = number * block + at
-            grads = gn[at : at + piece, :]
-            if part:
-                grads = grads * kvf_ref[2 - part, begin : begin + piece, :]
+        filt_acc[group] = skewed
+
+    def turn(chunk):
+        slot = lax.rem(chunk, 2)
+        for number in range(blocks):
+            gn[0, number] = qg[slot, number].reshape(LANES, block).T
+            gn[1, number] = pg[slot, number].reshape(LANES, block).T
+
+    def tap_steps(chunk):
+        piece = 32
+        totals = {}
+
+        def step(part, number):
+            for at in range(0, block, piece):
+                if part:
+                    grads = gn[1, number, at : at + piece, :]
+                    grads = grads * kvf_ref[chunk, number, 2 - part, at : at + piece, :]
+                else:
+                    grads = gn[0, number, at : at + piece, :]
+                for tap in range(taps):
+                    start = HALO + at - tap
+                    term = grads * xf_ref[chunk, number, part, start : start + piece, :]
+                    term = term.reshape(piece // 8, 8, LANES).sum(axis=0)
+                    totals[part, tap] = totals[part, tap] + term if (part, tap) in totals else term
+            if number == blocks - 1:
+                for tap in range(taps):
+                    sums[chunk, part * taps + tap] = totals[part, tap]
+
+        return [functools.partial(step, part, number) for part in range(parts) for number in range(blocks)]
+
+    def group_steps(chunk):
+        return [functools.partial(group_part, chunk, within) for within in range(groups)]
+
+    braid(group_steps(0), [])
+
+    @pl.loop(1, chunks)
+    def _(chunk):
+        turn(chunk - 1)
+        braid(group_steps(chunk), tap_steps(chunk - 1))
+
+    turn(chunks - 1)
+    braid([], tap_steps(chunks - 1))
+
+    flip = jnp.where(((row + col) % block) == 0, 1.0, 0.0).astype(F32)
+    lags = filt_acc[:, 0, :]
+    for at in range(1, 8):
+        lags = lags + pltpu.roll(filt_acc[:, at, :], block - at, 1)
+    lags = lax.dot_general(
+        lags, flip, (((1,), (0,)), ((), ())), preferred_element_type=F32, precision=lax.Precision.HIGHEST
+    )
+    for chunk in range(chunks):
+        lane = slice(chunk * LANES, (chunk + 1) * LANES)
+        group_at = slice(chunk * groups, (chunk + 1) * groups)
+        out_ref[3 * 8 :, lane] = lags[group_at]
+        skip_row = jnp.sum(skip_acc[group_at].reshape(LANES, block).T, axis=0, keepdims=True)
+        for part in range(parts):
             for tap in range(taps):
-                start = HALO + begin - tap
-                term = grads * xf_ref[part, start : start + piece, :]
-                term = term.reshape(piece // 8, 8, lanes).sum(axis=0)
-                sums[part, tap] = term if (part, tap) not in sums else sums[part, tap] + term
-        if number == blocks - 1:
-            for tap in range(taps):
-                at = part * 8 + tap
-                out_ref[at : at + 1, :] = jnp.sum(sums[part, tap], axis=0, keepdims=True)
-
-    def last():
-        row, col = lag_masks(block)
-        flip = jnp.where(((row + col) % block) == 0, 1.0, 0.0).astype(F32)
-        lags = filt_acc[pl.ds(0, groups, stride=8), :]
-        for at in range(1, 8):
-            lags = lags + pltpu.roll(filt_acc[pl.ds(at, groups, stride=8), :], block - at, 1)
-        out_ref[3 * 8 :, :] = lax.dot_general(
-            lags, flip, (((1,), (0,)), ((), ())),
-            preferred_element_type=F32, precision=lax.Precision.HIGHEST,
-        )
-        skip_row = jnp.sum(skip_acc[...].T, axis=0, keepdims=True)
-        for part in range(parts):
-            out_ref[part * 8 + taps : part * 8 + 8, :] = skip_row
-
-    steps = [functools.partial(step, number, 0) for number in range(blocks)]
-    steps += [functools.partial(step, number, part) for number in range(blocks) for part in (1, 2)]
-    return [last] + steps
+                out_ref[part * 8 + tap : part * 8 + tap + 1, lane] = jnp.sum(
+                    sums[chunk, part * taps + tap], axis=0, keepdims=True
+                )
+            out_ref[part * 8 + taps : part * 8 + 8, lane] = skip_row
 
 
 def finish_kernel(n_in, *refs):
@@ -504,7 +493,7 @@
         [sds((block + parts * HALO, channels), BF16), sds((parts, taps, channels), BF16)],
         [
             pltpu.VMEM((2, tail, channels), BF16),
-            pltpu.VMEM((parts, tail, LANES), F32),
+            pltpu.VMEM((2, parts, tail, LANES), F32),
             pltpu.SemaphoreType.DMA((4,)),
         ],
         (projected, taps_major),
@@ -512,10 +501,11 @@
     )
     near = shifted(near, "seq", 1)
 
-    far, x_all, kv, q0, pt, qt, ct, w = on_chip(
+    far, skt, x_all, kv, q0, pt, qt, ct, w = on_chip(
         front_kernel,
         [
             sds((2 * tail, channels), BF16),
+            sds((groups, members, block), F32),
             sds((chunks, parts, rows, LANES), BF16),
             sds((chunks, 2, rows, LANES), BF16),
             sds((block, channels), BF16),
@@ -531,8 +521,8 @@
             pltpu.SemaphoreType.DMA((chunks,)),
             pltpu.SemaphoreType.DMA((chunks,)),
         ],
-        (projected, taps_major, long_filter, out_cotangent),
-        outside=(0, 3),
+        (projected, taps_major, long_filter, skip_row, out_cotangent),
+        outside=(0, 4),
     )
     far = shifted(far, "seq", 1)
     kve, pta, qta, inner, stats = on_chip(
@@ -548,7 +538,7 @@
             pltpu.VMEM((parts, HALO + EDGE, LANES), F32),
             pltpu.VMEM((2, 8 * blocks, block), F32),
         ],
-        (near, x_all, taps_major, skip_row, kv, q0, pt, qt, ct, w),
+        (near, x_all, taps_major, skt, kv, q0, pt, qt, ct, w),
     )
 
     dp_size = lax.axis_size("dp")
@@ -564,24 +554,27 @@
             bit *= 2
     xf, kvf = on_chip(
         prep_kernel,
-        [sds((chunks, parts, HALO + rows, LANES), F32), sds((chunks, 2, rows, LANES), F32)],
+        [
+            sds((chunks, blocks, parts, HALO + block, LANES), F32),
+            sds((chunks, blocks, 2, block, LANES), F32),
+        ],
         [],
         (near, x_all, kv, kve),
     )
     token_scale = 1.0 / math.sqrt(rows * lax.axis_size("seq"))
     out, pgr = on_chip(
         functools.partial(back_kernel, channels * dp_size, token_scale, taps, len(stat_parts)),
-        [sds((24 + chunk_groups, channels), F32), sds((chunks, LANES, block), F32)],
-        [pltpu.VMEM((2, width, block), F32)]
-        + [
-            pltpu.VMEM((LANES, block), F32),
-            pltpu.VMEM((chunk_groups * 8, block), F32),
-            pltpu.VMEM((blocks, LANES, block), F32),
-            pltpu.VMEM((blocks, LANES, block), F32),
-            pltpu.VMEM((block, LANES), F32),
-        ]
-        * 2,
-        (*stat_parts, skip_row, xf, kvf, pt, pta, qt, qta, ct, inner, w),
+        [sds((24 + chunk_groups, channels), F32), sds((groups, members, block), F32)],
+        [
+            pltpu.VMEM((2, width, block), F32),
+            pltpu.VMEM((groups, members, block), F32),
+            pltpu.VMEM((groups, 8, block), F32),
+            pltpu.VMEM((chunks, parts * taps, 8, LANES), F32),
+            pltpu.VMEM((2, blocks, chunk_groups, members, block), F32),
+            pltpu.VMEM((2, blocks, chunk_groups, members, block), F32),
+            pltpu.VMEM((2, blocks, block, LANES), F32),
+        ],
+        (*stat_parts, skt, xf, kvf, pt, pta, qt, qta, ct, inner, w),
     )
     (out,) = on_chip(
         rim_kernel,

time: 57.1 us -> 56.7 us (level)
  Pallas kernels: 22 us -> 20.8 us
  local copies, waits for them, and re-layouts: 0.01 us -> 0.7 us
    pallas_call x7, Pallas kernels: 22 us -> 20.8 us  [on_chip(): pl.pallas_call(kernel, in_specs=[apart if number in outside else place fo...]
    reshape x1, local copies, waits for them, and re-layouts: 0.01 us -> 0.69 us  [body(): skip_row = skip_gain.reshape(1, channels)]
  transfers between devices with their start and end apart: 9 -> 9, of which waited for: 6 -> 6; matrix products, arithmetic and copies ran while one was open for 0% -> 0% of each run, Pallas kernels for 21% -> 19%
where the time goes in v4:
time: 56.7 us; the launch traced here: 56.5 us
  starting transfers between devices  23.3 us (41%)
  Pallas kernels  20.8 us (37%)
  waiting for transfers between devices  10.9 us (19%)
  between operations  0.73 us (1%)
  local copies, waits for them, and re-layouts  0.7 us (1%)
    pallas_call x7, Pallas kernels, on_chip(): pl.pallas_call(kernel, in_specs=[apart if number in outside else place fo...  20.8 us
    ppermute x7, starting transfers between devices, crossed(): return lax.ppermute(array, axis, [(i, i ^ bit) for i in range(length)])  16.4 us
    ppermute x7, waiting for transfers between devices, crossed(): return lax.ppermute(array, axis, [(i, i ^ bit) for i in range(length)])  9.73 us
    ppermute x2, starting transfers between devices, shifted(): return lax.ppermute(array, axis, pairs)  6.91 us
    ppermute x2, waiting for transfers between devices, shifted(): return lax.ppermute(array, axis, pairs)  1.2 us
  transfers between devices with their start and end apart: 9, of which 6 were waited for; matrix products, arithmetic and copies ran while one was open for 0% of the time, Pallas kernels for 19%

profile of v4, /device:TPU:0, one launch (start us, length us, event | category | flops | bytes accessed | tf_op | source)
XLA Modules:
  0.0 56.5 jit_solution(15546567965713039214)
XLA Ops:
  0.6 0.0 copy-start
  0.6 0.7 %reshape.12.skip_ref = bf16[1,1024]{1,0:T(2,128)(2,1)S(1)} reshape(bf16[1024]{0:T(1024)(128)(2,1)} %param.8) | data formatting | bytes 4096 | tf_op jit(solution)/shard_map/reshape | solution.py:486
  1.3 1.8 %shard_map.76 = (bf16[152,1024]{1,0:T(8,128)(2,1)S(1)}, bf16[3,7,1024]{2,1,0:T(8,128)(2,1)S(1)}) custom-call(bf16[3,512,1024]{2,1,0:T(8,128)(2,1)} %x_ref.3, bf16[3,7,1024]{2,1,0:T(8,128)(2,1)} %bitcast.3), custom_call_target="tpu_custom_call" | custom-call | tf_op jit(solution)/shard_map/pallas_call | solution.py:466
  3.2 0.0 copy-done
  3.2 6.1 %shard_map.77 = (bf16[272,1024]{1,0:T(8,128)(2,1)S(1)}, f32[64,16,128]{2,1,0:T(8,128)S(1)}, bf16[8,3,512,128]{3,2,1,0:T(8,128)(2,1)S(1)}, bf16[8,2,512,128]{3,2,...) custom-call(bf16[3,512,1024]{2,1,0:T(8,128)(2,1)} %x_ref.3, ...), custom_call_target="tpu_custom_call" | custom-call | tf_op jit(solution)/shard_map/pallas_call | solution.py:466
  9.3 2.4 %collective-permute-start = (bf16[272,1024]{1,0:T(8,128)(2,1)S(1)}, bf16[272,1024]{1,0:T(8,128)(2,1)S(1)}, u32[]{:S(2)}, u32[]{:S(2)}) collective-permute-start(bf16[272,1024]{1,0:T(8,128)(2,1)S(1)} %get-tuple-element.27), channel_id=1, source_target_pairs={{0,4},{4,8},{8,12},{12,16},{16,20},{20,24},{24,28},{1,5},{5,9},{9,... | collective-permute-start | bytes 1671176 | tf_op jit(solution)/shard_map/ppermute | solution.py:439
  11.7 4.5 %collective-permute-start.1 = (bf16[152,1024]{1,0:T(8,128)(2,1)S(1)}, bf16[152,1024]{1,0:T(8,128)(2,1)S(1)}, u32[]{:S(2)}, u32[]{:S(2)}) collective-permute-start(bf16[152,1024]{1,0:T(8,128)(2,1)S(1)} %get-tuple-element.28), channel_id=1, source_target_pairs={{0,4},{4,8},{8,12},{12,16},{16,20},{20,24},{24,28},{1,5},{5,9},{9,... | collective-permute-start | bytes 933896 | tf_op jit(solution)/shard_map/ppermute | solution.py:439
  16.2 1.2 %collective-permute-done.1.near_ref = bf16[152,1024]{1,0:T(8,128)(2,1)S(1)} collective-permute-done((bf16[152,1024]{1,0:T(8,128)(2,1)S(1)}, bf16[152,1024]{1,0:T(8,128)(2,1)S(1)}, u32[]{:S(2)}, u32[]{:S(2)}) %collective-permute-start.1) | collective-permute-done | bytes 311328 | tf_op jit(solution)/shard_map/ppermute | solution.py:439
  17.4 2.1 %shard_map.78 = (bf16[8,2,16,128]{3,2,1,0:T(8,128)(2,1)S(1)}, bf16[64,32,128]{2,1,0:T(8,128)(2,1)S(1)}, bf16[64,16,128]{2,1,0:T(8,128)(2,1)S(1)}, f32[64,64,128]{2,1,0:T(8,128)S(1)}, f32[8,128]{1,0:T(8,128)S(1)}) custom-call(bf16[152,1024]{1,0:T(8,128)(2,1)S(1)} %collective-permute-done.1.near_ref, bf16[8,3,512,128]{3,2,1,0:T(8,128)(2,1)S(1)} %get-tuple-element.29.x_ref, ...), custom_call_target="tpu_custom_call" | custom-call | tf_op jit(solution)/shard_map/pallas_call | solution.py:466
  19.5 1.6 %collective-permute-start.2 = (f32[8,128]{1,0:T(8,128)S(1)}, f32[8,128]{1,0:T(8,128)S(1)}, u32[]{:S(2)}, u32[]{:S(2)}) collective-permute-start(f32[8,128]{1,0:T(8,128)S(1)} %get-tuple-element.37.refs_0_), channel_id=1, source_target_pairs={{0,1},{1,0},{2,3},{3,2},{4,5},{5,4},{6,7},{7,6},{8,9},{9,8},{10,11... | collective-permute-start | bytes 12296 | tf_op jit(solution)/shard_map/ppermute | solution.py:444
  21.1 2.6 %collective-permute-start.3 = (f32[8,128]{1,0:T(8,128)S(1)}, f32[8,128]{1,0:T(8,128)S(1)}, u32[]{:S(2)}, u32[]{:S(2)}) collective-permute-start(f32[8,128]{1,0:T(8,128)S(1)} %get-tuple-element.37.refs_0_), channel_id=1, source_target_pairs={{0,2},{1,3},{2,0},{3,1},{4,6},{5,7},{6,4},{7,5},{8,10},{9,11},{10,... | collective-permute-start | bytes 12296 | tf_op jit(solution)/shard_map/ppermute | solution.py:444
  23.7 0.2 collective-permute-start.4
  23.9 0.7 %shard_map.79 = (f32[8,4,3,136,128]{4,3,2,1,0:T(8,128)S(1)}, f32[8,4,2,128,128]{4,3,2,1,0:T(8,128)S(1)}) custom-call(bf16[152,1024]{1,0:T(8,128)(2,1)S(1)} %collective-permute-done.1.near_ref, bf16[8,3,512,128]{3,2,1,0:T(8,128)(2,1)S(1)} %get-tuple-element.29.x_ref, bf16[8,2,512,128]{3,2,1,0:T(8,128)(2,1)S(1)} %get-tuple-element.31.kv_ref, ...), custom_call_target="tpu_custom_call" | custom-call | tf_op jit(solution)/shard_map/pallas_call | solution.py:466
  24.7 0.0 collective-permute-done.2.refs_1_
  24.7 1.0 %collective-permute-done.3.refs_2_ = f32[8,128]{1,0:T(8,128)S(1)} collective-permute-done((f32[8,128]{1,0:T(8,128)S(1)}, f32[8,128]{1,0:T(8,128)S(1)}, u32[]{:S(2)}, u32[]{:S(2)}) %collective-permute-start.3) | collective-permute-done | bytes 4128 | tf_op jit(solution)/shard_map/ppermute | solution.py:444
  25.6 3.5 %collective-permute-done.4.refs_3_ = f32[8,128]{1,0:T(8,128)S(1)} collective-permute-done((f32[8,128]{1,0:T(8,128)S(1)}, f32[8,128]{1,0:T(8,128)S(1)}, u32[]{:S(2)}, u32[]{:S(2)}) %collective-permute-start.4) | collective-permute-done | bytes 4128 | tf_op jit(solution)/shard_map/ppermute | solution.py:444
  29.1 8.0 %shard_map.80 = (f32[32,1024]{1,0:T(8,128)S(1)}, f32[64,16,128]{2,1,0:T(8,128)S(1)}) custom-call(f32[8,128]{1,0:T(8,128)S(1)} %get-tuple-element.37.refs_0_, f32[8,128]{1,0:T(8,128)S(1)} %collective-permute-done.2.refs_1_, f32[8,128]{1,0:T(8,128)S(1)} %collective-permute-done.3.refs_2_, f32[8,128]{1,0:T(8,128)S(1)} %collective-permute-done.4.refs_3_, ...), custom_call_target="tpu_custom_call" | custom-call | tf_op jit(solution)/shard_map/pallas_call | solution.py:466
  37.2 0.0 collective-permute-done.far_ref
  37.2 1.4 %shard_map.81 = f32[32,1024]{1,0:T(8,128)S(1)} custom-call(bf16[272,1024]{1,0:T(8,128)(2,1)S(1)} %collective-permute-done.far_ref, bf16[3,7,1024]{2,1,0:T(8,128)(2,1)S(1)} %get-tuple-element.26.taps_ref, f32[64,16,128]{2,1,0:T(8,128)S(1)} %get-tuple-element.44.pgr_ref, f32[32,1024]{1,0:T(8,128)S(1)} %get-tuple-element.45.out_ref), custom_call_target="tpu_custom_call" | custom-call | tf_op jit(solution)/shard_map/pallas_call | solution.py:466
  38.6 5.0 %collective-permute-start.5 = (f32[32,1024]{1,0:T(8,128)S(1)}, f32[32,1024]{1,0:T(8,128)S(1)}, u32[]{:S(2)}, u32[]{:S(2)}) collective-permute-start(f32[32,1024]{1,0:T(8,128)S(1)} %shard_map.81), channel_id=1, source_target_pairs={{0,4},{4,0},{8,12},{12,8},{16,20},{20,16},{24,28},{28,24},{1,5},{5... | collective-permute-start | bytes 393224 | tf_op jit(solution)/shard_map/ppermute | solution.py:444
  43.6 1.0 %collective-permute-done.5 = f32[32,1024]{1,0:T(8,128)S(1)} collective-permute-done((f32[32,1024]{1,0:T(8,128)S(1)}, f32[32,1024]{1,0:T(8,128)S(1)}, u32[]{:S(2)}, u32[]{:S(2)}) %collective-permute-start.5) | collective-permute-done | bytes 131104 | tf_op jit(solution)/shard_map/ppermute | solution.py:444
  44.6 4.5 %collective-permute-start.6 = (bf16[32,1024]{1,0:T(8,128)(2,1)S(1)}, bf16[32,1024]{1,0:T(8,128)(2,1)S(1)}, u32[]{:S(2)}, u32[]{:S(2)}) collective-permute-start(bf16[32,1024]{1,0:T(8,128)(2,1)S(1)} %add_convert_fusion.refs_0_), channel_id=1, source_target_pairs={{0,8},{4,12},{8,0},{12,4},{16,24},{20,28},{24,16},{28,20},{1,9},{5... | collective-permute-start | bytes 196616 | tf_op jit(solution)/shard_map/ppermute | solution.py:444
  49.1 1.5 %collective-permute-start.7 = (bf16[32,1024]{1,0:T(8,128)(2,1)S(1)}, bf16[32,1024]{1,0:T(8,128)(2,1)S(1)}, u32[]{:S(2)}, u32[]{:S(2)}) collective-permute-start(bf16[32,1024]{1,0:T(8,128)(2,1)S(1)} %add_convert_fusion.refs_0_), channel_id=1, source_target_pairs={{0,16},{4,20},{8,24},{12,28},{16,0},{20,4},{24,8},{28,12},{1,17},{... | collective-permute-start | bytes 196616 | tf_op jit(solution)/shard_map/ppermute | solution.py:444
  50.6 0.9 %collective-permute-start.8 = (bf16[32,1024]{1,0:T(8,128)(2,1)S(1)}, bf16[32,1024]{1,0:T(8,128)(2,1)S(1)}, u32[]{:S(2)}, u32[]{:S(2)}) collective-permute-start(bf16[32,1024]{1,0:T(8,128)(2,1)S(1)} %add_convert_fusion.refs_0_), channel_id=1, source_target_pairs={{0,24},{4,28},{8,16},{12,20},{16,8},{20,12},{24,0},{28,4},{1,25},{... | collective-permute-start | bytes 196616 | tf_op jit(solution)/shard_map/ppermute | solution.py:444
  51.5 0.0 collective-permute-done.6.refs_1_
  51.5 1.9 %collective-permute-done.7.refs_2_ = bf16[32,1024]{1,0:T(8,128)(2,1)S(1)} collective-permute-done((bf16[32,1024]{1,0:T(8,128)(2,1)S(1)}, bf16[32,1024]{1,0:T(8,128)(2,1)S(1)}, u32[]{:S(2)}, u32[]{:S(2)}) %collective-permute-start.7) | collective-permute-done | bytes 65568 | tf_op jit(solution)/shard_map/ppermute | solution.py:444
  53.4 2.4 %collective-permute-done.8.refs_3_ = bf16[32,1024]{1,0:T(8,128)(2,1)S(1)} collective-permute-done((bf16[32,1024]{1,0:T(8,128)(2,1)S(1)}, bf16[32,1024]{1,0:T(8,128)(2,1)S(1)}, u32[]{:S(2)}, u32[]{:S(2)}) %collective-permute-start.8) | collective-permute-done | bytes 65568 | tf_op jit(solution)/shard_map/ppermute | solution.py:444
  55.8 0.7 %shard_map.82 = (f32[3,7,1024]{2,1,0:T(8,128)}, f32[64,128]{1,0:T(8,128)}, f32[1,1024]{1,0:T(1,128)}) custom-call(bf16[32,1024]{1,0:T(8,128)(2,1)S(1)} %add_convert_fusion.refs_0_, bf16[32,1024]{1,0:T(8,128)(2,1)S(1)} %collective-permute-done.6.refs_1_, bf16[32,1024]{1,0:T(8,128)(2,1)S(1)} %collective-permute-done.7.refs_2_, ...), custom_call_target="tpu_custom_call" | custom-call | tf_op jit(solution)/shard_map/pallas_call | solution.py:466
  (1 shorter events, 0.0 us)
Async XLA Ops:
  0.6 2.6 %copy-start = (bf16[64,128]{1,0:T(8,128)(2,1)S(1)}, bf16[64,128]{1,0:T(8,128)(2,1)}, u32[]{:S(2)}) copy-start(bf16[64,128]{1,0:T(8,128)(2,1)} %filt_ref.1) | copy-start | bytes 49156
  9.3 27.9 %collective-permute-start = (bf16[272,1024]{1,0:T(8,128)(2,1)S(1)}, bf16[272,1024]{1,0:T(8,128)(2,1)S(1)}, u32[]{:S(2)}, u32[]{:S(2)}) collective-permute-start(bf16[272,1024]{1,0:T(8,128)(2,1)S(1)} %get-tuple-element.27), channel_id=1, source_target_pairs={{0,4},{4,8},{8,12},{12,16},{16,20},{20,24},{24,28},{1,5},{5,9},{9,... | collective-permute-start | bytes 1671176 | tf_op jit(solution)/shard_map/ppermute | solution.py:439
  11.7 5.7 %collective-permute-start.1 = (bf16[152,1024]{1,0:T(8,128)(2,1)S(1)}, bf16[152,1024]{1,0:T(8,128)(2,1)S(1)}, u32[]{:S(2)}, u32[]{:S(2)}) collective-permute-start(bf16[152,1024]{1,0:T(8,128)(2,1)S(1)} %get-tuple-element.28), channel_id=1, source_target_pairs={{0,4},{4,8},{8,12},{12,16},{16,20},{20,24},{24,28},{1,5},{5,9},{9,... | collective-permute-start | bytes 933896 | tf_op jit(solution)/shard_map/ppermute | solution.py:439
  19.5 5.2 %collective-permute-start.2 = (f32[8,128]{1,0:T(8,128)S(1)}, f32[8,128]{1,0:T(8,128)S(1)}, u32[]{:S(2)}, u32[]{:S(2)}) collective-permute-start(f32[8,128]{1,0:T(8,128)S(1)} %get-tuple-element.37.refs_0_), channel_id=1, source_target_pairs={{0,1},{1,0},{2,3},{3,2},{4,5},{5,4},{6,7},{7,6},{8,9},{9,8},{10,11... | collective-permute-start | bytes 12296 | tf_op jit(solution)/shard_map/ppermute | solution.py:444
  21.1 4.5 %collective-permute-start.3 = (f32[8,128]{1,0:T(8,128)S(1)}, f32[8,128]{1,0:T(8,128)S(1)}, u32[]{:S(2)}, u32[]{:S(2)}) collective-permute-start(f32[8,128]{1,0:T(8,128)S(1)} %get-tuple-element.37.refs_0_), channel_id=1, source_target_pairs={{0,2},{1,3},{2,0},{3,1},{4,6},{5,7},{6,4},{7,5},{8,10},{9,11},{10,... | collective-permute-start | bytes 12296 | tf_op jit(solution)/shard_map/ppermute | solution.py:444
  23.7 5.4 %collective-permute-start.4 = (f32[8,128]{1,0:T(8,128)S(1)}, f32[8,128]{1,0:T(8,128)S(1)}, u32[]{:S(2)}, u32[]{:S(2)}) collective-permute-start(f32[8,128]{1,0:T(8,128)S(1)} %get-tuple-element.37.refs_0_), channel_id=1, source_target_pairs={{0,3},{1,2},{2,1},{3,0},{4,7},{5,6},{6,5},{7,4},{8,11},{9,10},{10,... | collective-permute-start | bytes 12296 | tf_op jit(solution)/shard_map/ppermute | solution.py:444
  38.6 6.0 %collective-permute-start.5 = (f32[32,1024]{1,0:T(8,128)S(1)}, f32[32,1024]{1,0:T(8,128)S(1)}, u32[]{:S(2)}, u32[]{:S(2)}) collective-permute-start(f32[32,1024]{1,0:T(8,128)S(1)} %shard_map.81), channel_id=1, source_target_pairs={{0,4},{4,0},{8,12},{12,8},{16,20},{20,16},{24,28},{28,24},{1,5},{5... | collective-permute-start | bytes 393224 | tf_op jit(solution)/shard_map/ppermute | solution.py:444
  44.6 6.9 %collective-permute-start.6 = (bf16[32,1024]{1,0:T(8,128)(2,1)S(1)}, bf16[32,1024]{1,0:T(8,128)(2,1)S(1)}, u32[]{:S(2)}, u32[]{:S(2)}) collective-permute-start(bf16[32,1024]{1,0:T(8,128)(2,1)S(1)} %add_convert_fusion.refs_0_), channel_id=1, source_target_pairs={{0,8},{4,12},{8,0},{12,4},{16,24},{20,28},{24,16},{28,20},{1,9},{5... | collective-permute-start | bytes 196616 | tf_op jit(solution)/shard_map/ppermute | solution.py:444
  49.1 4.3 %collective-permute-start.7 = (bf16[32,1024]{1,0:T(8,128)(2,1)S(1)}, bf16[32,1024]{1,0:T(8,128)(2,1)S(1)}, u32[]{:S(2)}, u32[]{:S(2)}) collective-permute-start(bf16[32,1024]{1,0:T(8,128)(2,1)S(1)} %add_convert_fusion.refs_0_), channel_id=1, source_target_pairs={{0,16},{4,20},{8,24},{12,28},{16,0},{20,4},{24,8},{28,12},{1,17},{... | collective-permute-start | bytes 196616 | tf_op jit(solution)/shard_map/ppermute | solution.py:444
  50.6 5.2 %collective-permute-start.8 = (bf16[32,1024]{1,0:T(8,128)(2,1)S(1)}, bf16[32,1024]{1,0:T(8,128)(2,1)S(1)}, u32[]{:S(2)}, u32[]{:S(2)}) collective-permute-start(bf16[32,1024]{1,0:T(8,128)(2,1)S(1)} %add_convert_fusion.refs_0_), channel_id=1, source_target_pairs={{0,24},{4,28},{8,16},{12,20},{16,8},{20,12},{24,0},{28,4},{1,25},{... | collective-permute-start | bytes 196616 | tf_op jit(solution)/shard_map/ppermute | solution.py:444

commit v5 on v4

--- a/solution.py
+++ b/solution.py
@@ -38,7 +38,9 @@
     return row, col
 
 
-def edge_kernel(x_ref, taps_hbm, near_ref, taps_ref, far_ref, bufs, sems):
+def edge_kernel(
+    x_ref, taps_hbm, filt_hbm, cot_hbm, near_ref, taps_ref, filt_ref, cot_ref, far_ref, bufs, sems
+):
     _, rows, channels = x_ref.shape
     tail = far_ref.shape[1]
     block = tail - HALO
@@ -54,20 +56,27 @@
         )
     )
     copies.append(pltpu.make_async_copy(taps_hbm, taps_ref, sems.at[3]))
-    for copy in copies:
+    others = [
+        pltpu.make_async_copy(filt_hbm, filt_ref, sems.at[4]),
+        pltpu.make_async_copy(cot_hbm, cot_ref, sems.at[5]),
+    ]
+    for copy in copies + others:
         copy.start()
     for copy in copies:
         copy.wait()
+    inside = lax.axis_index("seq") < lax.axis_size("seq") - 1
+    near_ref[block : block + HALO, :] = jnp.where(inside, near_ref[block : block + HALO, :], 0)
 
     def product(chunk, buf):
         lane = pl.ds(pl.multiple_of(chunk * LANES, LANES), LANES)
         for part in range(2):
             buf[1 + part] = far_ref[part, :, lane].astype(F32)
             at = block + (1 + part) * HALO
-            near_ref[at : at + HALO, lane] = far_ref[part, tail - HALO :, lane]
+            near_ref[at : at + HALO, lane] = jnp.where(inside, far_ref[part, tail - HALO :, lane], 0)
         k = featurize(buf, 1, HALO, block, taps_ref.at[:, :, lane])
         v = featurize(buf, 2, HALO, block, taps_ref.at[:, :, lane])
-        near_ref[:block, lane] = (k.astype(F32) * v.astype(F32)).astype(BF16)
+        both = (k.astype(F32) * v.astype(F32)).astype(BF16)
+        near_ref[:block, lane] = jnp.where(inside, both, 0)
 
     at_once = math.gcd(channels // LANES, bufs.shape[0])
 
@@ -76,85 +85,67 @@
         for number in range(at_once):
             product(turn * at_once + number, bufs.at[number])
 
+    for copy in others:
+        copy.wait()
+
 
 def front_kernel(
     x_ref, taps_ref, filt_ref, skip_ref, cot_ref,
-    far_ref, skt_ref, x_all, kv_ref, q0_ref, pt_ref, qt_ref, ct_ref, w_ref,
-    buf, mask, cot_all, x_sems, cot_sems,
+    far_ref, skt_ref, kv_ref, q0_ref, pt_ref, qt_ref, ct_ref, w_ref,
+    buf, mask,
 ):
     parts, rows, channels = x_ref.shape
     block = filt_ref.shape[1]
     members = channels // filt_ref.shape[0]
     groups = LANES // members
-
-    def copies(chunk):
-        lane = pl.ds(pl.multiple_of(chunk * LANES, LANES), LANES)
-        return (
-            pltpu.make_async_copy(x_ref.at[:, :, lane], x_all.at[chunk], x_sems.at[chunk]),
-            pltpu.make_async_copy(cot_ref.at[:, lane], cot_all.at[chunk], cot_sems.at[chunk]),
-        )
-
-    @pl.loop(0, channels // LANES)
-    def _(chunk):
-        for copy in copies(chunk):
-            copy.start()
-
+    blocks = rows // block
+    tail = far_ref.shape[0] // 2
     buf[:, :HALO, :] = jnp.zeros((parts, HALO, LANES), F32)
     row, col = lag_masks(block)
     mask[...] = jnp.where(col >= row, 1.0, 0.0).astype(BF16)
+    inside = lax.axis_index("seq") < lax.axis_size("seq") - 1
+
+    def filters(chunk, within, filt):
+        group = chunk * groups + within
+        taps = jnp.broadcast_to(filt[within : within + 1], (block, block))
+        circ = pltpu.roll(taps, 0, 1, stride=1, stride_axis=0).astype(BF16)
+        near = circ * mask[...]
+        w_ref[group, :block, :] = near
+        w_ref[group, block:, :] = circ - near
+
+    def features(chunk, number):
+        lane = pl.ds(pl.multiple_of(chunk * LANES, LANES), LANES)
+        group_at = pl.ds(pl.multiple_of(chunk * groups, groups), groups)
+        span = slice(number * block, (number + 1) * block)
+        start = HALO + number * block
+        for part in range(parts):
+            buf[part, start : start + block, :] = x_ref[part, span, lane].astype(F32)
+        q, k, v = (featurize(buf, part, start, block, taps_ref.at[:, :, lane]) for part in range(3))
+        kv_ref[chunk, 0, span, :] = k
+        kv_ref[chunk, 1, span, :] = v
+        if number == 0:
+            q0_ref[:, lane] = q
+        else:
+            place = slice((number - 1) * members, number * members)
+            product = (k.astype(F32) * v.astype(F32)).astype(BF16)
+            pt_ref[group_at, place, :] = product.T.reshape(groups, members, block)
+            qt_ref[group_at, place, :] = q.T.reshape(groups, members, block)
+        place = slice(number * members, (number + 1) * members)
+        ct_ref[group_at, place, :] = cot_ref[span, lane].T.reshape(groups, members, block)
 
     @pl.loop(0, channels // LANES)
     def _(chunk):
         lane = pl.ds(pl.multiple_of(chunk * LANES, LANES), LANES)
         group_at = pl.ds(pl.multiple_of(chunk * groups, groups), groups)
+        filt = filt_ref[group_at, :].astype(F32)
         skt_ref[group_at] = skip_columns(skip_ref.at[:, lane], block).reshape(groups, members, block)
-        rows_here = filt_ref[pl.ds(pl.multiple_of(chunk * groups, groups), groups), :].astype(F32)
-        for number in range(groups):
-            group = chunk * groups + number
-            taps = jnp.broadcast_to(rows_here[number : number + 1], (block, block))
-            circ = pltpu.roll(taps, 0, 1, stride=1, stride_axis=0).astype(BF16)
-            near = circ * mask[...]
-            w_ref[group, :block, :] = near
-            w_ref[group, block:, :] = circ - near
-
-    @pl.loop(0, channels // LANES)
-    def _(chunk):
-        lane = pl.ds(pl.multiple_of(chunk * LANES, LANES), LANES)
-        group_at = pl.ds(pl.multiple_of(chunk * groups, groups), groups)
-        for copy in copies(chunk):
-            copy.wait()
-        front_chunk(
-            x_all.at[chunk], taps_ref.at[:, :, lane], cot_all.at[chunk],
-            kv_ref.at[chunk], q0_ref.at[:, lane], pt_ref.at[group_at], qt_ref.at[group_at],
-            ct_ref.at[group_at], buf,
+        braid(
+            [functools.partial(features, chunk, number) for number in range(blocks)],
+            [functools.partial(filters, chunk, within, filt) for within in range(groups)],
         )
-        tail = far_ref.shape[0] // 2
         for part in range(2):
-            far_ref[part * tail : (part + 1) * tail, lane] = x_all[chunk, 1 + part, rows - tail :, :]
-
-
-def front_chunk(x_ref, taps_ref, cot_ref, kv_ref, q0_ref, pt_ref, qt_ref, ct_ref, buf):
-    parts, rows, lanes = x_ref.shape
-    groups, _, block = ct_ref.shape
-    members = lanes // groups
-    blocks = rows // block
-    for part in range(parts):
-        buf[part, HALO:, :] = x_ref[part].astype(F32)
-    for number in range(blocks):
-        span = slice(number * block, (number + 1) * block)
-        start = HALO + number * block
-        q, k, v = (featurize(buf, part, start, block, taps_ref) for part in range(3))
-        kv_ref[0, span, :] = k
-        kv_ref[1, span, :] = v
-        if number == 0:
-            q0_ref[...] = q
-        else:
-            place = slice((number - 1) * members, number * members)
-            product = (k.astype(F32) * v.astype(F32)).astype(BF16)
-            pt_ref[:, place, :] = product.T.reshape(groups, members, block)
-            qt_ref[:, place, :] = q.T.reshape(groups, members, block)
-        place = slice(number * members, (number + 1) * members)
-        ct_ref[:, place, :] = cot_ref[span, :].T.reshape(groups, members, block)
+            ends = jnp.where(inside, x_ref[1 + part, rows - tail :, lane], 0)
+            far_ref[part * tail : (part + 1) * tail, lane] = ends
 
 
 def skip_columns(skip_ref, block):
@@ -182,7 +173,7 @@
         for part in range(3):
             at = block + part * HALO
             buf[part, :HALO, :] = near_ref[at : at + HALO, lane].astype(F32)
-            buf[part, HALO:, :] = x_ref[chunk, part, :EDGE, :].astype(F32)
+            buf[part, HALO:, :] = x_ref[part, :EDGE, lane].astype(F32)
         q_edge, k_edge, v_edge = (
             featurize(buf, part, HALO, EDGE, taps_ref.at[:, :, lane]) for part in range(3)
         )
@@ -237,11 +228,11 @@
 
 
 def prep_kernel(near_ref, x_ref, kv_ref, kve_ref, xf_ref, kvf_ref):
-    parts, rows, _ = x_ref.shape[1:]
+    parts, rows, channels = x_ref.shape
     block = near_ref.shape[0] - parts * HALO
     blocks = rows // block
 
-    @pl.loop(0, x_ref.shape[0])
+    @pl.loop(0, channels // LANES)
     def _(chunk):
         lane = pl.ds(pl.multiple_of(chunk * LANES, LANES), LANES)
         for part in range(parts):
@@ -250,8 +241,8 @@
             for number in range(blocks):
                 at = number * block
                 if number:
-                    xf_ref[chunk, number, part, :HALO, :] = x_ref[chunk, part, at - HALO : at, :].astype(F32)
-                xf_ref[chunk, number, part, HALO:, :] = x_ref[chunk, part, at : at + block, :].astype(F32)
+                    xf_ref[chunk, number, part, :HALO, :] = x_ref[part, at - HALO : at, lane].astype(F32)
+                xf_ref[chunk, number, part, HALO:, :] = x_ref[part, at : at + block, lane].astype(F32)
         for part in range(2):
             kvf_ref[chunk, 0, part, :EDGE, :] = kve_ref[chunk, part].astype(F32)
             kvf_ref[chunk, 0, part, EDGE:, :] = kv_ref[chunk, part, EDGE:block, :].astype(F32)
@@ -301,7 +292,7 @@
 def back_kernel(channels_all, token_scale, taps, n_stats, *refs):
     stats_refs = refs[:n_stats]
     (skt_ref, xf_ref, kvf_ref, pt_ref, pta_ref, qt_ref, qta_ref, ct_ref, inner_ref, w_ref,
-     out_ref, pgr_ref, coef, skip_acc, filt_acc, sums, pg, qg, gn) = refs[n_stats:]
+     out_ref, pgr_ref, coef, skip_acc, filt_acc, sums, *slots) = refs[n_stats:]
     chunks, blocks = xf_ref.shape[:2]
     parts = xf_ref.shape[2]
     width, block = ct_ref.shape[1:]
@@ -318,10 +309,11 @@
         coef[0, place, :] = jnp.broadcast_to(inv[number : number + 1], (members, block))
         coef[1, place, :] = jnp.broadcast_to(fall[number : number + 1], (members, block))
     row, col = lag_masks(block)
-
-    def group_part(chunk, within):
+    slots = (slots[:3], slots[3:])
+
+    def group_part(chunk, slot, within):
+        pg, qg, _ = slots[slot]
         group = chunk * groups + within
-        slot = lax.rem(chunk, 2)
         every = jnp.concatenate([pta_ref[group], pt_ref[group]], axis=0)
         now = every[members:]
         q = jnp.concatenate([qta_ref[group], qt_ref[group]], axis=0).astype(F32)
@@ -348,10 +340,10 @@
         pgr_ref[group] = grad[:members]
         for number in range(blocks):
             span = slice(number * members, (number + 1) * members)
-            pg[slot, number, within] = (
+            pg[number, within] = (
                 grad[(number + 1) * members : (number + 2) * members] + own * conv_grad[span]
             )
-            qg[slot, number, within] = query_grad[span]
+            qg[number, within] = query_grad[span]
         both = matmul(cot, jnp.concatenate([now, every[:width]], axis=1), ((0,), (0,)))
         lagged = jnp.where(col <= row, both[:, :block], both[:, block:])
         skewed = lagged[:8]
@@ -359,13 +351,14 @@
             skewed = skewed + pltpu.roll(lagged[start : start + 8], block - start, 1)
         filt_acc[group] = skewed
 
-    def turn(chunk):
-        slot = lax.rem(chunk, 2)
+    def turn(slot):
+        pg, qg, gn = slots[slot]
         for number in range(blocks):
-            gn[0, number] = qg[slot, number].reshape(LANES, block).T
-            gn[1, number] = pg[slot, number].reshape(LANES, block).T
-
-    def tap_steps(chunk):
+            gn[0, number] = qg[number].reshape(LANES, block).T
+            gn[1, number] = pg[number].reshape(LANES, block).T
+
+    def tap_steps(chunk, slot):
+        gn = slots[slot][2]
         piece = 32
         totals = {}
 
@@ -387,18 +380,30 @@
 
         return [functools.partial(step, part, number) for part in range(parts) for number in range(blocks)]
 
-    def group_steps(chunk):
-        return [functools.partial(group_part, chunk, within) for within in range(groups)]
-
-    braid(group_steps(0), [])
-
-    @pl.loop(1, chunks)
-    def _(chunk):
-        turn(chunk - 1)
-        braid(group_steps(chunk), tap_steps(chunk - 1))
-
-    turn(chunks - 1)
-    braid([], tap_steps(chunks - 1))
+    def group_steps(chunk, slot):
+        return [functools.partial(group_part, chunk, slot, within) for within in range(groups)]
+
+    def whole_step(chunk, slot):
+        turn(1 - slot)
+        braid(group_steps(chunk, slot), tap_steps(chunk - 2, slot))
+
+    braid(group_steps(0, 0), [])
+    if chunks > 1:
+        braid(group_steps(1, 1), [])
+        turn(0)
+
+        @pl.loop(1, chunks // 2)
+        def _(pair):
+            whole_step(2 * pair, 0)
+            whole_step(2 * pair + 1, 1)
+
+        if chunks % 2:
+            whole_step(chunks - 1, 0)
+        turn((chunks - 1) % 2)
+        braid([], tap_steps(chunks - 2, chunks % 2))
+    else:
+        turn(0)
+    braid([], tap_steps(chunks - 1, (chunks - 1) % 2))
 
     flip = jnp.where(((row + col) % block) == 0, 1.0, 0.0).astype(F32)
     lags = filt_acc[:, 0, :]
@@ -433,10 +438,9 @@
         filt_ref[chunk * groups : (chunk + 1) * groups, :] = total[24:, chunk * LANES : (chunk + 1) * LANES]
 
 
-def shifted(array, axis, by):
+def ring(array, axis):
     length = lax.axis_size(axis)
-    pairs = [(i, i + by) for i in range(length) if 0 <= i + by < length]
-    return lax.ppermute(array, axis, pairs)
+    return lax.ppermute(array, axis, [(i, (i + 1) % length) for i in range(length)])
 
 
 def crossed(array, axis, bit):
@@ -488,25 +492,29 @@
     sds = jax.ShapeDtypeStruct
     chunks = channels // LANES
 
-    near, taps_major = on_chip(
+    near, taps_major, filters, cots = on_chip(
         edge_kernel,
-        [sds((block + parts * HALO, channels), BF16), sds((parts, taps, channels), BF16)],
+        [
+            sds((block + parts * HALO, channels), BF16),
+            sds((parts, taps, channels), BF16),
+            sds((groups, block), BF16),
+            sds((rows, channels), BF16),
+        ],
         [
             pltpu.VMEM((2, tail, channels), BF16),
             pltpu.VMEM((2, parts, tail, LANES), F32),
-            pltpu.SemaphoreType.DMA((4,)),
-        ],
-        (projected, taps_major),
-        outside=(0, 1),
-    )
-    near = shifted(near, "seq", 1)
-
-    far, skt, x_all, kv, q0, pt, qt, ct, w = on_chip(
+            pltpu.SemaphoreType.DMA((6,)),
+        ],
+        (projected, taps_major, long_filter, out_cotangent),
+        outside=(0, 1, 2, 3),
+    )
+    near = ring(near, "seq")
+
+    far, skt, kv, q0, pt, qt, ct, w = on_chip(
         front_kernel,
         [
             sds((2 * tail, channels), BF16),
             sds((groups, members, block), F32),
-            sds((chunks, parts, rows, LANES), BF16),
             sds((chunks, 2, rows, LANES), BF16),
             sds((block, channels), BF16),
             sds((groups, width - members, block), BF16),
@@ -517,14 +525,10 @@
         [
             pltpu.VMEM((parts, HALO + rows, LANES), F32),
             pltpu.VMEM((block, block), BF16),
-            pltpu.VMEM((chunks, rows, LANES), BF16),
-            pltpu.SemaphoreType.DMA((chunks,)),
-            pltpu.SemaphoreType.DMA((chunks,)),
-        ],
-        (projected, taps_major, long_filter, skip_row, out_cotangent),
-        outside=(0, 4),
-    )
-    far = shifted(far, "seq", 1)
+        ],
+        (projected, taps_major, filters, skip_row, cots),
+    )
+    far = ring(far, "seq")
     kve, pta, qta, inner, stats = on_chip(
         middle_kernel,
         [
@@ -538,7 +542,7 @@
             pltpu.VMEM((parts, HALO + EDGE, LANES), F32),
             pltpu.VMEM((2, 8 * blocks, block), F32),
         ],
-        (near, x_all, taps_major, skt, kv, q0, pt, qt, ct, w),
+        (near, projected, taps_major, skt, kv, q0, pt, qt, ct, w),
     )
 
     dp_size = lax.axis_size("dp")
@@ -559,7 +563,7 @@
             sds((chunks, blocks, 2, block, LANES), F32),
         ],
         [],
-        (near, x_all, kv, kve),
+        (near, projected, kv, kve),
     )
     token_scale = 1.0 / math.sqrt(rows * lax.axis_size("seq"))
     out, pgr = on_chip(
@@ -570,10 +574,13 @@
             pltpu.VMEM((groups, members, block), F32),
             pltpu.VMEM((groups, 8, block), F32),
             pltpu.VMEM((chunks, parts * taps, 8, LANES), F32),
-            pltpu.VMEM((2, blocks, chunk_groups, members, block), F32),
-            pltpu.VMEM((2, blocks, chunk_groups, members, block), F32),
+        ]
+        + [
+            pltpu.VMEM((blocks, chunk_groups, members, block), F32),
+            pltpu.VMEM((blocks, chunk_groups, members, block), F32),
             pltpu.VMEM((2, blocks, block, LANES), F32),
-        ],
+        ]
+        * 2,
         (*stat_parts, skt, xf, kvf, pt, pta, qt, qta, ct, inner, w),
     )
     (out,) = on_chip(

time: 56.7 us -> 53.9 us (0.951)
  starting transfers between devices: 23.3 us -> 11.7 us
  waiting for transfers between devices: 10.9 us -> 20.3 us
  Pallas kernels: 20.8 us -> 20.2 us
    ppermute x2, waiting for transfers between devices: 1.2 us -> 10.8 us  [ring(): lax.ppermute(array, axis, [(i, (i + 1) % length) for i in range(length)])]
    ppermute x7, starting transfers between devices: 16.4 us -> 8.61 us  [crossed(): return lax.ppermute(array, axis, [(i, i ^ bit) for i in range(length)])]
    ppermute x2, starting transfers between devices: 6.91 us -> 3.13 us  [ring(): lax.ppermute(array, axis, [(i, (i + 1) % length) for i in range(length)])]
    pallas_call x7, Pallas kernels: 20.8 us -> 20.2 us  [on_chip(): pl.pallas_call(kernel, in_specs=[apart if number in outside else place fo...]
  transfers between devices with their start and end apart: 9 -> 9, of which waited for: 6 -> 7; matrix products, arithmetic and copies ran while one was open for 0% -> 0% of each run, Pallas kernels for 19% -> 20%
where the time goes in v5:
time: 53.9 us; the launch traced here: 53.7 us
  waiting for transfers between devices  20.3 us (38%)
  Pallas kernels  20.2 us (37%)
  starting transfers between devices  11.7 us (22%)
  local copies, waits for them, and re-layouts  0.84 us (2%)
  between operations  0.72 us (1%)
    pallas_call x7, Pallas kernels, on_chip(): pl.pallas_call(kernel, in_specs=[apart if number in outside else place fo...  20.2 us
    ppermute x2, waiting for transfers between devices, ring(): lax.ppermute(array, axis, [(i, (i + 1) % length) for i in range(length)])  10.8 us
    ppermute x7, waiting for transfers between devices, crossed(): return lax.ppermute(array, axis, [(i, i ^ bit) for i in range(length)])  9.42 us
    ppermute x7, starting transfers between devices, crossed(): return lax.ppermute(array, axis, [(i, i ^ bit) for i in range(length)])  8.61 us
    ppermute x2, starting transfers between devices, ring(): lax.ppermute(array, axis, [(i, (i + 1) % length) for i in range(length)])  3.13 us
  transfers between devices with their start and end apart: 9, of which 7 were waited for; matrix products, arithmetic and copies ran while one was open for 0% of the time, Pallas kernels for 20%

profile of v5, /device:TPU:0, one launch (start us, length us, event | category | flops | bytes accessed | tf_op | source)
XLA Modules:
  0.0 53.7 jit_solution(6689202854061553628)
XLA Ops:
  0.6 0.0 copy-start
  0.6 0.8 %reshape.12.skip_ref = bf16[1,1024]{1,0:T(2,128)(2,1)S(1)} reshape(bf16[1024]{0:T(1024)(128)(2,1)} %param.8) | data formatting | bytes 4096 | tf_op jit(solution)/shard_map/reshape | solution.py:490
  1.5 2.0 %shard_map.76 = (bf16[152,1024]{1,0:T(8,128)(2,1)S(1)}, bf16[3,7,1024]{2,1,0:T(8,128)(2,1)S(1)}, bf16[64,128]{1,0:T(8,128)(2,1)S(1)}, bf16[512,1024]{1,0:T(8,128)(2,1)S(1)}) custom-call(bf16[3,512,1024]{2,1,0:T(8,128)(2,1)} %x_ref.7, bf16[3,7,1024]{2,1,0:T(8,128)(2,1)} %bitcast.3, bf16[64,128]{1,0:T(8,128)(2,1)} %filt_hbm.1, bf16[512,1024]{1,0:T(8,128)(2,1)} %cot_hbm.1), custom_call_target="tpu_custom_call" | custom-call | tf_op jit(solution)/shard_map/pallas_call | solution.py:470
  3.5 0.0 copy-done
  3.5 5.5 %shard_map.77 = (bf16[272,1024]{1,0:T(8,128)(2,1)S(1)}, f32[64,16,128]{2,1,0:T(8,128)S(1)}, bf16[8,2,512,128]{3,2,1,0:T(8,128)(2,1)S(1)}, bf16[128,1024]{1,0:T(8...) custom-call(bf16[3,512,1024]{2,1,0:T(8,128)(2,1)S(1)} %copy-done, ...), custom_call_target="tpu_custom_call" | custom-call | tf_op jit(solution)/shard_map/pallas_call | solution.py:470
  9.0 0.5 %collective-permute-start = (bf16[272,1024]{1,0:T(8,128)(2,1)S(1)}, bf16[272,1024]{1,0:T(8,128)(2,1)S(1)}, u32[]{:S(2)}, u32[]{:S(2)}) collective-permute-start(bf16[272,1024]{1,0:T(8,128)(2,1)S(1)} %get-tuple-element.30), channel_id=1, source_target_pairs={{0,4},{4,8},{8,12},{12,16},{16,20},{20,24},{24,28},{28,0},{1,5},{5... | collective-permute-start | bytes 1671176 | tf_op jit(solution)/shard_map/ppermute | solution.py:443
  9.5 2.6 %collective-permute-start.1 = (bf16[152,1024]{1,0:T(8,128)(2,1)S(1)}, bf16[152,1024]{1,0:T(8,128)(2,1)S(1)}, u32[]{:S(2)}, u32[]{:S(2)}) collective-permute-start(bf16[152,1024]{1,0:T(8,128)(2,1)S(1)} %get-tuple-element.31), channel_id=1, source_target_pairs={{0,4},{4,8},{8,12},{12,16},{16,20},{20,24},{24,28},{28,0},{1,5},{5... | collective-permute-start | bytes 933896 | tf_op jit(solution)/shard_map/ppermute | solution.py:443
  12.1 10.8 %collective-permute-done.1.near_ref = bf16[152,1024]{1,0:T(8,128)(2,1)S(1)} collective-permute-done((bf16[152,1024]{1,0:T(8,128)(2,1)S(1)}, bf16[152,1024]{1,0:T(8,128)(2,1)S(1)}, u32[]{:S(2)}, u32[]{:S(2)}) %collective-permute-start.1) | collective-permute-done | bytes 311328 | tf_op jit(solution)/shard_map/ppermute | solution.py:443
  23.0 2.1 %shard_map.78 = (bf16[8,2,16,128]{3,2,1,0:T(8,128)(2,1)S(1)}, bf16[64,32,128]{2,1,0:T(8,128)(2,1)S(1)}, bf16[64,16,128]{2,1,0:T(8,128)(2,1)S(1)}, f32[64,64,128]{2,1,0:T(8,128)S(1)}, f32[8,128]{1,0:T(8,128)S(1)}) custom-call(bf16[152,1024]{1,0:T(8,128)(2,1)S(1)} %collective-permute-done.1.near_ref, bf16[3,512,1024]{2,1,0:T(8,128)(2,1)S(1)} %copy-done, ...), custom_call_target="tpu_custom_call" | custom-call | tf_op jit(solution)/shard_map/pallas_call | solution.py:470
  25.1 2.4 %collective-permute-start.2 = (f32[8,128]{1,0:T(8,128)S(1)}, f32[8,128]{1,0:T(8,128)S(1)}, u32[]{:S(2)}, u32[]{:S(2)}) collective-permute-start(f32[8,128]{1,0:T(8,128)S(1)} %get-tuple-element.39.refs_0_), channel_id=1, source_target_pairs={{0,1},{1,0},{2,3},{3,2},{4,5},{5,4},{6,7},{7,6},{8,9},{9,8},{10,11... | collective-permute-start | bytes 12296 | tf_op jit(solution)/shard_map/ppermute | solution.py:448
  27.4 2.6 %collective-permute-start.3 = (f32[8,128]{1,0:T(8,128)S(1)}, f32[8,128]{1,0:T(8,128)S(1)}, u32[]{:S(2)}, u32[]{:S(2)}) collective-permute-start(f32[8,128]{1,0:T(8,128)S(1)} %get-tuple-element.39.refs_0_), channel_id=1, source_target_pairs={{0,2},{1,3},{2,0},{3,1},{4,6},{5,7},{6,4},{7,5},{8,10},{9,11},{10,... | collective-permute-start | bytes 12296 | tf_op jit(solution)/shard_map/ppermute | solution.py:448
  30.0 0.0 collective-permute-start.4
  30.0 1.1 %shard_map.79 = (f32[8,4,3,136,128]{4,3,2,1,0:T(8,128)S(1)}, f32[8,4,2,128,128]{4,3,2,1,0:T(8,128)S(1)}) custom-call(bf16[152,1024]{1,0:T(8,128)(2,1)S(1)} %collective-permute-done.1.near_ref, bf16[3,512,1024]{2,1,0:T(8,128)(2,1)S(1)} %copy-done, bf16[8,2,512,128]{3,2,1,0:T(8,128)(2,1)S(1)} %get-tuple-element.33.kv_ref, ...), custom_call_target="tpu_custom_call" | custom-call | tf_op jit(solution)/shard_map/pallas_call | solution.py:470
  31.1 0.0 collective-permute-done.2.refs_1_
  31.1 0.8 %collective-permute-done.3.refs_2_ = f32[8,128]{1,0:T(8,128)S(1)} collective-permute-done((f32[8,128]{1,0:T(8,128)S(1)}, f32[8,128]{1,0:T(8,128)S(1)}, u32[]{:S(2)}, u32[]{:S(2)}) %collective-permute-start.3) | collective-permute-done | bytes 4128 | tf_op jit(solution)/shard_map/ppermute | solution.py:448
  32.0 3.5 %collective-permute-done.4.refs_3_ = f32[8,128]{1,0:T(8,128)S(1)} collective-permute-done((f32[8,128]{1,0:T(8,128)S(1)}, f32[8,128]{1,0:T(8,128)S(1)}, u32[]{:S(2)}, u32[]{:S(2)}) %collective-permute-start.4) | collective-permute-done | bytes 4128 | tf_op jit(solution)/shard_map/ppermute | solution.py:448
  35.4 7.5 %shard_map.80 = (f32[32,1024]{1,0:T(8,128)S(1)}, f32[64,16,128]{2,1,0:T(8,128)S(1)}) custom-call(f32[8,128]{1,0:T(8,128)S(1)} %get-tuple-element.39.refs_0_, f32[8,128]{1,0:T(8,128)S(1)} %collective-permute-done.2.refs_1_, f32[8,128]{1,0:T(8,128)S(1)} %collective-permute-done.3.refs_2_, f32[8,128]{1,0:T(8,128)S(1)} %collective-permute-done.4.refs_3_, ...), custom_call_target="tpu_custom_call" | custom-call | tf_op jit(solution)/shard_map/pallas_call | solution.py:470
  42.9 0.0 collective-permute-done.far_ref
  42.9 1.4 %shard_map.81 = f32[32,1024]{1,0:T(8,128)S(1)} custom-call(bf16[272,1024]{1,0:T(8,128)(2,1)S(1)} %collective-permute-done.far_ref, bf16[3,7,1024]{2,1,0:T(8,128)(2,1)S(1)} %get-tuple-element.27.taps_ref, f32[64,16,128]{2,1,0:T(8,128)S(1)} %get-tuple-element.46.pgr_ref, f32[32,1024]{1,0:T(8,128)S(1)} %get-tuple-element.47.out_ref), custom_call_target="tpu_custom_call" | custom-call | tf_op jit(solution)/shard_map/pallas_call | solution.py:470
  44.3 0.1 collective-permute-start.5
  44.4 1.3 %collective-permute-done.5 = f32[32,1024]{1,0:T(8,128)S(1)} collective-permute-done((f32[32,1024]{1,0:T(8,128)S(1)}, f32[32,1024]{1,0:T(8,128)S(1)}, u32[]{:S(2)}, u32[]{:S(2)}) %collective-permute-start.5) | collective-permute-done | bytes 131104 | tf_op jit(solution)/shard_map/ppermute | solution.py:448
  45.7 0.6 %collective-permute-start.6 = (bf16[32,1024]{1,0:T(8,128)(2,1)S(1)}, bf16[32,1024]{1,0:T(8,128)(2,1)S(1)}, u32[]{:S(2)}, u32[]{:S(2)}) collective-permute-start(bf16[32,1024]{1,0:T(8,128)(2,1)S(1)} %add_convert_fusion.refs_0_), channel_id=1, source_target_pairs={{0,8},{4,12},{8,0},{12,4},{16,24},{20,28},{24,16},{28,20},{1,9},{5... | collective-permute-start | bytes 196616 | tf_op jit(solution)/shard_map/ppermute | solution.py:448
  46.4 1.5 %collective-permute-start.7 = (bf16[32,1024]{1,0:T(8,128)(2,1)S(1)}, bf16[32,1024]{1,0:T(8,128)(2,1)S(1)}, u32[]{:S(2)}, u32[]{:S(2)}) collective-permute-start(bf16[32,1024]{1,0:T(8,128)(2,1)S(1)} %add_convert_fusion.refs_0_), channel_id=1, source_target_pairs={{0,16},{4,20},{8,24},{12,28},{16,0},{20,4},{24,8},{28,12},{1,17},{... | collective-permute-start | bytes 196616 | tf_op jit(solution)/shard_map/ppermute | solution.py:448
  47.9 1.4 %collective-permute-start.8 = (bf16[32,1024]{1,0:T(8,128)(2,1)S(1)}, bf16[32,1024]{1,0:T(8,128)(2,1)S(1)}, u32[]{:S(2)}, u32[]{:S(2)}) collective-permute-start(bf16[32,1024]{1,0:T(8,128)(2,1)S(1)} %add_convert_fusion.refs_0_), channel_id=1, source_target_pairs={{0,24},{4,28},{8,16},{12,20},{16,8},{20,12},{24,0},{28,4},{1,25},{... | collective-permute-start | bytes 196616 | tf_op jit(solution)/shard_map/ppermute | solution.py:448
  49.3 0.8 %collective-permute-done.6.refs_1_ = bf16[32,1024]{1,0:T(8,128)(2,1)S(1)} collective-permute-done((bf16[32,1024]{1,0:T(8,128)(2,1)S(1)}, bf16[32,1024]{1,0:T(8,128)(2,1)S(1)}, u32[]{:S(2)}, u32[]{:S(2)}) %collective-permute-start.6) | collective-permute-done | bytes 65568 | tf_op jit(solution)/shard_map/ppermute | solution.py:448
  50.1 0.5 collective-permute-done.7.refs_2_
  50.6 2.4 %collective-permute-done.8.refs_3_ = bf16[32,1024]{1,0:T(8,128)(2,1)S(1)} collective-permute-done((bf16[32,1024]{1,0:T(8,128)(2,1)S(1)}, bf16[32,1024]{1,0:T(8,128)(2,1)S(1)}, u32[]{:S(2)}, u32[]{:S(2)}) %collective-permute-start.8) | collective-permute-done | bytes 65568 | tf_op jit(solution)/shard_map/ppermute | solution.py:448
  53.1 0.7 %shard_map.82 = (f32[3,7,1024]{2,1,0:T(8,128)}, f32[64,128]{1,0:T(8,128)}, f32[1,1024]{1,0:T(1,128)}) custom-call(bf16[32,1024]{1,0:T(8,128)(2,1)S(1)} %add_convert_fusion.refs_0_, bf16[32,1024]{1,0:T(8,128)(2,1)S(1)} %collective-permute-done.6.refs_1_, bf16[32,1024]{1,0:T(8,128)(2,1)S(1)} %collective-permute-done.7.refs_2_, ...), custom_call_target="tpu_custom_call" | custom-call | tf_op jit(solution)/shard_map/pallas_call | solution.py:470
  (1 shorter events, 0.0 us)
Async XLA Ops:
  0.6 2.9 %copy-start = (bf16[3,512,1024]{2,1,0:T(8,128)(2,1)S(1)}, bf16[3,512,1024]{2,1,0:T(8,128)(2,1)}, u32[]{:S(2)}) copy-start(bf16[3,512,1024]{2,1,0:T(8,128)(2,1)} %x_ref.7) | copy-start | bytes 9437188
  9.0 33.9 %collective-permute-start = (bf16[272,1024]{1,0:T(8,128)(2,1)S(1)}, bf16[272,1024]{1,0:T(8,128)(2,1)S(1)}, u32[]{:S(2)}, u32[]{:S(2)}) collective-permute-start(bf16[272,1024]{1,0:T(8,128)(2,1)S(1)} %get-tuple-element.30), channel_id=1, source_target_pairs={{0,4},{4,8},{8,12},{12,16},{16,20},{20,24},{24,28},{28,0},{1,5},{5... | collective-permute-start | bytes 1671176 | tf_op jit(solution)/shard_map/ppermute | solution.py:443
  9.5 13.4 %collective-permute-start.1 = (bf16[152,1024]{1,0:T(8,128)(2,1)S(1)}, bf16[152,1024]{1,0:T(8,128)(2,1)S(1)}, u32[]{:S(2)}, u32[]{:S(2)}) collective-permute-start(bf16[152,1024]{1,0:T(8,128)(2,1)S(1)} %get-tuple-element.31), channel_id=1, source_target_pairs={{0,4},{4,8},{8,12},{12,16},{16,20},{20,24},{24,28},{28,0},{1,5},{5... | collective-permute-start | bytes 933896 | tf_op jit(solution)/shard_map/ppermute | solution.py:443
  25.1 6.1 %collective-permute-start.2 = (f32[8,128]{1,0:T(8,128)S(1)}, f32[8,128]{1,0:T(8,128)S(1)}, u32[]{:S(2)}, u32[]{:S(2)}) collective-permute-start(f32[8,128]{1,0:T(8,128)S(1)} %get-tuple-element.39.refs_0_), channel_id=1, source_target_pairs={{0,1},{1,0},{2,3},{3,2},{4,5},{5,4},{6,7},{7,6},{8,9},{9,8},{10,11... | collective-permute-start | bytes 12296 | tf_op jit(solution)/shard_map/ppermute | solution.py:448
  27.4 4.5 %collective-permute-start.3 = (f32[8,128]{1,0:T(8,128)S(1)}, f32[8,128]{1,0:T(8,128)S(1)}, u32[]{:S(2)}, u32[]{:S(2)}) collective-permute-start(f32[8,128]{1,0:T(8,128)S(1)} %get-tuple-element.39.refs_0_), channel_id=1, source_target_pairs={{0,2},{1,3},{2,0},{3,1},{4,6},{5,7},{6,4},{7,5},{8,10},{9,11},{10,... | collective-permute-start | bytes 12296 | tf_op jit(solution)/shard_map/ppermute | solution.py:448
  30.0 5.4 %collective-permute-start.4 = (f32[8,128]{1,0:T(8,128)S(1)}, f32[8,128]{1,0:T(8,128)S(1)}, u32[]{:S(2)}, u32[]{:S(2)}) collective-permute-start(f32[8,128]{1,0:T(8,128)S(1)} %get-tuple-element.39.refs_0_), channel_id=1, source_target_pairs={{0,3},{1,2},{2,1},{3,0},{4,7},{5,6},{6,5},{7,4},{8,11},{9,10},{10,... | collective-permute-start | bytes 12296 | tf_op jit(solution)/shard_map/ppermute | solution.py:448
  44.3 1.4 %collective-permute-start.5 = (f32[32,1024]{1,0:T(8,128)S(1)}, f32[32,1024]{1,0:T(8,128)S(1)}, u32[]{:S(2)}, u32[]{:S(2)}) collective-permute-start(f32[32,1024]{1,0:T(8,128)S(1)} %shard_map.81), channel_id=1, source_target_pairs={{0,4},{4,0},{8,12},{12,8},{16,20},{20,16},{24,28},{28,24},{1,5},{5... | collective-permute-start | bytes 393224 | tf_op jit(solution)/shard_map/ppermute | solution.py:448
  45.7 4.4 %collective-permute-start.6 = (bf16[32,1024]{1,0:T(8,128)(2,1)S(1)}, bf16[32,1024]{1,0:T(8,128)(2,1)S(1)}, u32[]{:S(2)}, u32[]{:S(2)}) collective-permute-start(bf16[32,1024]{1,0:T(8,128)(2,1)S(1)} %add_convert_fusion.refs_0_), channel_id=1, source_target_pairs={{0,8},{4,12},{8,0},{12,4},{16,24},{20,28},{24,16},{28,20},{1,9},{5... | collective-permute-start | bytes 196616 | tf_op jit(solution)/shard_map/ppermute | solution.py:448
  46.4 4.3 %collective-permute-start.7 = (bf16[32,1024]{1,0:T(8,128)(2,1)S(1)}, bf16[32,1024]{1,0:T(8,128)(2,1)S(1)}, u32[]{:S(2)}, u32[]{:S(2)}) collective-permute-start(bf16[32,1024]{1,0:T(8,128)(2,1)S(1)} %add_convert_fusion.refs_0_), channel_id=1, source_target_pairs={{0,16},{4,20},{8,24},{12,28},{16,0},{20,4},{24,8},{28,12},{1,17},{... | collective-permute-start | bytes 196616 | tf_op jit(solution)/shard_map/ppermute | solution.py:448
  47.9 5.2 %collective-permute-start.8 = (bf16[32,1024]{1,0:T(8,128)(2,1)S(1)}, bf16[32,1024]{1,0:T(8,128)(2,1)S(1)}, u32[]{:S(2)}, u32[]{:S(2)}) collective-permute-start(bf16[32,1024]{1,0:T(8,128)(2,1)S(1)} %add_convert_fusion.refs_0_), channel_id=1, source_target_pairs={{0,24},{4,28},{8,16},{12,20},{16,8},{20,12},{24,0},{28,4},{1,25},{... | collective-permute-start | bytes 196616 | tf_op jit(solution)/shard_map/ppermute | solution.py:448

commit v6 on v5

--- a/solution.py
+++ b/solution.py
@@ -75,8 +75,7 @@
             near_ref[at : at + HALO, lane] = jnp.where(inside, far_ref[part, tail - HALO :, lane], 0)
         k = featurize(buf, 1, HALO, block, taps_ref.at[:, :, lane])
         v = featurize(buf, 2, HALO, block, taps_ref.at[:, :, lane])
-        both = (k.astype(F32) * v.astype(F32)).astype(BF16)
-        near_ref[:block, lane] = jnp.where(inside, both, 0)
+        near_ref[:block, lane] = jnp.where(inside, k * v, 0)
 
     at_once = math.gcd(channels // LANES, bufs.shape[0])
 
@@ -127,7 +126,7 @@
             q0_ref[:, lane] = q
         else:
             place = slice((number - 1) * members, number * members)
-            product = (k.astype(F32) * v.astype(F32)).astype(BF16)
+            product = k * v
             pt_ref[group_at, place, :] = product.T.reshape(groups, members, block)
             qt_ref[group_at, place, :] = q.T.reshape(groups, members, block)
         place = slice(number * members, (number + 1) * members)
@@ -182,7 +181,7 @@
         k0 = jnp.concatenate([k_edge, kv_ref[chunk, 0, EDGE:block, :]], axis=0)
         v0 = jnp.concatenate([v_edge, kv_ref[chunk, 1, EDGE:block, :]], axis=0)
         q0 = jnp.concatenate([q_edge, q0_ref[EDGE:, lane]], axis=0)
-        p0 = (k0.astype(F32) * v0.astype(F32)).astype(BF16)
+        p0 = k0 * v0
         pta_ref[group_at, :members, :] = near_ref[:block, lane].T.reshape(groups, members, block)
         pta_ref[group_at, members:, :] = p0.T.reshape(groups, members, block)
         qta_ref[group_at] = q0.T.reshape(groups, members, block)
@@ -227,7 +226,7 @@
             )
 
 
-def prep_kernel(near_ref, x_ref, kv_ref, kve_ref, xf_ref, kvf_ref):
+def prep_kernel(near_ref, x_ref, kv_ref, kve_ref, xf_ref, kvf_ref, xq_ref, buf):
     parts, rows, channels = x_ref.shape
     block = near_ref.shape[0] - parts * HALO
     blocks = rows // block
@@ -235,14 +234,18 @@
     @pl.loop(0, channels // LANES)
     def _(chunk):
         lane = pl.ds(pl.multiple_of(chunk * LANES, LANES), LANES)
-        for part in range(parts):
+        buf[:HALO, :] = near_ref[block : block + HALO, lane].astype(F32)
+        buf[HALO:, :] = x_ref[0, :, lane].astype(F32)
+        for tap in range(xq_ref.shape[1]):
+            xq_ref[chunk, tap] = buf[HALO - tap : HALO - tap + rows, :].astype(BF16)
+        for part in range(1, parts):
             at = block + part * HALO
-            xf_ref[chunk, 0, part, :HALO, :] = near_ref[at : at + HALO, lane].astype(F32)
+            xf_ref[chunk, 0, part - 1, :HALO, :] = near_ref[at : at + HALO, lane].astype(F32)
             for number in range(blocks):
                 at = number * block
                 if number:
-                    xf_ref[chunk, number, part, :HALO, :] = x_ref[part, at - HALO : at, lane].astype(F32)
-                xf_ref[chunk, number, part, HALO:, :] = x_ref[part, at : at + block, lane].astype(F32)
+                    xf_ref[chunk, number, part - 1, :HALO, :] = x_ref[part, at - HALO : at, lane].astype(F32)
+                xf_ref[chunk, number, part - 1, HALO:, :] = x_ref[part, at : at + block, lane].astype(F32)
         for part in range(2):
             kvf_ref[chunk, 0, part, :EDGE, :] = kve_ref[chunk, part].astype(F32)
             kvf_ref[chunk, 0, part, EDGE:, :] = kv_ref[chunk, part, EDGE:block, :].astype(F32)
@@ -291,10 +294,10 @@
 
 def back_kernel(channels_all, token_scale, taps, n_stats, *refs):
     stats_refs = refs[:n_stats]
-    (skt_ref, xf_ref, kvf_ref, pt_ref, pta_ref, qt_ref, qta_ref, ct_ref, inner_ref, w_ref,
-     out_ref, pgr_ref, coef, skip_acc, filt_acc, sums, *slots) = refs[n_stats:]
+    (skt_ref, xf_ref, kvf_ref, xq_ref, pt_ref, pta_ref, qt_ref, qta_ref, ct_ref, inner_ref, w_ref,
+     out_ref, pgr_ref, coef, skip_acc, filt_acc, sums, eye, *slots) = refs[n_stats:]
     chunks, blocks = xf_ref.shape[:2]
-    parts = xf_ref.shape[2]
+    parts = 1 + xf_ref.shape[2]
     width, block = ct_ref.shape[1:]
     members = width // blocks
     groups = LANES // members
@@ -310,6 +313,7 @@
         coef[1, place, :] = jnp.broadcast_to(fall[number : number + 1], (members, block))
     row, col = lag_masks(block)
     slots = (slots[:3], slots[3:])
+    eye[...] = jnp.where(row == col, 1.0, 0.0)
 
     def group_part(chunk, slot, within):
         pg, qg, _ = slots[slot]
@@ -343,7 +347,7 @@
             pg[number, within] = (
                 grad[(number + 1) * members : (number + 2) * members] + own * conv_grad[span]
             )
-            qg[number, within] = query_grad[span]
+            qg[number, within] = query_grad[span].astype(BF16)
         both = matmul(cot, jnp.concatenate([now, every[:width]], axis=1), ((0,), (0,)))
         lagged = jnp.where(col <= row, both[:, :block], both[:, block:])
         skewed = lagged[:8]
@@ -352,10 +356,24 @@
         filt_acc[group] = skewed
 
     def turn(slot):
-        pg, qg, gn = slots[slot]
+        pg, _, gn = slots[slot]
         for number in range(blocks):
-            gn[0, number] = qg[number].reshape(LANES, block).T
-            gn[1, number] = pg[number].reshape(LANES, block).T
+            gn[number] = pg[number].reshape(LANES, block).T
+
+    def query_steps(chunk, slot):
+        qg = slots[slot][1]
+
+        def step(first):
+            grads = jnp.concatenate([qg[number].reshape(LANES, block) for number in range(blocks)], axis=1)
+            some = range(first, min(first + 2, taps))
+            every = matmul(
+                grads, jnp.concatenate([xq_ref[chunk, tap] for tap in some], axis=1), ((1,), (0,))
+            )
+            for place, tap in enumerate(some):
+                own = every[:, place * LANES : (place + 1) * LANES] * eye[...]
+                sums[chunk, tap] = own.reshape(LANES // 8, 8, LANES).sum(axis=0)
+
+        return [functools.partial(step, first) for first in range(0, taps, 2)]
 
     def tap_steps(chunk, slot):
         gn = slots[slot][2]
@@ -364,32 +382,29 @@
 
         def step(part, number):
             for at in range(0, block, piece):
-                if part:
-                    grads = gn[1, number, at : at + piece, :]
-                    grads = grads * kvf_ref[chunk, number, 2 - part, at : at + piece, :]
-                else:
-                    grads = gn[0, number, at : at + piece, :]
+                grads = gn[number, at : at + piece, :]
+                grads = grads * kvf_ref[chunk, number, 2 - part, at : at + piece, :]
                 for tap in range(taps):
                     start = HALO + at - tap
-                    term = grads * xf_ref[chunk, number, part, start : start + piece, :]
+                    term = grads * xf_ref[chunk, number, part - 1, start : start + piece, :]
                     term = term.reshape(piece // 8, 8, LANES).sum(axis=0)
                     totals[part, tap] = totals[part, tap] + term if (part, tap) in totals else term
             if number == blocks - 1:
                 for tap in range(taps):
                     sums[chunk, part * taps + tap] = totals[part, tap]
 
-        return [functools.partial(step, part, number) for part in range(parts) for number in range(blocks)]
+        return [functools.partial(step, part, number) for part in range(1, parts) for number in range(blocks)]
 
     def group_steps(chunk, slot):
         return [functools.partial(group_part, chunk, slot, within) for within in range(groups)]
 
     def whole_step(chunk, slot):
         turn(1 - slot)
-        braid(group_steps(chunk, slot), tap_steps(chunk - 2, slot))
+        braid(group_steps(chunk, slot), tap_steps(chunk - 2, slot) + query_steps(chunk - 1, 1 - slot))
 
     braid(group_steps(0, 0), [])
     if chunks > 1:
-        braid(group_steps(1, 1), [])
+        braid(group_steps(1, 1), query_steps(0, 0))
         turn(0)
 
         @pl.loop(1, chunks // 2)
@@ -403,7 +418,8 @@
         braid([], tap_steps(chunks - 2, chunks % 2))
     else:
         turn(0)
-    braid([], tap_steps(chunks - 1, (chunks - 1) % 2))
+    last = (chunks - 1) % 2
+    braid(query_steps(chunks - 1, last), tap_steps(chunks - 1, last))
 
     flip = jnp.where(((row + col) % block) == 0, 1.0, 0.0).astype(F32)
     lags = filt_acc[:, 0, :]
@@ -502,7 +518,7 @@
         ],
         [
             pltpu.VMEM((2, tail, channels), BF16),
-            pltpu.VMEM((2, parts, tail, LANES), F32),
+            pltpu.VMEM((4, parts, tail, LANES), F32),
             pltpu.SemaphoreType.DMA((6,)),
         ],
         (projected, taps_major, long_filter, out_cotangent),
@@ -556,13 +572,14 @@
         else:
             stat_parts = [current + crossed(current, "dp", bit)]
             bit *= 2
-    xf, kvf = on_chip(
+    xf, kvf, xq = on_chip(
         prep_kernel,
         [
-            sds((chunks, blocks, parts, HALO + block, LANES), F32),
+            sds((chunks, blocks, 2, HALO + block, LANES), F32),
             sds((chunks, blocks, 2, block, LANES), F32),
-        ],
-        [],
+            sds((chunks, taps, rows, LANES), BF16),
+        ],
+        [pltpu.VMEM((HALO + rows, LANES), F32)],
         (near, projected, kv, kve),
     )
     token_scale = 1.0 / math.sqrt(rows * lax.axis_size("seq"))
@@ -574,14 +591,15 @@
             pltpu.VMEM((groups, members, block), F32),
             pltpu.VMEM((groups, 8, block), F32),
             pltpu.VMEM((chunks, parts * taps, 8, LANES), F32),
+            pltpu.VMEM((LANES, LANES), F32),
         ]
         + [
             pltpu.VMEM((blocks, chunk_groups, members, block), F32),
-            pltpu.VMEM((blocks, chunk_groups, members, block), F32),
-            pltpu.VMEM((2, blocks, block, LANES), F32),
+            pltpu.VMEM((blocks, chunk_groups, members, block), BF16),
+            pltpu.VMEM((blocks, block, LANES), F32),
         ]
         * 2,
-        (*stat_parts, skt, xf, kvf, pt, pta, qt, qta, ct, inner, w),
+        (*stat_parts, skt, xf, kvf, xq, pt, pta, qt, qta, ct, inner, w),
     )
     (out,) = on_chip(
         rim_kernel,

time: 53.9 us -> 53.3 us (0.989)
  waiting for transfers between devices: 20.3 us -> 19.7 us
    ppermute x7, waiting for transfers between devices: 9.42 us -> 8.83 us  [crossed(): return lax.ppermute(array, axis, [(i, i ^ bit) for i in range(length)])]
where the time goes in v6:
time: 53.3 us; the launch traced here: 53.2 us
  Pallas kernels  20.2 us (38%)
  waiting for transfers between devices  19.7 us (37%)
  starting transfers between devices  11.7 us (22%)
  local copies, waits for them, and re-layouts  0.84 us (2%)
  between operations  0.73 us (1%)
    pallas_call x7, Pallas kernels, on_chip(): pl.pallas_call(kernel, in_specs=[apart if number in outside else place fo...  20.2 us
    ppermute x2, waiting for transfers between devices, ring(): lax.ppermute(array, axis, [(i, (i + 1) % length) for i in range(length)])  10.8 us
    ppermute x7, waiting for transfers between devices, crossed(): return lax.ppermute(array, axis, [(i, i ^ bit) for i in range(length)])  8.83 us
    ppermute x7, starting transfers between devices, crossed(): return lax.ppermute(array, axis, [(i, i ^ bit) for i in range(length)])  8.6 us
    ppermute x2, starting transfers between devices, ring(): lax.ppermute(array, axis, [(i, (i + 1) % length) for i in range(length)])  3.13 us
  transfers between devices with their start and end apart: 9, of which 7 were waited for; matrix products, arithmetic and copies ran while one was open for 0% of the time, Pallas kernels for 20%

profile of v6, /device:TPU:0, one launch (start us, length us, event | category | flops | bytes accessed | tf_op | source)
XLA Modules:
  0.0 53.2 jit_solution(5137815014232202565)
XLA Ops:
  0.6 0.0 copy-start
  0.6 0.8 %reshape.12.skip_ref = bf16[1,1024]{1,0:T(2,128)(2,1)S(1)} reshape(bf16[1024]{0:T(1024)(128)(2,1)} %param.8) | data formatting | bytes 4096 | tf_op jit(solution)/shard_map/reshape | solution.py:506
  1.5 1.9 %shard_map.76 = (bf16[152,1024]{1,0:T(8,128)(2,1)S(1)}, bf16[3,7,1024]{2,1,0:T(8,128)(2,1)S(1)}, bf16[64,128]{1,0:T(8,128)(2,1)S(1)}, bf16[512,1024]{1,0:T(8,128)(2,1)S(1)}) custom-call(bf16[3,512,1024]{2,1,0:T(8,128)(2,1)} %x_ref.7, bf16[3,7,1024]{2,1,0:T(8,128)(2,1)} %bitcast.3, bf16[64,128]{1,0:T(8,128)(2,1)} %filt_hbm.1, bf16[512,1024]{1,0:T(8,128)(2,1)} %cot_hbm.1), custom_call_target="tpu_custom_call" | custom-call | tf_op jit(solution)/shard_map/pallas_call | solution.py:486
  3.4 0.0 copy-done
  3.4 5.3 %shard_map.77 = (bf16[272,1024]{1,0:T(8,128)(2,1)S(1)}, f32[64,16,128]{2,1,0:T(8,128)S(1)}, bf16[8,2,512,128]{3,2,1,0:T(8,128)(2,1)S(1)}, bf16[128,1024]{1,0:T(8...) custom-call(bf16[3,512,1024]{2,1,0:T(8,128)(2,1)S(1)} %copy-done, ...), custom_call_target="tpu_custom_call" | custom-call | tf_op jit(solution)/shard_map/pallas_call | solution.py:486
  8.8 0.5 %collective-permute-start = (bf16[272,1024]{1,0:T(8,128)(2,1)S(1)}, bf16[272,1024]{1,0:T(8,128)(2,1)S(1)}, u32[]{:S(2)}, u32[]{:S(2)}) collective-permute-start(bf16[272,1024]{1,0:T(8,128)(2,1)S(1)} %get-tuple-element.31), channel_id=1, source_target_pairs={{0,4},{4,8},{8,12},{12,16},{16,20},{20,24},{24,28},{28,0},{1,5},{5... | collective-permute-start | bytes 1671176 | tf_op jit(solution)/shard_map/ppermute | solution.py:459
  9.3 2.6 %collective-permute-start.1 = (bf16[152,1024]{1,0:T(8,128)(2,1)S(1)}, bf16[152,1024]{1,0:T(8,128)(2,1)S(1)}, u32[]{:S(2)}, u32[]{:S(2)}) collective-permute-start(bf16[152,1024]{1,0:T(8,128)(2,1)S(1)} %get-tuple-element.32), channel_id=1, source_target_pairs={{0,4},{4,8},{8,12},{12,16},{16,20},{20,24},{24,28},{28,0},{1,5},{5... | collective-permute-start | bytes 933896 | tf_op jit(solution)/shard_map/ppermute | solution.py:459
  11.9 10.8 %collective-permute-done.1.near_ref = bf16[152,1024]{1,0:T(8,128)(2,1)S(1)} collective-permute-done((bf16[152,1024]{1,0:T(8,128)(2,1)S(1)}, bf16[152,1024]{1,0:T(8,128)(2,1)S(1)}, u32[]{:S(2)}, u32[]{:S(2)}) %collective-permute-start.1) | collective-permute-done | bytes 311328 | tf_op jit(solution)/shard_map/ppermute | solution.py:459
  22.7 2.1 %shard_map.78 = (bf16[8,2,16,128]{3,2,1,0:T(8,128)(2,1)S(1)}, bf16[64,32,128]{2,1,0:T(8,128)(2,1)S(1)}, bf16[64,16,128]{2,1,0:T(8,128)(2,1)S(1)}, f32[64,64,128]{2,1,0:T(8,128)S(1)}, f32[8,128]{1,0:T(8,128)S(1)}) custom-call(bf16[152,1024]{1,0:T(8,128)(2,1)S(1)} %collective-permute-done.1.near_ref, bf16[3,512,1024]{2,1,0:T(8,128)(2,1)S(1)} %copy-done, ...), custom_call_target="tpu_custom_call" | custom-call | tf_op jit(solution)/shard_map/pallas_call | solution.py:486
  24.8 2.4 %collective-permute-start.2 = (f32[8,128]{1,0:T(8,128)S(1)}, f32[8,128]{1,0:T(8,128)S(1)}, u32[]{:S(2)}, u32[]{:S(2)}) collective-permute-start(f32[8,128]{1,0:T(8,128)S(1)} %get-tuple-element.40.refs_0_), channel_id=1, source_target_pairs={{0,1},{1,0},{2,3},{3,2},{4,5},{5,4},{6,7},{7,6},{8,9},{9,8},{10,11... | collective-permute-start | bytes 12296 | tf_op jit(solution)/shard_map/ppermute | solution.py:464
  27.2 2.6 %collective-permute-start.3 = (f32[8,128]{1,0:T(8,128)S(1)}, f32[8,128]{1,0:T(8,128)S(1)}, u32[]{:S(2)}, u32[]{:S(2)}) collective-permute-start(f32[8,128]{1,0:T(8,128)S(1)} %get-tuple-element.40.refs_0_), channel_id=1, source_target_pairs={{0,2},{1,3},{2,0},{3,1},{4,6},{5,7},{6,4},{7,5},{8,10},{9,11},{10,... | collective-permute-start | bytes 12296 | tf_op jit(solution)/shard_map/ppermute | solution.py:464
  29.8 0.0 collective-permute-start.4
  29.8 1.7 %shard_map.79 = (f32[8,4,2,136,128]{4,3,2,1,0:T(8,128)S(1)}, f32[8,4,2,128,128]{4,3,2,1,0:T(8,128)S(1)}, bf16[8,7,512,128]{3,2,1,0:T(8,128)(2,1)S(1)}) custom-call(bf16[152,1024]{1,0:T(8,128)(2,1)S(1)} %collective-permute-done.1.near_ref, bf16[3,512,1024]{2,1,0:T(8,128)(2,1)S(1)} %copy-done, bf16[8,2,512,128]{3,2,1,0:T(8,128)(2,1)S(1)} %get-tuple-element.34.kv_ref, ...), custom_call_target="tpu_custom_call" | custom-call | tf_op jit(solution)/shard_map/pallas_call | solution.py:486
  31.5 0.0 collective-permute-done.2.refs_1_
  31.5 0.2 collective-permute-done.3.refs_2_
  31.7 3.5 %collective-permute-done.4.refs_3_ = f32[8,128]{1,0:T(8,128)S(1)} collective-permute-done((f32[8,128]{1,0:T(8,128)S(1)}, f32[8,128]{1,0:T(8,128)S(1)}, u32[]{:S(2)}, u32[]{:S(2)}) %collective-permute-start.4) | collective-permute-done | bytes 4128 | tf_op jit(solution)/shard_map/ppermute | solution.py:464
  35.2 7.1 %shard_map.80 = (f32[32,1024]{1,0:T(8,128)S(1)}, f32[64,16,128]{2,1,0:T(8,128)S(1)}) custom-call(f32[8,128]{1,0:T(8,128)S(1)} %get-tuple-element.40.refs_0_, f32[8,128]{1,0:T(8,128)S(1)} %collective-permute-done.2.refs_1_, f32[8,128]{1,0:T(8,128)S(1)} %collective-permute-done.3.refs_2_, f32[8,128]{1,0:T(8,128)S(1)} %collective-permute-done.4.refs_3_, ...), custom_call_target="tpu_custom_call" | custom-call | tf_op jit(solution)/shard_map/pallas_call | solution.py:486
  42.3 0.0 collective-permute-done.far_ref
  42.3 1.4 %shard_map.81 = f32[32,1024]{1,0:T(8,128)S(1)} custom-call(bf16[272,1024]{1,0:T(8,128)(2,1)S(1)} %collective-permute-done.far_ref, bf16[3,7,1024]{2,1,0:T(8,128)(2,1)S(1)} %get-tuple-element.28.taps_ref, f32[64,16,128]{2,1,0:T(8,128)S(1)} %get-tuple-element.48.pgr_ref, f32[32,1024]{1,0:T(8,128)S(1)} %get-tuple-element.49.out_ref), custom_call_target="tpu_custom_call" | custom-call | tf_op jit(solution)/shard_map/pallas_call | solution.py:486
  43.7 0.1 collective-permute-start.5
  43.8 1.3 %collective-permute-done.5 = f32[32,1024]{1,0:T(8,128)S(1)} collective-permute-done((f32[32,1024]{1,0:T(8,128)S(1)}, f32[32,1024]{1,0:T(8,128)S(1)}, u32[]{:S(2)}, u32[]{:S(2)}) %collective-permute-start.5) | collective-permute-done | bytes 131104 | tf_op jit(solution)/shard_map/ppermute | solution.py:464
  45.1 0.7 %collective-permute-start.6 = (bf16[32,1024]{1,0:T(8,128)(2,1)S(1)}, bf16[32,1024]{1,0:T(8,128)(2,1)S(1)}, u32[]{:S(2)}, u32[]{:S(2)}) collective-permute-start(bf16[32,1024]{1,0:T(8,128)(2,1)S(1)} %add_convert_fusion.refs_0_), channel_id=1, source_target_pairs={{0,8},{4,12},{8,0},{12,4},{16,24},{20,28},{24,16},{28,20},{1,9},{5... | collective-permute-start | bytes 196616 | tf_op jit(solution)/shard_map/ppermute | solution.py:464
  45.8 1.5 %collective-permute-start.7 = (bf16[32,1024]{1,0:T(8,128)(2,1)S(1)}, bf16[32,1024]{1,0:T(8,128)(2,1)S(1)}, u32[]{:S(2)}, u32[]{:S(2)}) collective-permute-start(bf16[32,1024]{1,0:T(8,128)(2,1)S(1)} %add_convert_fusion.refs_0_), channel_id=1, source_target_pairs={{0,16},{4,20},{8,24},{12,28},{16,0},{20,4},{24,8},{28,12},{1,17},{... | collective-permute-start | bytes 196616 | tf_op jit(solution)/shard_map/ppermute | solution.py:464
  47.3 1.4 %collective-permute-start.8 = (bf16[32,1024]{1,0:T(8,128)(2,1)S(1)}, bf16[32,1024]{1,0:T(8,128)(2,1)S(1)}, u32[]{:S(2)}, u32[]{:S(2)}) collective-permute-start(bf16[32,1024]{1,0:T(8,128)(2,1)S(1)} %add_convert_fusion.refs_0_), channel_id=1, source_target_pairs={{0,24},{4,28},{8,16},{12,20},{16,8},{20,12},{24,0},{28,4},{1,25},{... | collective-permute-start | bytes 196616 | tf_op jit(solution)/shard_map/ppermute | solution.py:464
  48.7 0.8 %collective-permute-done.6.refs_1_ = bf16[32,1024]{1,0:T(8,128)(2,1)S(1)} collective-permute-done((bf16[32,1024]{1,0:T(8,128)(2,1)S(1)}, bf16[32,1024]{1,0:T(8,128)(2,1)S(1)}, u32[]{:S(2)}, u32[]{:S(2)}) %collective-permute-start.6) | collective-permute-done | bytes 65568 | tf_op jit(solution)/shard_map/ppermute | solution.py:464
  49.5 0.6 %collective-permute-done.7.refs_2_ = bf16[32,1024]{1,0:T(8,128)(2,1)S(1)} collective-permute-done((bf16[32,1024]{1,0:T(8,128)(2,1)S(1)}, bf16[32,1024]{1,0:T(8,128)(2,1)S(1)}, u32[]{:S(2)}, u32[]{:S(2)}) %collective-permute-start.7) | collective-permute-done | bytes 65568 | tf_op jit(solution)/shard_map/ppermute | solution.py:464
  50.1 2.4 %collective-permute-done.8.refs_3_ = bf16[32,1024]{1,0:T(8,128)(2,1)S(1)} collective-permute-done((bf16[32,1024]{1,0:T(8,128)(2,1)S(1)}, bf16[32,1024]{1,0:T(8,128)(2,1)S(1)}, u32[]{:S(2)}, u32[]{:S(2)}) %collective-permute-start.8) | collective-permute-done | bytes 65568 | tf_op jit(solution)/shard_map/ppermute | solution.py:464
  52.5 0.7 %shard_map.82 = (f32[3,7,1024]{2,1,0:T(8,128)}, f32[64,128]{1,0:T(8,128)}, f32[1,1024]{1,0:T(1,128)}) custom-call(bf16[32,1024]{1,0:T(8,128)(2,1)S(1)} %add_convert_fusion.refs_0_, bf16[32,1024]{1,0:T(8,128)(2,1)S(1)} %collective-permute-done.6.refs_1_, bf16[32,1024]{1,0:T(8,128)(2,1)S(1)} %collective-permute-done.7.refs_2_, ...), custom_call_target="tpu_custom_call" | custom-call | tf_op jit(solution)/shard_map/pallas_call | solution.py:486
  (1 shorter events, 0.0 us)
Async XLA Ops:
  0.6 2.8 %copy-start = (bf16[3,512,1024]{2,1,0:T(8,128)(2,1)S(1)}, bf16[3,512,1024]{2,1,0:T(8,128)(2,1)}, u32[]{:S(2)}) copy-start(bf16[3,512,1024]{2,1,0:T(8,128)(2,1)} %x_ref.7) | copy-start | bytes 9437188
  8.8 33.6 %collective-permute-start = (bf16[272,1024]{1,0:T(8,128)(2,1)S(1)}, bf16[272,1024]{1,0:T(8,128)(2,1)S(1)}, u32[]{:S(2)}, u32[]{:S(2)}) collective-permute-start(bf16[272,1024]{1,0:T(8,128)(2,1)S(1)} %get-tuple-element.31), channel_id=1, source_target_pairs={{0,4},{4,8},{8,12},{12,16},{16,20},{20,24},{24,28},{28,0},{1,5},{5... | collective-permute-start | bytes 1671176 | tf_op jit(solution)/shard_map/ppermute | solution.py:459
  9.3 13.4 %collective-permute-start.1 = (bf16[152,1024]{1,0:T(8,128)(2,1)S(1)}, bf16[152,1024]{1,0:T(8,128)(2,1)S(1)}, u32[]{:S(2)}, u32[]{:S(2)}) collective-permute-start(bf16[152,1024]{1,0:T(8,128)(2,1)S(1)} %get-tuple-element.32), channel_id=1, source_target_pairs={{0,4},{4,8},{8,12},{12,16},{16,20},{20,24},{24,28},{28,0},{1,5},{5... | collective-permute-start | bytes 933896 | tf_op jit(solution)/shard_map/ppermute | solution.py:459
  24.8 6.7 %collective-permute-start.2 = (f32[8,128]{1,0:T(8,128)S(1)}, f32[8,128]{1,0:T(8,128)S(1)}, u32[]{:S(2)}, u32[]{:S(2)}) collective-permute-start(f32[8,128]{1,0:T(8,128)S(1)} %get-tuple-element.40.refs_0_), channel_id=1, source_target_pairs={{0,1},{1,0},{2,3},{3,2},{4,5},{5,4},{6,7},{7,6},{8,9},{9,8},{10,11... | collective-permute-start | bytes 12296 | tf_op jit(solution)/shard_map/ppermute | solution.py:464
  27.2 4.5 %collective-permute-start.3 = (f32[8,128]{1,0:T(8,128)S(1)}, f32[8,128]{1,0:T(8,128)S(1)}, u32[]{:S(2)}, u32[]{:S(2)}) collective-permute-start(f32[8,128]{1,0:T(8,128)S(1)} %get-tuple-element.40.refs_0_), channel_id=1, source_target_pairs={{0,2},{1,3},{2,0},{3,1},{4,6},{5,7},{6,4},{7,5},{8,10},{9,11},{10,... | collective-permute-start | bytes 12296 | tf_op jit(solution)/shard_map/ppermute | solution.py:464
  29.8 5.4 %collective-permute-start.4 = (f32[8,128]{1,0:T(8,128)S(1)}, f32[8,128]{1,0:T(8,128)S(1)}, u32[]{:S(2)}, u32[]{:S(2)}) collective-permute-start(f32[8,128]{1,0:T(8,128)S(1)} %get-tuple-element.40.refs_0_), channel_id=1, source_target_pairs={{0,3},{1,2},{2,1},{3,0},{4,7},{5,6},{6,5},{7,4},{8,11},{9,10},{10,... | collective-permute-start | bytes 12296 | tf_op jit(solution)/shard_map/ppermute | solution.py:464
  43.7 1.4 %collective-permute-start.5 = (f32[32,1024]{1,0:T(8,128)S(1)}, f32[32,1024]{1,0:T(8,128)S(1)}, u32[]{:S(2)}, u32[]{:S(2)}) collective-permute-start(f32[32,1024]{1,0:T(8,128)S(1)} %shard_map.81), channel_id=1, source_target_pairs={{0,4},{4,0},{8,12},{12,8},{16,20},{20,16},{24,28},{28,24},{1,5},{5... | collective-permute-start | bytes 393224 | tf_op jit(solution)/shard_map/ppermute | solution.py:464
  45.1 4.3 %collective-permute-start.6 = (bf16[32,1024]{1,0:T(8,128)(2,1)S(1)}, bf16[32,1024]{1,0:T(8,128)(2,1)S(1)}, u32[]{:S(2)}, u32[]{:S(2)}) collective-permute-start(bf16[32,1024]{1,0:T(8,128)(2,1)S(1)} %add_convert_fusion.refs_0_), channel_id=1, source_target_pairs={{0,8},{4,12},{8,0},{12,4},{16,24},{20,28},{24,16},{28,20},{1,9},{5... | collective-permute-start | bytes 196616 | tf_op jit(solution)/shard_map/ppermute | solution.py:464
  45.8 4.3 %collective-permute-start.7 = (bf16[32,1024]{1,0:T(8,128)(2,1)S(1)}, bf16[32,1024]{1,0:T(8,128)(2,1)S(1)}, u32[]{:S(2)}, u32[]{:S(2)}) collective-permute-start(bf16[32,1024]{1,0:T(8,128)(2,1)S(1)} %add_convert_fusion.refs_0_), channel_id=1, source_target_pairs={{0,16},{4,20},{8,24},{12,28},{16,0},{20,4},{24,8},{28,12},{1,17},{... | collective-permute-start | bytes 196616 | tf_op jit(solution)/shard_map/ppermute | solution.py:464
  47.3 5.2 %collective-permute-start.8 = (bf16[32,1024]{1,0:T(8,128)(2,1)S(1)}, bf16[32,1024]{1,0:T(8,128)(2,1)S(1)}, u32[]{:S(2)}, u32[]{:S(2)}) collective-permute-start(bf16[32,1024]{1,0:T(8,128)(2,1)S(1)} %add_convert_fusion.refs_0_), channel_id=1, source_target_pairs={{0,24},{4,28},{8,16},{12,20},{16,8},{20,12},{24,0},{28,4},{1,25},{... | collective-permute-start | bytes 196616 | tf_op jit(solution)/shard_map/ppermute | solution.py:464

commit v7 on v6

--- a/solution.py
+++ b/solution.py
@@ -155,7 +155,7 @@
 def middle_kernel(
     near_ref, x_ref, taps_ref, skt_ref, kv_ref, q0_ref, pt_ref, qt_ref, ct_ref, w_ref,
     kve_ref, pta_ref, qta_ref, inner_ref, stats_ref,
-    buf, acc,
+    bufs, acc,
 ):
     channels = near_ref.shape[1]
     block = q0_ref.shape[0]
@@ -166,7 +166,7 @@
     chunks = channels // LANES
     acc[...] = jnp.zeros_like(acc)
 
-    def heads(chunk):
+    def heads(chunk, buf):
         lane = pl.ds(pl.multiple_of(chunk * LANES, LANES), LANES)
         group_at = pl.ds(pl.multiple_of(chunk * groups, groups), groups)
         for part in range(3):
@@ -210,14 +210,19 @@
                 place = slice(number * 8, number * 8 + 8)
                 acc[which, place, :] += sums[which][number]
 
-    heads(0)
-
-    @pl.loop(1, chunks)
-    def _(chunk):
-        filters(chunk - 1)
-        heads(chunk)
-
-    filters(chunks - 1)
+    at_once = math.gcd(chunks, bufs.shape[0])
+    for number in range(at_once):
+        heads(number, bufs.at[number])
+
+    @pl.loop(1, chunks // at_once)
+    def _(turn):
+        for number in range(at_once):
+            filters((turn - 1) * at_once + number)
+        for number in range(at_once):
+            heads(turn * at_once + number, bufs.at[number])
+
+    for number in range(at_once):
+        filters(chunks - at_once + number)
     for which in range(2):
         for number in range(blocks):
             at = which * blocks + number
@@ -555,7 +560,7 @@
             sds((2 * blocks, block), F32),
         ],
         [
-            pltpu.VMEM((parts, HALO + EDGE, LANES), F32),
+            pltpu.VMEM((2, parts, HALO + EDGE, LANES), F32),
             pltpu.VMEM((2, 8 * blocks, block), F32),
         ],
         (near, projected, taps_major, skt, kv, q0, pt, qt, ct, w),

time: 53.3 us -> 53.1 us (level)
  no operation moved by 1% of the time
where the time goes in v7:
time: 53.1 us; the launch traced here: 52.9 us
  Pallas kernels  20 us (38%)
  waiting for transfers between devices  19.6 us (37%)
  starting transfers between devices  11.7 us (22%)
  local copies, waits for them, and re-layouts  0.84 us (2%)
  between operations  0.72 us (1%)
    pallas_call x7, Pallas kernels, on_chip(): pl.pallas_call(kernel, in_specs=[apart if number in outside else place fo...  20 us
    ppermute x2, waiting for transfers between devices, ring(): lax.ppermute(array, axis, [(i, (i + 1) % length) for i in range(length)])  10.8 us
    ppermute x7, waiting for transfers between devices, crossed(): return lax.ppermute(array, axis, [(i, i ^ bit) for i in range(length)])  8.81 us
    ppermute x7, starting transfers between devices, crossed(): return lax.ppermute(array, axis, [(i, i ^ bit) for i in range(length)])  8.61 us
    ppermute x2, starting transfers between devices, ring(): lax.ppermute(array, axis, [(i, (i + 1) % length) for i in range(length)])  3.13 us
  transfers between devices with their start and end apart: 9, of which 7 were waited for; matrix products, arithmetic and copies ran while one was open for 0% of the time, Pallas kernels for 20%

profile of v7, /device:TPU:0, one launch (start us, length us, event | category | flops | bytes accessed | tf_op | source)
XLA Modules:
  0.0 52.9 jit_solution(1201665034168849861)
XLA Ops:
  0.6 0.0 copy-start
  0.6 0.8 %reshape.12.skip_ref = bf16[1,1024]{1,0:T(2,128)(2,1)S(1)} reshape(bf16[1024]{0:T(1024)(128)(2,1)} %param.8) | data formatting | bytes 4096 | tf_op jit(solution)/shard_map/reshape | solution.py:511
  1.5 1.9 %shard_map.76 = (bf16[152,1024]{1,0:T(8,128)(2,1)S(1)}, bf16[3,7,1024]{2,1,0:T(8,128)(2,1)S(1)}, bf16[64,128]{1,0:T(8,128)(2,1)S(1)}, bf16[512,1024]{1,0:T(8,128)(2,1)S(1)}) custom-call(bf16[3,512,1024]{2,1,0:T(8,128)(2,1)} %x_ref.7, bf16[3,7,1024]{2,1,0:T(8,128)(2,1)} %bitcast.3, bf16[64,128]{1,0:T(8,128)(2,1)} %filt_hbm.1, bf16[512,1024]{1,0:T(8,128)(2,1)} %cot_hbm.1), custom_call_target="tpu_custom_call" | custom-call | tf_op jit(solution)/shard_map/pallas_call | solution.py:491
  3.4 0.0 copy-done
  3.4 5.3 %shard_map.77 = (bf16[272,1024]{1,0:T(8,128)(2,1)S(1)}, f32[64,16,128]{2,1,0:T(8,128)S(1)}, bf16[8,2,512,128]{3,2,1,0:T(8,128)(2,1)S(1)}, bf16[128,1024]{1,0:T(8...) custom-call(bf16[3,512,1024]{2,1,0:T(8,128)(2,1)S(1)} %copy-done, ...), custom_call_target="tpu_custom_call" | custom-call | tf_op jit(solution)/shard_map/pallas_call | solution.py:491
  8.8 0.5 %collective-permute-start = (bf16[272,1024]{1,0:T(8,128)(2,1)S(1)}, bf16[272,1024]{1,0:T(8,128)(2,1)S(1)}, u32[]{:S(2)}, u32[]{:S(2)}) collective-permute-start(bf16[272,1024]{1,0:T(8,128)(2,1)S(1)} %get-tuple-element.31), channel_id=1, source_target_pairs={{0,4},{4,8},{8,12},{12,16},{16,20},{20,24},{24,28},{28,0},{1,5},{5... | collective-permute-start | bytes 1671176 | tf_op jit(solution)/shard_map/ppermute | solution.py:464
  9.3 2.6 %collective-permute-start.1 = (bf16[152,1024]{1,0:T(8,128)(2,1)S(1)}, bf16[152,1024]{1,0:T(8,128)(2,1)S(1)}, u32[]{:S(2)}, u32[]{:S(2)}) collective-permute-start(bf16[152,1024]{1,0:T(8,128)(2,1)S(1)} %get-tuple-element.32), channel_id=1, source_target_pairs={{0,4},{4,8},{8,12},{12,16},{16,20},{20,24},{24,28},{28,0},{1,5},{5... | collective-permute-start | bytes 933896 | tf_op jit(solution)/shard_map/ppermute | solution.py:464
  11.9 10.8 %collective-permute-done.1.near_ref = bf16[152,1024]{1,0:T(8,128)(2,1)S(1)} collective-permute-done((bf16[152,1024]{1,0:T(8,128)(2,1)S(1)}, bf16[152,1024]{1,0:T(8,128)(2,1)S(1)}, u32[]{:S(2)}, u32[]{:S(2)}) %collective-permute-start.1) | collective-permute-done | bytes 311328 | tf_op jit(solution)/shard_map/ppermute | solution.py:464
  22.7 1.9 %shard_map.78 = (bf16[8,2,16,128]{3,2,1,0:T(8,128)(2,1)S(1)}, bf16[64,32,128]{2,1,0:T(8,128)(2,1)S(1)}, bf16[64,16,128]{2,1,0:T(8,128)(2,1)S(1)}, f32[64,64,128]{2,1,0:T(8,128)S(1)}, f32[8,128]{1,0:T(8,128)S(1)}) custom-call(bf16[152,1024]{1,0:T(8,128)(2,1)S(1)} %collective-permute-done.1.near_ref, bf16[3,512,1024]{2,1,0:T(8,128)(2,1)S(1)} %copy-done, ...), custom_call_target="tpu_custom_call" | custom-call | tf_op jit(solution)/shard_map/pallas_call | solution.py:491
  24.6 2.4 %collective-permute-start.2 = (f32[8,128]{1,0:T(8,128)S(1)}, f32[8,128]{1,0:T(8,128)S(1)}, u32[]{:S(2)}, u32[]{:S(2)}) collective-permute-start(f32[8,128]{1,0:T(8,128)S(1)} %get-tuple-element.40.refs_0_), channel_id=1, source_target_pairs={{0,1},{1,0},{2,3},{3,2},{4,5},{5,4},{6,7},{7,6},{8,9},{9,8},{10,11... | collective-permute-start | bytes 12296 | tf_op jit(solution)/shard_map/ppermute | solution.py:469
  27.0 2.6 %collective-permute-start.3 = (f32[8,128]{1,0:T(8,128)S(1)}, f32[8,128]{1,0:T(8,128)S(1)}, u32[]{:S(2)}, u32[]{:S(2)}) collective-permute-start(f32[8,128]{1,0:T(8,128)S(1)} %get-tuple-element.40.refs_0_), channel_id=1, source_target_pairs={{0,2},{1,3},{2,0},{3,1},{4,6},{5,7},{6,4},{7,5},{8,10},{9,11},{10,... | collective-permute-start | bytes 12296 | tf_op jit(solution)/shard_map/ppermute | solution.py:469
  29.6 0.0 collective-permute-start.4
  29.6 1.7 %shard_map.79 = (f32[8,4,2,136,128]{4,3,2,1,0:T(8,128)S(1)}, f32[8,4,2,128,128]{4,3,2,1,0:T(8,128)S(1)}, bf16[8,7,512,128]{3,2,1,0:T(8,128)(2,1)S(1)}) custom-call(bf16[152,1024]{1,0:T(8,128)(2,1)S(1)} %collective-permute-done.1.near_ref, bf16[3,512,1024]{2,1,0:T(8,128)(2,1)S(1)} %copy-done, bf16[8,2,512,128]{3,2,1,0:T(8,128)(2,1)S(1)} %get-tuple-element.34.kv_ref, ...), custom_call_target="tpu_custom_call" | custom-call | tf_op jit(solution)/shard_map/pallas_call | solution.py:491
  31.3 0.0 collective-permute-done.2.refs_1_
  31.3 0.2 collective-permute-done.3.refs_2_
  31.5 3.5 %collective-permute-done.4.refs_3_ = f32[8,128]{1,0:T(8,128)S(1)} collective-permute-done((f32[8,128]{1,0:T(8,128)S(1)}, f32[8,128]{1,0:T(8,128)S(1)}, u32[]{:S(2)}, u32[]{:S(2)}) %collective-permute-start.4) | collective-permute-done | bytes 4128 | tf_op jit(solution)/shard_map/ppermute | solution.py:469
  35.0 7.1 %shard_map.80 = (f32[32,1024]{1,0:T(8,128)S(1)}, f32[64,16,128]{2,1,0:T(8,128)S(1)}) custom-call(f32[8,128]{1,0:T(8,128)S(1)} %get-tuple-element.40.refs_0_, f32[8,128]{1,0:T(8,128)S(1)} %collective-permute-done.2.refs_1_, f32[8,128]{1,0:T(8,128)S(1)} %collective-permute-done.3.refs_2_, f32[8,128]{1,0:T(8,128)S(1)} %collective-permute-done.4.refs_3_, ...), custom_call_target="tpu_custom_call" | custom-call | tf_op jit(solution)/shard_map/pallas_call | solution.py:491
  42.1 0.0 collective-permute-done.far_ref
  42.1 1.4 %shard_map.81 = f32[32,1024]{1,0:T(8,128)S(1)} custom-call(bf16[272,1024]{1,0:T(8,128)(2,1)S(1)} %collective-permute-done.far_ref, bf16[3,7,1024]{2,1,0:T(8,128)(2,1)S(1)} %get-tuple-element.28.taps_ref, f32[64,16,128]{2,1,0:T(8,128)S(1)} %get-tuple-element.48.pgr_ref, f32[32,1024]{1,0:T(8,128)S(1)} %get-tuple-element.49.out_ref), custom_call_target="tpu_custom_call" | custom-call | tf_op jit(solution)/shard_map/pallas_call | solution.py:491
  43.5 0.1 collective-permute-start.5
  43.6 1.3 %collective-permute-done.5 = f32[32,1024]{1,0:T(8,128)S(1)} collective-permute-done((f32[32,1024]{1,0:T(8,128)S(1)}, f32[32,1024]{1,0:T(8,128)S(1)}, u32[]{:S(2)}, u32[]{:S(2)}) %collective-permute-start.5) | collective-permute-done | bytes 131104 | tf_op jit(solution)/shard_map/ppermute | solution.py:469
  44.9 0.6 %collective-permute-start.6 = (bf16[32,1024]{1,0:T(8,128)(2,1)S(1)}, bf16[32,1024]{1,0:T(8,128)(2,1)S(1)}, u32[]{:S(2)}, u32[]{:S(2)}) collective-permute-start(bf16[32,1024]{1,0:T(8,128)(2,1)S(1)} %add_convert_fusion.refs_0_), channel_id=1, source_target_pairs={{0,8},{4,12},{8,0},{12,4},{16,24},{20,28},{24,16},{28,20},{1,9},{5... | collective-permute-start | bytes 196616 | tf_op jit(solution)/shard_map/ppermute | solution.py:469
  45.6 1.5 %collective-permute-start.7 = (bf16[32,1024]{1,0:T(8,128)(2,1)S(1)}, bf16[32,1024]{1,0:T(8,128)(2,1)S(1)}, u32[]{:S(2)}, u32[]{:S(2)}) collective-permute-start(bf16[32,1024]{1,0:T(8,128)(2,1)S(1)} %add_convert_fusion.refs_0_), channel_id=1, source_target_pairs={{0,16},{4,20},{8,24},{12,28},{16,0},{20,4},{24,8},{28,12},{1,17},{... | collective-permute-start | bytes 196616 | tf_op jit(solution)/shard_map/ppermute | solution.py:469
  47.1 1.4 %collective-permute-start.8 = (bf16[32,1024]{1,0:T(8,128)(2,1)S(1)}, bf16[32,1024]{1,0:T(8,128)(2,1)S(1)}, u32[]{:S(2)}, u32[]{:S(2)}) collective-permute-start(bf16[32,1024]{1,0:T(8,128)(2,1)S(1)} %add_convert_fusion.refs_0_), channel_id=1, source_target_pairs={{0,24},{4,28},{8,16},{12,20},{16,8},{20,12},{24,0},{28,4},{1,25},{... | collective-permute-start | bytes 196616 | tf_op jit(solution)/shard_map/ppermute | solution.py:469
  48.5 0.8 %collective-permute-done.6.refs_1_ = bf16[32,1024]{1,0:T(8,128)(2,1)S(1)} collective-permute-done((bf16[32,1024]{1,0:T(8,128)(2,1)S(1)}, bf16[32,1024]{1,0:T(8,128)(2,1)S(1)}, u32[]{:S(2)}, u32[]{:S(2)}) %collective-permute-start.6) | collective-permute-done | bytes 65568 | tf_op jit(solution)/shard_map/ppermute | solution.py:469
  49.3 0.5 %collective-permute-done.7.refs_2_ = bf16[32,1024]{1,0:T(8,128)(2,1)S(1)} collective-permute-done((bf16[32,1024]{1,0:T(8,128)(2,1)S(1)}, bf16[32,1024]{1,0:T(8,128)(2,1)S(1)}, u32[]{:S(2)}, u32[]{:S(2)}) %collective-permute-start.7) | collective-permute-done | bytes 65568 | tf_op jit(solution)/shard_map/ppermute | solution.py:469
  49.8 2.4 %collective-permute-done.8.refs_3_ = bf16[32,1024]{1,0:T(8,128)(2,1)S(1)} collective-permute-done((bf16[32,1024]{1,0:T(8,128)(2,1)S(1)}, bf16[32,1024]{1,0:T(8,128)(2,1)S(1)}, u32[]{:S(2)}, u32[]{:S(2)}) %collective-permute-start.8) | collective-permute-done | bytes 65568 | tf_op jit(solution)/shard_map/ppermute | solution.py:469
  52.3 0.7 %shard_map.82 = (f32[3,7,1024]{2,1,0:T(8,128)}, f32[64,128]{1,0:T(8,128)}, f32[1,1024]{1,0:T(1,128)}) custom-call(bf16[32,1024]{1,0:T(8,128)(2,1)S(1)} %add_convert_fusion.refs_0_, bf16[32,1024]{1,0:T(8,128)(2,1)S(1)} %collective-permute-done.6.refs_1_, bf16[32,1024]{1,0:T(8,128)(2,1)S(1)} %collective-permute-done.7.refs_2_, ...), custom_call_target="tpu_custom_call" | custom-call | tf_op jit(solution)/shard_map/pallas_call | solution.py:491
  (1 shorter events, 0.0 us)
Async XLA Ops:
  0.6 2.8 %copy-start = (bf16[3,512,1024]{2,1,0:T(8,128)(2,1)S(1)}, bf16[3,512,1024]{2,1,0:T(8,128)(2,1)}, u32[]{:S(2)}) copy-start(bf16[3,512,1024]{2,1,0:T(8,128)(2,1)} %x_ref.7) | copy-start | bytes 9437188
  8.8 33.3 %collective-permute-start = (bf16[272,1024]{1,0:T(8,128)(2,1)S(1)}, bf16[272,1024]{1,0:T(8,128)(2,1)S(1)}, u32[]{:S(2)}, u32[]{:S(2)}) collective-permute-start(bf16[272,1024]{1,0:T(8,128)(2,1)S(1)} %get-tuple-element.31), channel_id=1, source_target_pairs={{0,4},{4,8},{8,12},{12,16},{16,20},{20,24},{24,28},{28,0},{1,5},{5... | collective-permute-start | bytes 1671176 | tf_op jit(solution)/shard_map/ppermute | solution.py:464
  9.3 13.4 %collective-permute-start.1 = (bf16[152,1024]{1,0:T(8,128)(2,1)S(1)}, bf16[152,1024]{1,0:T(8,128)(2,1)S(1)}, u32[]{:S(2)}, u32[]{:S(2)}) collective-permute-start(bf16[152,1024]{1,0:T(8,128)(2,1)S(1)} %get-tuple-element.32), channel_id=1, source_target_pairs={{0,4},{4,8},{8,12},{12,16},{16,20},{20,24},{24,28},{28,0},{1,5},{5... | collective-permute-start | bytes 933896 | tf_op jit(solution)/shard_map/ppermute | solution.py:464
  24.6 6.7 %collective-permute-start.2 = (f32[8,128]{1,0:T(8,128)S(1)}, f32[8,128]{1,0:T(8,128)S(1)}, u32[]{:S(2)}, u32[]{:S(2)}) collective-permute-start(f32[8,128]{1,0:T(8,128)S(1)} %get-tuple-element.40.refs_0_), channel_id=1, source_target_pairs={{0,1},{1,0},{2,3},{3,2},{4,5},{5,4},{6,7},{7,6},{8,9},{9,8},{10,11... | collective-permute-start | bytes 12296 | tf_op jit(solution)/shard_map/ppermute | solution.py:469
  27.0 4.5 %collective-permute-start.3 = (f32[8,128]{1,0:T(8,128)S(1)}, f32[8,128]{1,0:T(8,128)S(1)}, u32[]{:S(2)}, u32[]{:S(2)}) collective-permute-start(f32[8,128]{1,0:T(8,128)S(1)} %get-tuple-element.40.refs_0_), channel_id=1, source_target_pairs={{0,2},{1,3},{2,0},{3,1},{4,6},{5,7},{6,4},{7,5},{8,10},{9,11},{10,... | collective-permute-start | bytes 12296 | tf_op jit(solution)/shard_map/ppermute | solution.py:469
  29.6 5.4 %collective-permute-start.4 = (f32[8,128]{1,0:T(8,128)S(1)}, f32[8,128]{1,0:T(8,128)S(1)}, u32[]{:S(2)}, u32[]{:S(2)}) collective-permute-start(f32[8,128]{1,0:T(8,128)S(1)} %get-tuple-element.40.refs_0_), channel_id=1, source_target_pairs={{0,3},{1,2},{2,1},{3,0},{4,7},{5,6},{6,5},{7,4},{8,11},{9,10},{10,... | collective-permute-start | bytes 12296 | tf_op jit(solution)/shard_map/ppermute | solution.py:469
  43.5 1.4 %collective-permute-start.5 = (f32[32,1024]{1,0:T(8,128)S(1)}, f32[32,1024]{1,0:T(8,128)S(1)}, u32[]{:S(2)}, u32[]{:S(2)}) collective-permute-start(f32[32,1024]{1,0:T(8,128)S(1)} %shard_map.81), channel_id=1, source_target_pairs={{0,4},{4,0},{8,12},{12,8},{16,20},{20,16},{24,28},{28,24},{1,5},{5... | collective-permute-start | bytes 393224 | tf_op jit(solution)/shard_map/ppermute | solution.py:469
  44.9 4.4 %collective-permute-start.6 = (bf16[32,1024]{1,0:T(8,128)(2,1)S(1)}, bf16[32,1024]{1,0:T(8,128)(2,1)S(1)}, u32[]{:S(2)}, u32[]{:S(2)}) collective-permute-start(bf16[32,1024]{1,0:T(8,128)(2,1)S(1)} %add_convert_fusion.refs_0_), channel_id=1, source_target_pairs={{0,8},{4,12},{8,0},{12,4},{16,24},{20,28},{24,16},{28,20},{1,9},{5... | collective-permute-start | bytes 196616 | tf_op jit(solution)/shard_map/ppermute | solution.py:469
  45.6 4.3 %collective-permute-start.7 = (bf16[32,1024]{1,0:T(8,128)(2,1)S(1)}, bf16[32,1024]{1,0:T(8,128)(2,1)S(1)}, u32[]{:S(2)}, u32[]{:S(2)}) collective-permute-start(bf16[32,1024]{1,0:T(8,128)(2,1)S(1)} %add_convert_fusion.refs_0_), channel_id=1, source_target_pairs={{0,16},{4,20},{8,24},{12,28},{16,0},{20,4},{24,8},{28,12},{1,17},{... | collective-permute-start | bytes 196616 | tf_op jit(solution)/shard_map/ppermute | solution.py:469
  47.1 5.2 %collective-permute-start.8 = (bf16[32,1024]{1,0:T(8,128)(2,1)S(1)}, bf16[32,1024]{1,0:T(8,128)(2,1)S(1)}, u32[]{:S(2)}, u32[]{:S(2)}) collective-permute-start(bf16[32,1024]{1,0:T(8,128)(2,1)S(1)} %add_convert_fusion.refs_0_), channel_id=1, source_target_pairs={{0,24},{4,28},{8,16},{12,20},{16,8},{20,12},{24,0},{28,4},{1,25},{... | collective-permute-start | bytes 196616 | tf_op jit(solution)/shard_map/ppermute | solution.py:469

commit v8 on v7

--- a/solution.py
+++ b/solution.py
@@ -412,10 +412,15 @@
         braid(group_steps(1, 1), query_steps(0, 0))
         turn(0)
 
-        @pl.loop(1, chunks // 2)
-        def _(pair):
-            whole_step(2 * pair, 0)
-            whole_step(2 * pair + 1, 1)
+        pairs = chunks // 2 - 1
+        at_once = 3 if pairs % 3 == 0 else 1
+
+        @pl.loop(0, pairs // at_once)
+        def _(turn):
+            for number in range(at_once):
+                pair = 1 + turn * at_once + number
+                whole_step(2 * pair, 0)
+                whole_step(2 * pair + 1, 1)
 
         if chunks % 2:
             whole_step(chunks - 1, 0)
@@ -560,7 +565,7 @@
             sds((2 * blocks, block), F32),
         ],
         [
-            pltpu.VMEM((2, parts, HALO + EDGE, LANES), F32),
+            pltpu.VMEM((4, parts, HALO + EDGE, LANES), F32),
             pltpu.VMEM((2, 8 * blocks, block), F32),
         ],
         (near, projected, taps_major, skt, kv, q0, pt, qt, ct, w),

time: 53.1 us -> 52 us (0.979)
  Pallas kernels: 20 us -> 18.8 us
    pallas_call x7, Pallas kernels: 20 us -> 18.8 us  [on_chip(): pl.pallas_call(kernel, in_specs=[apart if number in outside else place fo...]
  transfers between devices with their start and end apart: 9 -> 9, of which waited for: 7 -> 7; matrix products, arithmetic and copies ran while one was open for 0% -> 0% of each run, Pallas kernels for 20% -> 18%
where the time goes in v8:
time: 52 us; the launch traced here: 51.8 us
  waiting for transfers between devices  19.6 us (38%)
  Pallas kernels  18.8 us (36%)
  starting transfers between devices  11.7 us (22%)
  local copies, waits for them, and re-layouts  0.84 us (2%)
  between operations  0.71 us (1%)
    pallas_call x7, Pallas kernels, on_chip(): pl.pallas_call(kernel, in_specs=[apart if number in outside else place fo...  18.8 us
    ppermute x2, waiting for transfers between devices, ring(): lax.ppermute(array, axis, [(i, (i + 1) % length) for i in range(length)])  10.8 us
    ppermute x7, waiting for transfers between devices, crossed(): return lax.ppermute(array, axis, [(i, i ^ bit) for i in range(length)])  8.8 us
    ppermute x7, starting transfers between devices, crossed(): return lax.ppermute(array, axis, [(i, i ^ bit) for i in range(length)])  8.61 us
    ppermute x2, starting transfers between devices, ring(): lax.ppermute(array, axis, [(i, (i + 1) % length) for i in range(length)])  3.13 us
  transfers between devices with their start and end apart: 9, of which 7 were waited for; matrix products, arithmetic and copies ran while one was open for 0% of the time, Pallas kernels for 18%

profile of v8, /device:TPU:0, one launch (start us, length us, event | category | flops | bytes accessed | tf_op | source)
XLA Modules:
  0.0 51.8 jit_solution(11715488608042250599)
XLA Ops:
  0.6 0.0 copy-start
  0.6 0.8 %reshape.12.skip_ref = bf16[1,1024]{1,0:T(2,128)(2,1)S(1)} reshape(bf16[1024]{0:T(1024)(128)(2,1)} %param.8) | data formatting | bytes 4096 | tf_op jit(solution)/shard_map/reshape | solution.py:516
  1.5 1.9 %shard_map.76 = (bf16[152,1024]{1,0:T(8,128)(2,1)S(1)}, bf16[3,7,1024]{2,1,0:T(8,128)(2,1)S(1)}, bf16[64,128]{1,0:T(8,128)(2,1)S(1)}, bf16[512,1024]{1,0:T(8,128)(2,1)S(1)}) custom-call(bf16[3,512,1024]{2,1,0:T(8,128)(2,1)} %x_ref.7, bf16[3,7,1024]{2,1,0:T(8,128)(2,1)} %bitcast.3, bf16[64,128]{1,0:T(8,128)(2,1)} %filt_hbm.1, bf16[512,1024]{1,0:T(8,128)(2,1)} %cot_hbm.1), custom_call_target="tpu_custom_call" | custom-call | tf_op jit(solution)/shard_map/pallas_call | solution.py:496
  3.4 0.0 copy-done
  3.4 5.3 %shard_map.77 = (bf16[272,1024]{1,0:T(8,128)(2,1)S(1)}, f32[64,16,128]{2,1,0:T(8,128)S(1)}, bf16[8,2,512,128]{3,2,1,0:T(8,128)(2,1)S(1)}, bf16[128,1024]{1,0:T(8...) custom-call(bf16[3,512,1024]{2,1,0:T(8,128)(2,1)S(1)} %copy-done, ...), custom_call_target="tpu_custom_call" | custom-call | tf_op jit(solution)/shard_map/pallas_call | solution.py:496
  8.8 0.5 %collective-permute-start = (bf16[272,1024]{1,0:T(8,128)(2,1)S(1)}, bf16[272,1024]{1,0:T(8,128)(2,1)S(1)}, u32[]{:S(2)}, u32[]{:S(2)}) collective-permute-start(bf16[272,1024]{1,0:T(8,128)(2,1)S(1)} %get-tuple-element.31), channel_id=1, source_target_pairs={{0,4},{4,8},{8,12},{12,16},{16,20},{20,24},{24,28},{28,0},{1,5},{5... | collective-permute-start | bytes 1671176 | tf_op jit(solution)/shard_map/ppermute | solution.py:469
  9.3 2.6 %collective-permute-start.1 = (bf16[152,1024]{1,0:T(8,128)(2,1)S(1)}, bf16[152,1024]{1,0:T(8,128)(2,1)S(1)}, u32[]{:S(2)}, u32[]{:S(2)}) collective-permute-start(bf16[152,1024]{1,0:T(8,128)(2,1)S(1)} %get-tuple-element.32), channel_id=1, source_target_pairs={{0,4},{4,8},{8,12},{12,16},{16,20},{20,24},{24,28},{28,0},{1,5},{5... | collective-permute-start | bytes 933896 | tf_op jit(solution)/shard_map/ppermute | solution.py:469
  11.9 10.8 %collective-permute-done.1.near_ref = bf16[152,1024]{1,0:T(8,128)(2,1)S(1)} collective-permute-done((bf16[152,1024]{1,0:T(8,128)(2,1)S(1)}, bf16[152,1024]{1,0:T(8,128)(2,1)S(1)}, u32[]{:S(2)}, u32[]{:S(2)}) %collective-permute-start.1) | collective-permute-done | bytes 311328 | tf_op jit(solution)/shard_map/ppermute | solution.py:469
  22.7 1.3 %shard_map.78 = (bf16[8,2,16,128]{3,2,1,0:T(8,128)(2,1)S(1)}, bf16[64,32,128]{2,1,0:T(8,128)(2,1)S(1)}, bf16[64,16,128]{2,1,0:T(8,128)(2,1)S(1)}, f32[64,64,128]{2,1,0:T(8,128)S(1)}, f32[8,128]{1,0:T(8,128)S(1)}) custom-call(bf16[152,1024]{1,0:T(8,128)(2,1)S(1)} %collective-permute-done.1.near_ref, bf16[3,512,1024]{2,1,0:T(8,128)(2,1)S(1)} %copy-done, ...), custom_call_target="tpu_custom_call" | custom-call | tf_op jit(solution)/shard_map/pallas_call | solution.py:496
  24.1 2.4 %collective-permute-start.2 = (f32[8,128]{1,0:T(8,128)S(1)}, f32[8,128]{1,0:T(8,128)S(1)}, u32[]{:S(2)}, u32[]{:S(2)}) collective-permute-start(f32[8,128]{1,0:T(8,128)S(1)} %get-tuple-element.40.refs_0_), channel_id=1, source_target_pairs={{0,1},{1,0},{2,3},{3,2},{4,5},{5,4},{6,7},{7,6},{8,9},{9,8},{10,11... | collective-permute-start | bytes 12296 | tf_op jit(solution)/shard_map/ppermute | solution.py:474
  26.5 2.6 %collective-permute-start.3 = (f32[8,128]{1,0:T(8,128)S(1)}, f32[8,128]{1,0:T(8,128)S(1)}, u32[]{:S(2)}, u32[]{:S(2)}) collective-permute-start(f32[8,128]{1,0:T(8,128)S(1)} %get-tuple-element.40.refs_0_), channel_id=1, source_target_pairs={{0,2},{1,3},{2,0},{3,1},{4,6},{5,7},{6,4},{7,5},{8,10},{9,11},{10,... | collective-permute-start | bytes 12296 | tf_op jit(solution)/shard_map/ppermute | solution.py:474
  29.0 0.0 collective-permute-start.4
  29.0 1.7 %shard_map.79 = (f32[8,4,2,136,128]{4,3,2,1,0:T(8,128)S(1)}, f32[8,4,2,128,128]{4,3,2,1,0:T(8,128)S(1)}, bf16[8,7,512,128]{3,2,1,0:T(8,128)(2,1)S(1)}) custom-call(bf16[152,1024]{1,0:T(8,128)(2,1)S(1)} %collective-permute-done.1.near_ref, bf16[3,512,1024]{2,1,0:T(8,128)(2,1)S(1)} %copy-done, bf16[8,2,512,128]{3,2,1,0:T(8,128)(2,1)S(1)} %get-tuple-element.34.kv_ref, ...), custom_call_target="tpu_custom_call" | custom-call | tf_op jit(solution)/shard_map/pallas_call | solution.py:496
  30.8 0.0 collective-permute-done.2.refs_1_
  30.8 0.2 collective-permute-done.3.refs_2_
  31.0 3.5 %collective-permute-done.4.refs_3_ = f32[8,128]{1,0:T(8,128)S(1)} collective-permute-done((f32[8,128]{1,0:T(8,128)S(1)}, f32[8,128]{1,0:T(8,128)S(1)}, u32[]{:S(2)}, u32[]{:S(2)}) %collective-permute-start.4) | collective-permute-done | bytes 4128 | tf_op jit(solution)/shard_map/ppermute | solution.py:474
  34.5 6.5 %shard_map.80 = (f32[32,1024]{1,0:T(8,128)S(1)}, f32[64,16,128]{2,1,0:T(8,128)S(1)}) custom-call(f32[8,128]{1,0:T(8,128)S(1)} %get-tuple-element.40.refs_0_, f32[8,128]{1,0:T(8,128)S(1)} %collective-permute-done.2.refs_1_, f32[8,128]{1,0:T(8,128)S(1)} %collective-permute-done.3.refs_2_, f32[8,128]{1,0:T(8,128)S(1)} %collective-permute-done.4.refs_3_, ...), custom_call_target="tpu_custom_call" | custom-call | tf_op jit(solution)/shard_map/pallas_call | solution.py:496
  40.9 0.0 collective-permute-done.far_ref
  41.0 1.4 %shard_map.81 = f32[32,1024]{1,0:T(8,128)S(1)} custom-call(bf16[272,1024]{1,0:T(8,128)(2,1)S(1)} %collective-permute-done.far_ref, bf16[3,7,1024]{2,1,0:T(8,128)(2,1)S(1)} %get-tuple-element.28.taps_ref, f32[64,16,128]{2,1,0:T(8,128)S(1)} %get-tuple-element.48.pgr_ref, f32[32,1024]{1,0:T(8,128)S(1)} %get-tuple-element.49.out_ref), custom_call_target="tpu_custom_call" | custom-call | tf_op jit(solution)/shard_map/pallas_call | solution.py:496
  42.3 0.1 collective-permute-start.5
  42.4 1.3 %collective-permute-done.5 = f32[32,1024]{1,0:T(8,128)S(1)} collective-permute-done((f32[32,1024]{1,0:T(8,128)S(1)}, f32[32,1024]{1,0:T(8,128)S(1)}, u32[]{:S(2)}, u32[]{:S(2)}) %collective-permute-start.5) | collective-permute-done | bytes 131104 | tf_op jit(solution)/shard_map/ppermute | solution.py:474
  43.8 0.7 %collective-permute-start.6 = (bf16[32,1024]{1,0:T(8,128)(2,1)S(1)}, bf16[32,1024]{1,0:T(8,128)(2,1)S(1)}, u32[]{:S(2)}, u32[]{:S(2)}) collective-permute-start(bf16[32,1024]{1,0:T(8,128)(2,1)S(1)} %add_convert_fusion.refs_0_), channel_id=1, source_target_pairs={{0,8},{4,12},{8,0},{12,4},{16,24},{20,28},{24,16},{28,20},{1,9},{5... | collective-permute-start | bytes 196616 | tf_op jit(solution)/shard_map/ppermute | solution.py:474
  44.4 1.5 %collective-permute-start.7 = (bf16[32,1024]{1,0:T(8,128)(2,1)S(1)}, bf16[32,1024]{1,0:T(8,128)(2,1)S(1)}, u32[]{:S(2)}, u32[]{:S(2)}) collective-permute-start(bf16[32,1024]{1,0:T(8,128)(2,1)S(1)} %add_convert_fusion.refs_0_), channel_id=1, source_target_pairs={{0,16},{4,20},{8,24},{12,28},{16,0},{20,4},{24,8},{28,12},{1,17},{... | collective-permute-start | bytes 196616 | tf_op jit(solution)/shard_map/ppermute | solution.py:474
  45.9 1.4 %collective-permute-start.8 = (bf16[32,1024]{1,0:T(8,128)(2,1)S(1)}, bf16[32,1024]{1,0:T(8,128)(2,1)S(1)}, u32[]{:S(2)}, u32[]{:S(2)}) collective-permute-start(bf16[32,1024]{1,0:T(8,128)(2,1)S(1)} %add_convert_fusion.refs_0_), channel_id=1, source_target_pairs={{0,24},{4,28},{8,16},{12,20},{16,8},{20,12},{24,0},{28,4},{1,25},{... | collective-permute-start | bytes 196616 | tf_op jit(solution)/shard_map/ppermute | solution.py:474
  47.3 0.8 %collective-permute-done.6.refs_1_ = bf16[32,1024]{1,0:T(8,128)(2,1)S(1)} collective-permute-done((bf16[32,1024]{1,0:T(8,128)(2,1)S(1)}, bf16[32,1024]{1,0:T(8,128)(2,1)S(1)}, u32[]{:S(2)}, u32[]{:S(2)}) %collective-permute-start.6) | collective-permute-done | bytes 65568 | tf_op jit(solution)/shard_map/ppermute | solution.py:474
  48.1 0.6 %collective-permute-done.7.refs_2_ = bf16[32,1024]{1,0:T(8,128)(2,1)S(1)} collective-permute-done((bf16[32,1024]{1,0:T(8,128)(2,1)S(1)}, bf16[32,1024]{1,0:T(8,128)(2,1)S(1)}, u32[]{:S(2)}, u32[]{:S(2)}) %collective-permute-start.7) | collective-permute-done | bytes 65568 | tf_op jit(solution)/shard_map/ppermute | solution.py:474
  48.7 2.4 %collective-permute-done.8.refs_3_ = bf16[32,1024]{1,0:T(8,128)(2,1)S(1)} collective-permute-done((bf16[32,1024]{1,0:T(8,128)(2,1)S(1)}, bf16[32,1024]{1,0:T(8,128)(2,1)S(1)}, u32[]{:S(2)}, u32[]{:S(2)}) %collective-permute-start.8) | collective-permute-done | bytes 65568 | tf_op jit(solution)/shard_map/ppermute | solution.py:474
  51.1 0.7 %shard_map.82 = (f32[3,7,1024]{2,1,0:T(8,128)}, f32[64,128]{1,0:T(8,128)}, f32[1,1024]{1,0:T(1,128)}) custom-call(bf16[32,1024]{1,0:T(8,128)(2,1)S(1)} %add_convert_fusion.refs_0_, bf16[32,1024]{1,0:T(8,128)(2,1)S(1)} %collective-permute-done.6.refs_1_, bf16[32,1024]{1,0:T(8,128)(2,1)S(1)} %collective-permute-done.7.refs_2_, ...), custom_call_target="tpu_custom_call" | custom-call | tf_op jit(solution)/shard_map/pallas_call | solution.py:496
  (1 shorter events, 0.0 us)
Async XLA Ops:
  0.6 2.8 %copy-start = (bf16[3,512,1024]{2,1,0:T(8,128)(2,1)S(1)}, bf16[3,512,1024]{2,1,0:T(8,128)(2,1)}, u32[]{:S(2)}) copy-start(bf16[3,512,1024]{2,1,0:T(8,128)(2,1)} %x_ref.7) | copy-start | bytes 9437188
  8.8 32.2 %collective-permute-start = (bf16[272,1024]{1,0:T(8,128)(2,1)S(1)}, bf16[272,1024]{1,0:T(8,128)(2,1)S(1)}, u32[]{:S(2)}, u32[]{:S(2)}) collective-permute-start(bf16[272,1024]{1,0:T(8,128)(2,1)S(1)} %get-tuple-element.31), channel_id=1, source_target_pairs={{0,4},{4,8},{8,12},{12,16},{16,20},{20,24},{24,28},{28,0},{1,5},{5... | collective-permute-start | bytes 1671176 | tf_op jit(solution)/shard_map/ppermute | solution.py:469
  9.3 13.4 %collective-permute-start.1 = (bf16[152,1024]{1,0:T(8,128)(2,1)S(1)}, bf16[152,1024]{1,0:T(8,128)(2,1)S(1)}, u32[]{:S(2)}, u32[]{:S(2)}) collective-permute-start(bf16[152,1024]{1,0:T(8,128)(2,1)S(1)} %get-tuple-element.32), channel_id=1, source_target_pairs={{0,4},{4,8},{8,12},{12,16},{16,20},{20,24},{24,28},{28,0},{1,5},{5... | collective-permute-start | bytes 933896 | tf_op jit(solution)/shard_map/ppermute | solution.py:469
  24.1 6.7 %collective-permute-start.2 = (f32[8,128]{1,0:T(8,128)S(1)}, f32[8,128]{1,0:T(8,128)S(1)}, u32[]{:S(2)}, u32[]{:S(2)}) collective-permute-start(f32[8,128]{1,0:T(8,128)S(1)} %get-tuple-element.40.refs_0_), channel_id=1, source_target_pairs={{0,1},{1,0},{2,3},{3,2},{4,5},{5,4},{6,7},{7,6},{8,9},{9,8},{10,11... | collective-permute-start | bytes 12296 | tf_op jit(solution)/shard_map/ppermute | solution.py:474
  26.5 4.5 %collective-permute-start.3 = (f32[8,128]{1,0:T(8,128)S(1)}, f32[8,128]{1,0:T(8,128)S(1)}, u32[]{:S(2)}, u32[]{:S(2)}) collective-permute-start(f32[8,128]{1,0:T(8,128)S(1)} %get-tuple-element.40.refs_0_), channel_id=1, source_target_pairs={{0,2},{1,3},{2,0},{3,1},{4,6},{5,7},{6,4},{7,5},{8,10},{9,11},{10,... | collective-permute-start | bytes 12296 | tf_op jit(solution)/shard_map/ppermute | solution.py:474
  29.0 5.4 %collective-permute-start.4 = (f32[8,128]{1,0:T(8,128)S(1)}, f32[8,128]{1,0:T(8,128)S(1)}, u32[]{:S(2)}, u32[]{:S(2)}) collective-permute-start(f32[8,128]{1,0:T(8,128)S(1)} %get-tuple-element.40.refs_0_), channel_id=1, source_target_pairs={{0,3},{1,2},{2,1},{3,0},{4,7},{5,6},{6,5},{7,4},{8,11},{9,10},{10,... | collective-permute-start | bytes 12296 | tf_op jit(solution)/shard_map/ppermute | solution.py:474
  42.3 1.4 %collective-permute-start.5 = (f32[32,1024]{1,0:T(8,128)S(1)}, f32[32,1024]{1,0:T(8,128)S(1)}, u32[]{:S(2)}, u32[]{:S(2)}) collective-permute-start(f32[32,1024]{1,0:T(8,128)S(1)} %shard_map.81), channel_id=1, source_target_pairs={{0,4},{4,0},{8,12},{12,8},{16,20},{20,16},{24,28},{28,24},{1,5},{5... | collective-permute-start | bytes 393224 | tf_op jit(solution)/shard_map/ppermute | solution.py:474
  43.8 4.4 %collective-permute-start.6 = (bf16[32,1024]{1,0:T(8,128)(2,1)S(1)}, bf16[32,1024]{1,0:T(8,128)(2,1)S(1)}, u32[]{:S(2)}, u32[]{:S(2)}) collective-permute-start(bf16[32,1024]{1,0:T(8,128)(2,1)S(1)} %add_convert_fusion.refs_0_), channel_id=1, source_target_pairs={{0,8},{4,12},{8,0},{12,4},{16,24},{20,28},{24,16},{28,20},{1,9},{5... | collective-permute-start | bytes 196616 | tf_op jit(solution)/shard_map/ppermute | solution.py:474
  44.4 4.3 %collective-permute-start.7 = (bf16[32,1024]{1,0:T(8,128)(2,1)S(1)}, bf16[32,1024]{1,0:T(8,128)(2,1)S(1)}, u32[]{:S(2)}, u32[]{:S(2)}) collective-permute-start(bf16[32,1024]{1,0:T(8,128)(2,1)S(1)} %add_convert_fusion.refs_0_), channel_id=1, source_target_pairs={{0,16},{4,20},{8,24},{12,28},{16,0},{20,4},{24,8},{28,12},{1,17},{... | collective-permute-start | bytes 196616 | tf_op jit(solution)/shard_map/ppermute | solution.py:474
  45.9 5.2 %collective-permute-start.8 = (bf16[32,1024]{1,0:T(8,128)(2,1)S(1)}, bf16[32,1024]{1,0:T(8,128)(2,1)S(1)}, u32[]{:S(2)}, u32[]{:S(2)}) collective-permute-start(bf16[32,1024]{1,0:T(8,128)(2,1)S(1)} %add_convert_fusion.refs_0_), channel_id=1, source_target_pairs={{0,24},{4,28},{8,16},{12,20},{16,8},{20,12},{24,0},{28,4},{1,25},{... | collective-permute-start | bytes 196616 | tf_op jit(solution)/shard_map/ppermute | solution.py:474

commit v9 on v8

--- a/solution.py
+++ b/solution.py
@@ -91,7 +91,7 @@
 def front_kernel(
     x_ref, taps_ref, filt_ref, skip_ref, cot_ref,
     far_ref, skt_ref, kv_ref, q0_ref, pt_ref, qt_ref, ct_ref, w_ref,
-    buf, mask,
+    bufs, mask,
 ):
     parts, rows, channels = x_ref.shape
     block = filt_ref.shape[1]
@@ -99,7 +99,7 @@
     groups = LANES // members
     blocks = rows // block
     tail = far_ref.shape[0] // 2
-    buf[:, :HALO, :] = jnp.zeros((parts, HALO, LANES), F32)
+    bufs[:, :, :HALO, :] = jnp.zeros((bufs.shape[0], parts, HALO, LANES), F32)
     row, col = lag_masks(block)
     mask[...] = jnp.where(col >= row, 1.0, 0.0).astype(BF16)
     inside = lax.axis_index("seq") < lax.axis_size("seq") - 1
@@ -112,7 +112,7 @@
         w_ref[group, :block, :] = near
         w_ref[group, block:, :] = circ - near
 
-    def features(chunk, number):
+    def features(chunk, buf, number):
         lane = pl.ds(pl.multiple_of(chunk * LANES, LANES), LANES)
         group_at = pl.ds(pl.multiple_of(chunk * groups, groups), groups)
         span = slice(number * block, (number + 1) * block)
@@ -132,19 +132,25 @@
         place = slice(number * members, (number + 1) * members)
         ct_ref[group_at, place, :] = cot_ref[span, lane].T.reshape(groups, members, block)
 
-    @pl.loop(0, channels // LANES)
-    def _(chunk):
+    def everything(chunk, buf):
         lane = pl.ds(pl.multiple_of(chunk * LANES, LANES), LANES)
         group_at = pl.ds(pl.multiple_of(chunk * groups, groups), groups)
         filt = filt_ref[group_at, :].astype(F32)
         skt_ref[group_at] = skip_columns(skip_ref.at[:, lane], block).reshape(groups, members, block)
         braid(
-            [functools.partial(features, chunk, number) for number in range(blocks)],
+            [functools.partial(features, chunk, buf, number) for number in range(blocks)],
             [functools.partial(filters, chunk, within, filt) for within in range(groups)],
         )
         for part in range(2):
             ends = jnp.where(inside, x_ref[1 + part, rows - tail :, lane], 0)
             far_ref[part * tail : (part + 1) * tail, lane] = ends
+
+    at_once = math.gcd(channels // LANES, bufs.shape[0])
+
+    @pl.loop(0, channels // LANES // at_once)
+    def _(turn):
+        for number in range(at_once):
+            everything(turn * at_once + number, bufs.at[number])
 
 
 def skip_columns(skip_ref, block):
@@ -549,7 +555,7 @@
             sds((groups, 2 * block, block), BF16),
         ],
         [
-            pltpu.VMEM((parts, HALO + rows, LANES), F32),
+            pltpu.VMEM((2, parts, HALO + rows, LANES), F32),
             pltpu.VMEM((block, block), BF16),
         ],
         (projected, taps_major, filters, skip_row, cots),

time: 52 us -> 51.7 us (level)
  no operation moved by 1% of the time
where the time goes in v9:
time: 51.7 us; the launch traced here: 51.6 us
  waiting for transfers between devices  19.6 us (38%)
  Pallas kernels  18.6 us (36%)
  starting transfers between devices  11.7 us (23%)
  local copies, waits for them, and re-layouts  0.84 us (2%)
  between operations  0.71 us (1%)
    pallas_call x7, Pallas kernels, on_chip(): pl.pallas_call(kernel, in_specs=[apart if number in outside else place fo...  18.6 us
    ppermute x2, waiting for transfers between devices, ring(): lax.ppermute(array, axis, [(i, (i + 1) % length) for i in range(length)])  10.8 us
    ppermute x7, waiting for transfers between devices, crossed(): return lax.ppermute(array, axis, [(i, i ^ bit) for i in range(length)])  8.81 us
    ppermute x7, starting transfers between devices, crossed(): return lax.ppermute(array, axis, [(i, i ^ bit) for i in range(length)])  8.61 us
    ppermute x2, starting transfers between devices, ring(): lax.ppermute(array, axis, [(i, (i + 1) % length) for i in range(length)])  3.13 us
  transfers between devices with their start and end apart: 9, of which 7 were waited for; matrix products, arithmetic and copies ran while one was open for 0% of the time, Pallas kernels for 18%

profile of v9, /device:TPU:0, one launch (start us, length us, event | category | flops | bytes accessed | tf_op | source)
XLA Modules:
  0.0 51.6 jit_solution(18408628284756026067)
XLA Ops:
  0.6 0.0 copy-start
  0.6 0.8 %reshape.12.skip_ref = bf16[1,1024]{1,0:T(2,128)(2,1)S(1)} reshape(bf16[1024]{0:T(1024)(128)(2,1)} %param.8) | data formatting | bytes 4096 | tf_op jit(solution)/shard_map/reshape | solution.py:522
  1.5 1.9 %shard_map.76 = (bf16[152,1024]{1,0:T(8,128)(2,1)S(1)}, bf16[3,7,1024]{2,1,0:T(8,128)(2,1)S(1)}, bf16[64,128]{1,0:T(8,128)(2,1)S(1)}, bf16[512,1024]{1,0:T(8,128)(2,1)S(1)}) custom-call(bf16[3,512,1024]{2,1,0:T(8,128)(2,1)} %x_ref.7, bf16[3,7,1024]{2,1,0:T(8,128)(2,1)} %bitcast.3, bf16[64,128]{1,0:T(8,128)(2,1)} %filt_hbm.1, bf16[512,1024]{1,0:T(8,128)(2,1)} %cot_hbm.1), custom_call_target="tpu_custom_call" | custom-call | tf_op jit(solution)/shard_map/pallas_call | solution.py:502
  3.4 0.0 copy-done
  3.4 5.1 %shard_map.77 = (bf16[272,1024]{1,0:T(8,128)(2,1)S(1)}, f32[64,16,128]{2,1,0:T(8,128)S(1)}, bf16[8,2,512,128]{3,2,1,0:T(8,128)(2,1)S(1)}, bf16[128,1024]{1,0:T(8...) custom-call(bf16[3,512,1024]{2,1,0:T(8,128)(2,1)S(1)} %copy-done, ...), custom_call_target="tpu_custom_call" | custom-call | tf_op jit(solution)/shard_map/pallas_call | solution.py:502
  8.5 0.5 %collective-permute-start = (bf16[272,1024]{1,0:T(8,128)(2,1)S(1)}, bf16[272,1024]{1,0:T(8,128)(2,1)S(1)}, u32[]{:S(2)}, u32[]{:S(2)}) collective-permute-start(bf16[272,1024]{1,0:T(8,128)(2,1)S(1)} %get-tuple-element.31), channel_id=1, source_target_pairs={{0,4},{4,8},{8,12},{12,16},{16,20},{20,24},{24,28},{28,0},{1,5},{5... | collective-permute-start | bytes 1671176 | tf_op jit(solution)/shard_map/ppermute | solution.py:475
  9.1 2.6 %collective-permute-start.1 = (bf16[152,1024]{1,0:T(8,128)(2,1)S(1)}, bf16[152,1024]{1,0:T(8,128)(2,1)S(1)}, u32[]{:S(2)}, u32[]{:S(2)}) collective-permute-start(bf16[152,1024]{1,0:T(8,128)(2,1)S(1)} %get-tuple-element.32), channel_id=1, source_target_pairs={{0,4},{4,8},{8,12},{12,16},{16,20},{20,24},{24,28},{28,0},{1,5},{5... | collective-permute-start | bytes 933896 | tf_op jit(solution)/shard_map/ppermute | solution.py:475
  11.7 10.8 %collective-permute-done.1.near_ref = bf16[152,1024]{1,0:T(8,128)(2,1)S(1)} collective-permute-done((bf16[152,1024]{1,0:T(8,128)(2,1)S(1)}, bf16[152,1024]{1,0:T(8,128)(2,1)S(1)}, u32[]{:S(2)}, u32[]{:S(2)}) %collective-permute-start.1) | collective-permute-done | bytes 311328 | tf_op jit(solution)/shard_map/ppermute | solution.py:475
  22.5 1.3 %shard_map.78 = (bf16[8,2,16,128]{3,2,1,0:T(8,128)(2,1)S(1)}, bf16[64,32,128]{2,1,0:T(8,128)(2,1)S(1)}, bf16[64,16,128]{2,1,0:T(8,128)(2,1)S(1)}, f32[64,64,128]{2,1,0:T(8,128)S(1)}, f32[8,128]{1,0:T(8,128)S(1)}) custom-call(bf16[152,1024]{1,0:T(8,128)(2,1)S(1)} %collective-permute-done.1.near_ref, bf16[3,512,1024]{2,1,0:T(8,128)(2,1)S(1)} %copy-done, ...), custom_call_target="tpu_custom_call" | custom-call | tf_op jit(solution)/shard_map/pallas_call | solution.py:502
  23.9 2.4 %collective-permute-start.2 = (f32[8,128]{1,0:T(8,128)S(1)}, f32[8,128]{1,0:T(8,128)S(1)}, u32[]{:S(2)}, u32[]{:S(2)}) collective-permute-start(f32[8,128]{1,0:T(8,128)S(1)} %get-tuple-element.40.refs_0_), channel_id=1, source_target_pairs={{0,1},{1,0},{2,3},{3,2},{4,5},{5,4},{6,7},{7,6},{8,9},{9,8},{10,11... | collective-permute-start | bytes 12296 | tf_op jit(solution)/shard_map/ppermute | solution.py:480
  26.2 2.6 %collective-permute-start.3 = (f32[8,128]{1,0:T(8,128)S(1)}, f32[8,128]{1,0:T(8,128)S(1)}, u32[]{:S(2)}, u32[]{:S(2)}) collective-permute-start(f32[8,128]{1,0:T(8,128)S(1)} %get-tuple-element.40.refs_0_), channel_id=1, source_target_pairs={{0,2},{1,3},{2,0},{3,1},{4,6},{5,7},{6,4},{7,5},{8,10},{9,11},{10,... | collective-permute-start | bytes 12296 | tf_op jit(solution)/shard_map/ppermute | solution.py:480
  28.8 0.0 collective-permute-start.4
  28.8 1.7 %shard_map.79 = (f32[8,4,2,136,128]{4,3,2,1,0:T(8,128)S(1)}, f32[8,4,2,128,128]{4,3,2,1,0:T(8,128)S(1)}, bf16[8,7,512,128]{3,2,1,0:T(8,128)(2,1)S(1)}) custom-call(bf16[152,1024]{1,0:T(8,128)(2,1)S(1)} %collective-permute-done.1.near_ref, bf16[3,512,1024]{2,1,0:T(8,128)(2,1)S(1)} %copy-done, bf16[8,2,512,128]{3,2,1,0:T(8,128)(2,1)S(1)} %get-tuple-element.34.kv_ref, ...), custom_call_target="tpu_custom_call" | custom-call | tf_op jit(solution)/shard_map/pallas_call | solution.py:502
  30.5 0.0 collective-permute-done.2.refs_1_
  30.6 0.2 collective-permute-done.3.refs_2_
  30.8 3.5 %collective-permute-done.4.refs_3_ = f32[8,128]{1,0:T(8,128)S(1)} collective-permute-done((f32[8,128]{1,0:T(8,128)S(1)}, f32[8,128]{1,0:T(8,128)S(1)}, u32[]{:S(2)}, u32[]{:S(2)}) %collective-permute-start.4) | collective-permute-done | bytes 4128 | tf_op jit(solution)/shard_map/ppermute | solution.py:480
  34.2 6.5 %shard_map.80 = (f32[32,1024]{1,0:T(8,128)S(1)}, f32[64,16,128]{2,1,0:T(8,128)S(1)}) custom-call(f32[8,128]{1,0:T(8,128)S(1)} %get-tuple-element.40.refs_0_, f32[8,128]{1,0:T(8,128)S(1)} %collective-permute-done.2.refs_1_, f32[8,128]{1,0:T(8,128)S(1)} %collective-permute-done.3.refs_2_, f32[8,128]{1,0:T(8,128)S(1)} %collective-permute-done.4.refs_3_, ...), custom_call_target="tpu_custom_call" | custom-call | tf_op jit(solution)/shard_map/pallas_call | solution.py:502
  40.7 0.0 collective-permute-done.far_ref
  40.7 1.4 %shard_map.81 = f32[32,1024]{1,0:T(8,128)S(1)} custom-call(bf16[272,1024]{1,0:T(8,128)(2,1)S(1)} %collective-permute-done.far_ref, bf16[3,7,1024]{2,1,0:T(8,128)(2,1)S(1)} %get-tuple-element.28.taps_ref, f32[64,16,128]{2,1,0:T(8,128)S(1)} %get-tuple-element.48.pgr_ref, f32[32,1024]{1,0:T(8,128)S(1)} %get-tuple-element.49.out_ref), custom_call_target="tpu_custom_call" | custom-call | tf_op jit(solution)/shard_map/pallas_call | solution.py:502
  42.1 0.1 collective-permute-start.5
  42.2 1.3 %collective-permute-done.5 = f32[32,1024]{1,0:T(8,128)S(1)} collective-permute-done((f32[32,1024]{1,0:T(8,128)S(1)}, f32[32,1024]{1,0:T(8,128)S(1)}, u32[]{:S(2)}, u32[]{:S(2)}) %collective-permute-start.5) | collective-permute-done | bytes 131104 | tf_op jit(solution)/shard_map/ppermute | solution.py:480
  43.6 0.7 %collective-permute-start.6 = (bf16[32,1024]{1,0:T(8,128)(2,1)S(1)}, bf16[32,1024]{1,0:T(8,128)(2,1)S(1)}, u32[]{:S(2)}, u32[]{:S(2)}) collective-permute-start(bf16[32,1024]{1,0:T(8,128)(2,1)S(1)} %add_convert_fusion.refs_0_), channel_id=1, source_target_pairs={{0,8},{4,12},{8,0},{12,4},{16,24},{20,28},{24,16},{28,20},{1,9},{5... | collective-permute-start | bytes 196616 | tf_op jit(solution)/shard_map/ppermute | solution.py:480
  44.2 1.5 %collective-permute-start.7 = (bf16[32,1024]{1,0:T(8,128)(2,1)S(1)}, bf16[32,1024]{1,0:T(8,128)(2,1)S(1)}, u32[]{:S(2)}, u32[]{:S(2)}) collective-permute-start(bf16[32,1024]{1,0:T(8,128)(2,1)S(1)} %add_convert_fusion.refs_0_), channel_id=1, source_target_pairs={{0,16},{4,20},{8,24},{12,28},{16,0},{20,4},{24,8},{28,12},{1,17},{... | collective-permute-start | bytes 196616 | tf_op jit(solution)/shard_map/ppermute | solution.py:480
  45.7 1.4 %collective-permute-start.8 = (bf16[32,1024]{1,0:T(8,128)(2,1)S(1)}, bf16[32,1024]{1,0:T(8,128)(2,1)S(1)}, u32[]{:S(2)}, u32[]{:S(2)}) collective-permute-start(bf16[32,1024]{1,0:T(8,128)(2,1)S(1)} %add_convert_fusion.refs_0_), channel_id=1, source_target_pairs={{0,24},{4,28},{8,16},{12,20},{16,8},{20,12},{24,0},{28,4},{1,25},{... | collective-permute-start | bytes 196616 | tf_op jit(solution)/shard_map/ppermute | solution.py:480
  47.1 0.8 %collective-permute-done.6.refs_1_ = bf16[32,1024]{1,0:T(8,128)(2,1)S(1)} collective-permute-done((bf16[32,1024]{1,0:T(8,128)(2,1)S(1)}, bf16[32,1024]{1,0:T(8,128)(2,1)S(1)}, u32[]{:S(2)}, u32[]{:S(2)}) %collective-permute-start.6) | collective-permute-done | bytes 65568 | tf_op jit(solution)/shard_map/ppermute | solution.py:480
  47.9 0.6 %collective-permute-done.7.refs_2_ = bf16[32,1024]{1,0:T(8,128)(2,1)S(1)} collective-permute-done((bf16[32,1024]{1,0:T(8,128)(2,1)S(1)}, bf16[32,1024]{1,0:T(8,128)(2,1)S(1)}, u32[]{:S(2)}, u32[]{:S(2)}) %collective-permute-start.7) | collective-permute-done | bytes 65568 | tf_op jit(solution)/shard_map/ppermute | solution.py:480
  48.5 2.4 %collective-permute-done.8.refs_3_ = bf16[32,1024]{1,0:T(8,128)(2,1)S(1)} collective-permute-done((bf16[32,1024]{1,0:T(8,128)(2,1)S(1)}, bf16[32,1024]{1,0:T(8,128)(2,1)S(1)}, u32[]{:S(2)}, u32[]{:S(2)}) %collective-permute-start.8) | collective-permute-done | bytes 65568 | tf_op jit(solution)/shard_map/ppermute | solution.py:480
  50.9 0.7 %shard_map.82 = (f32[3,7,1024]{2,1,0:T(8,128)}, f32[64,128]{1,0:T(8,128)}, f32[1,1024]{1,0:T(1,128)}) custom-call(bf16[32,1024]{1,0:T(8,128)(2,1)S(1)} %add_convert_fusion.refs_0_, bf16[32,1024]{1,0:T(8,128)(2,1)S(1)} %collective-permute-done.6.refs_1_, bf16[32,1024]{1,0:T(8,128)(2,1)S(1)} %collective-permute-done.7.refs_2_, ...), custom_call_target="tpu_custom_call" | custom-call | tf_op jit(solution)/shard_map/pallas_call | solution.py:502
  (1 shorter events, 0.0 us)
Async XLA Ops:
  0.6 2.8 %copy-start = (bf16[3,512,1024]{2,1,0:T(8,128)(2,1)S(1)}, bf16[3,512,1024]{2,1,0:T(8,128)(2,1)}, u32[]{:S(2)}) copy-start(bf16[3,512,1024]{2,1,0:T(8,128)(2,1)} %x_ref.7) | copy-start | bytes 9437188
  8.5 32.2 %collective-permute-start = (bf16[272,1024]{1,0:T(8,128)(2,1)S(1)}, bf16[272,1024]{1,0:T(8,128)(2,1)S(1)}, u32[]{:S(2)}, u32[]{:S(2)}) collective-permute-start(bf16[272,1024]{1,0:T(8,128)(2,1)S(1)} %get-tuple-element.31), channel_id=1, source_target_pairs={{0,4},{4,8},{8,12},{12,16},{16,20},{20,24},{24,28},{28,0},{1,5},{5... | collective-permute-start | bytes 1671176 | tf_op jit(solution)/shard_map/ppermute | solution.py:475
  9.1 13.4 %collective-permute-start.1 = (bf16[152,1024]{1,0:T(8,128)(2,1)S(1)}, bf16[152,1024]{1,0:T(8,128)(2,1)S(1)}, u32[]{:S(2)}, u32[]{:S(2)}) collective-permute-start(bf16[152,1024]{1,0:T(8,128)(2,1)S(1)} %get-tuple-element.32), channel_id=1, source_target_pairs={{0,4},{4,8},{8,12},{12,16},{16,20},{20,24},{24,28},{28,0},{1,5},{5... | collective-permute-start | bytes 933896 | tf_op jit(solution)/shard_map/ppermute | solution.py:475
  23.9 6.7 %collective-permute-start.2 = (f32[8,128]{1,0:T(8,128)S(1)}, f32[8,128]{1,0:T(8,128)S(1)}, u32[]{:S(2)}, u32[]{:S(2)}) collective-permute-start(f32[8,128]{1,0:T(8,128)S(1)} %get-tuple-element.40.refs_0_), channel_id=1, source_target_pairs={{0,1},{1,0},{2,3},{3,2},{4,5},{5,4},{6,7},{7,6},{8,9},{9,8},{10,11... | collective-permute-start | bytes 12296 | tf_op jit(solution)/shard_map/ppermute | solution.py:480
  26.2 4.5 %collective-permute-start.3 = (f32[8,128]{1,0:T(8,128)S(1)}, f32[8,128]{1,0:T(8,128)S(1)}, u32[]{:S(2)}, u32[]{:S(2)}) collective-permute-start(f32[8,128]{1,0:T(8,128)S(1)} %get-tuple-element.40.refs_0_), channel_id=1, source_target_pairs={{0,2},{1,3},{2,0},{3,1},{4,6},{5,7},{6,4},{7,5},{8,10},{9,11},{10,... | collective-permute-start | bytes 12296 | tf_op jit(solution)/shard_map/ppermute | solution.py:480
  28.8 5.4 %collective-permute-start.4 = (f32[8,128]{1,0:T(8,128)S(1)}, f32[8,128]{1,0:T(8,128)S(1)}, u32[]{:S(2)}, u32[]{:S(2)}) collective-permute-start(f32[8,128]{1,0:T(8,128)S(1)} %get-tuple-element.40.refs_0_), channel_id=1, source_target_pairs={{0,3},{1,2},{2,1},{3,0},{4,7},{5,6},{6,5},{7,4},{8,11},{9,10},{10,... | collective-permute-start | bytes 12296 | tf_op jit(solution)/shard_map/ppermute | solution.py:480
  42.1 1.4 %collective-permute-start.5 = (f32[32,1024]{1,0:T(8,128)S(1)}, f32[32,1024]{1,0:T(8,128)S(1)}, u32[]{:S(2)}, u32[]{:S(2)}) collective-permute-start(f32[32,1024]{1,0:T(8,128)S(1)} %shard_map.81), channel_id=1, source_target_pairs={{0,4},{4,0},{8,12},{12,8},{16,20},{20,16},{24,28},{28,24},{1,5},{5... | collective-permute-start | bytes 393224 | tf_op jit(solution)/shard_map/ppermute | solution.py:480
  43.6 4.4 %collective-permute-start.6 = (bf16[32,1024]{1,0:T(8,128)(2,1)S(1)}, bf16[32,1024]{1,0:T(8,128)(2,1)S(1)}, u32[]{:S(2)}, u32[]{:S(2)}) collective-permute-start(bf16[32,1024]{1,0:T(8,128)(2,1)S(1)} %add_convert_fusion.refs_0_), channel_id=1, source_target_pairs={{0,8},{4,12},{8,0},{12,4},{16,24},{20,28},{24,16},{28,20},{1,9},{5... | collective-permute-start | bytes 196616 | tf_op jit(solution)/shard_map/ppermute | solution.py:480
  44.2 4.3 %collective-permute-start.7 = (bf16[32,1024]{1,0:T(8,128)(2,1)S(1)}, bf16[32,1024]{1,0:T(8,128)(2,1)S(1)}, u32[]{:S(2)}, u32[]{:S(2)}) collective-permute-start(bf16[32,1024]{1,0:T(8,128)(2,1)S(1)} %add_convert_fusion.refs_0_), channel_id=1, source_target_pairs={{0,16},{4,20},{8,24},{12,28},{16,0},{20,4},{24,8},{28,12},{1,17},{... | collective-permute-start | bytes 196616 | tf_op jit(solution)/shard_map/ppermute | solution.py:480
  45.7 5.2 %collective-permute-start.8 = (bf16[32,1024]{1,0:T(8,128)(2,1)S(1)}, bf16[32,1024]{1,0:T(8,128)(2,1)S(1)}, u32[]{:S(2)}, u32[]{:S(2)}) collective-permute-start(bf16[32,1024]{1,0:T(8,128)(2,1)S(1)} %add_convert_fusion.refs_0_), channel_id=1, source_target_pairs={{0,24},{4,28},{8,16},{12,20},{16,8},{20,12},{24,0},{28,4},{1,25},{... | collective-permute-start | bytes 196616 | tf_op jit(solution)/shard_map/ppermute | solution.py:480
